TPU v7x, 256 devices: a whole 4x4x8 slice. The times are simulated.
256 devices in a mesh: seq: 32 (over y, z), chan: 8 (over x, core).
Axes of the slice: x: 4, y: 4, z: 8, core: 2. Of those that a mesh axis runs over, the one named last changes fastest.
Arguments:
- features: bfloat16 [3, 8192, 8192], P(None, 'seq', 'chan'), may hold values from -6 to 6
- short_filter: bfloat16 [7, 3, 512], P(None, None, 'chan'), may hold values from -3 to 3
- decay: float32 [16, 8192], P(None, 'chan'), may hold values from 2.4414063e-05 to 0.05
- angle_rate: float32 [16, 8192], P(None, 'chan'), may hold values from -1 to 1
- residues: float32 [2, 16, 8192], P(None, None, 'chan'), may hold values from -0.12 to 0.12
- skip: float32 [8192], P('chan'), may hold values from -4 to 4
- entry_states: float32 [8, 2, 16, 8192], P(None, None, None, 'chan'), may hold values from -48 to 48
- segment_ids: int32 [8192], replicated, may hold values from 0 to 7, never falling along the last dimension, each value on 1 to 2048 neighbouring positions
- state_ids: int32 [8], replicated, may hold values from 0 to 7
- out_weight: bfloat16 [8192, 8192], P('chan', 'seq'), may hold values from -0.125 to 0.125
Outputs:
- mixed_out: bfloat16 [8192, 8192], P('seq', 'chan')
Inputs may be any that keep to these rules, and one draw needn't show every extreme that they name: `segment_ids`: never falls along the window; each of the 8 records holds 1 to 2048 positions and one holds exactly 2048.
All inputs are finite; a program needn't handle non-finite values.
Results may differ from a plain program's by a relative error of at most 0.025.
Values may be sent and summed in bfloat16 or wider, within the bound.
No kernel may reach another device: no remote copies, remote signals or barrier semaphores. Data moves between devices by JAX's collectives and lax.ppermute only.
A program may use at most 128 MiB of HBM per device.

v0:
```python
import jax
import jax.numpy as jnp
from jax import lax
from jax.sharding import PartitionSpec as P


def from_behind(value, axis, steps):
    count = lax.axis_size(axis)
    leading, last = (max(0, -steps), min(count, count - steps))
    return lax.ppermute(value, axis, [(source, source + steps) for source in range(leading, last)])


def entering_2(value, axis, join, neutral):
    place = lax.axis_index(axis)
    gathered = jax.tree.map(
        lambda a, kind: lax.all_gather(a.astype(kind), axis),
        value,
        (jnp.bfloat16, jnp.bfloat16, jnp.bfloat16, jnp.bfloat16),
    )
    state = jax.tree.map(lambda a, e: jnp.zeros_like(a) + jnp.asarray(e, a.dtype), value, neutral)

    def one(hop, state):
        return join(
            state,
            jax.tree.map(
                lambda a, own: lax.dynamic_index_in_dim(a, hop, 0, False).astype(own.dtype),
                gathered,
                value,
            ),
        )

    return lax.fori_loop(0, place, one, state)


def featurize(extended, records, short_filter, count):
    taps = short_filter.shape[0]
    lead = taps - 1
    group_size = extended.shape[2] // short_filter.shape[2]
    filters = jnp.repeat(short_filter.astype(jnp.float32), group_size, axis=2)
    result = jnp.zeros((extended.shape[0], count, extended.shape[2]), jnp.float32)
    current = records[lead : lead + count]
    for offset in range(taps):
        same = (records[lead - offset : lead - offset + count] == current).astype(jnp.float32)
        result = (
            result
            + filters[offset][:, None, :]
            * extended[:, lead - offset : lead - offset + count, :]
            * same[None, :, None]
        )
    return result


def local_modes(product_f, starts, entry_index, entry_states, pole_re, pole_im, residues):
    count, channels = product_f.shape
    step_rows = 16
    blocks = count // step_rows

    def local_block_step(carry, inputs_now):
        state_re, state_im = carry
        values, flags, picks = inputs_now
        outputs = []
        for offset in range(step_rows):
            entering = lax.dynamic_index_in_dim(entry_states, picks[offset], 0, keepdims=False)
            before_re = jnp.where(flags[offset], entering[0], state_re)
            before_im = jnp.where(flags[offset], entering[1], state_im)
            state_re = pole_re * before_re - pole_im * before_im + values[offset][None, :]
            state_im = pole_re * before_im + pole_im * before_re
            outputs.append(jnp.sum(residues[0] * state_re - residues[1] * state_im, axis=0))
        return ((state_re, state_im), jnp.stack(outputs))

    zeros = jnp.zeros(pole_re.shape, jnp.float32)
    final, result = lax.scan(
        local_block_step,
        (zeros, zeros),
        (
            product_f.reshape(blocks, step_rows, channels),
            starts.reshape(blocks, step_rows),
            entry_index.reshape(blocks, step_rows),
        ),
    )
    return (final, result.reshape(count, channels))


def carried_modes(carry_re, carry_im, alive, pole_re, pole_im, residues, count):
    step_rows = 16
    blocks = count // step_rows

    def carried_block_step(carry, flags):
        state_re, state_im = carry
        outputs = []
        for offset in range(step_rows):
            new_re = pole_re * state_re - pole_im * state_im
            new_im = pole_re * state_im + pole_im * state_re
            state_re, state_im = (new_re, new_im)
            outputs.append(
                flags[offset] * jnp.sum(residues[0] * state_re - residues[1] * state_im, axis=0)
            )
        return ((state_re, state_im), jnp.stack(outputs))

    unused, result = lax.scan(
        carried_block_step, (carry_re, carry_im), alive.reshape(blocks, step_rows)
    )
    return result.reshape(count, pole_re.shape[1])


def combine_spans(earlier, later):
    first_re, first_im, sum_re, sum_im = earlier
    second_re, second_im, add_re, add_im = later
    return (
        second_re * first_re - second_im * first_im,
        second_re * first_im + second_im * first_re,
        second_re * sum_re - second_im * sum_im + add_re,
        second_re * sum_im + second_im * sum_re + add_im,
    )


def shards(
    features,
    short_filter,
    decay,
    angle_rate,
    residues,
    skip,
    entry_states,
    segment_ids,
    state_ids,
    out_weight,
):
    row_count = features.shape[1]
    lead = short_filter.shape[0] - 1
    device = lax.axis_index("seq")
    position = device * row_count
    padded_ids = jnp.concatenate([jnp.full((lead,), -1, jnp.int32), segment_ids])
    window_ids = lax.dynamic_slice_in_dim(padded_ids, position, row_count + lead, 0)
    own_ids = window_ids[lead:]
    border = from_behind(features[:, row_count - lead :, :], "seq", 1)
    extended = jnp.concatenate([border, features], axis=1)
    featured = featurize(extended, window_ids, short_filter, row_count)
    product = (featured[1] * featured[2]).astype(jnp.bfloat16)
    query = featured[0]
    product_f = product.astype(jnp.float32)
    starts = own_ids != window_ids[lead - 1 : lead - 1 + row_count]
    entry_index = state_ids[own_ids]
    magnitude = jnp.exp(-decay)
    pole_re = magnitude * jnp.cos(angle_rate)
    pole_im = magnitude * jnp.sin(angle_rate)
    final, local_modal = local_modes(
        product_f, starts, entry_index, entry_states, pole_re, pole_im, residues
    )
    span_mag = jnp.exp(-decay * row_count)
    whole_re = span_mag * jnp.cos(angle_rate * row_count)
    whole_im = span_mag * jnp.sin(angle_rate * row_count)
    zeros = jnp.zeros(pole_re.shape, jnp.float32)
    has_start = jnp.any(starts)
    span_re = jnp.where(has_start, 0.0, whole_re)
    span_im = jnp.where(has_start, 0.0, whole_im)
    identity = (jnp.ones(pole_re.shape, jnp.float32), zeros, zeros, zeros)
    prefix = entering_2((span_re, span_im, final[0], final[1]), "seq", combine_spans, identity)
    carry_re, carry_im = (prefix[2], prefix[3])
    alive = (jnp.cumsum(starts.astype(jnp.int32)) == 0).astype(jnp.float32)
    carried = carried_modes(carry_re, carry_im, alive, pole_re, pole_im, residues, row_count)
    modal = local_modal + carried
    gated = (query * (modal + skip[None, :] * product_f)).astype(jnp.bfloat16)
    terms = jnp.dot(
        gated,
        lax.all_gather(out_weight, "seq", axis=1, tiled=True),
        preferred_element_type=jnp.float32,
    )
    return lax.psum_scatter(terms.astype(jnp.bfloat16), "chan", scatter_dimension=1, tiled=True)


def solution(mesh):
    in_specs = (
        P(None, "seq", "chan"),
        P(None, None, "chan"),
        P(None, "chan"),
        P(None, "chan"),
        P(None, None, "chan"),
        P("chan"),
        P(None, None, None, "chan"),
        P(),
        P(),
        P("chan", "seq"),
    )
    out_specs = P("seq", "chan")
    return jax.shard_map(shards, mesh=mesh, in_specs=in_specs, out_specs=out_specs, check_vma=False)
```

profile of v0, /device:TPU:1, one launch (start us, length us, event | category | flops | bytes accessed | tf_op | source)
XLA Modules:
  0.0 1192.6 jit_solution(17586864218004246644)
XLA Ops:
  8.2 2.6 select_convert_fusion
  11.7 4.4 collective-permute-start
  17.2 1.6 fusion.117
  18.8 5.1 compare_select_fusion.1
  25.6 3.8 multiply_add_fusion.32
  29.4 1.7 copy-done.2
  32.7 738.7 %while.46 = (s32[]{:T(128)}, f32[16,1024]{1,0:T(8,128)S(1)}, f32[16,1024]{1,0:T(8,128)S(1)}, f32[16,16,1024]{2,1,0:T(8,128)S(1)}, pred[16,16]{1,0:T(8,128)(4,1)S...) while((s32[]{:T(128)}, f32[16,1024]{1,0:T(8,128)S(1)}, ...), condition=%wide.region_17.18_spmd.clone, body=%wide.region_0.17_spmd.clone.sunk | while | flops 3670082 | bytes 8525295 | solution.py:72
  39.2 1.4 fusion.137
  51.7 1.9 multiply_add_fusion.50
  62.5 1.9 multiply_add_fusion.51
  73.4 1.9 multiply_add_fusion.52
  97.8 1.9 multiply_add_fusion.50
  108.6 1.9 multiply_add_fusion.51
  119.5 1.9 multiply_add_fusion.52
  129.4 1.6 constant_dynamic-slice_fusion.26
  131.7 1.4 fusion.137
  144.2 1.9 multiply_add_fusion.50
  155.0 1.9 multiply_add_fusion.51
  165.9 1.9 multiply_add_fusion.52
  190.4 1.9 multiply_add_fusion.50
  201.2 1.9 multiply_add_fusion.51
  212.1 1.9 multiply_add_fusion.52
  236.5 1.9 multiply_add_fusion.50
  247.3 1.9 multiply_add_fusion.51
  258.2 1.9 multiply_add_fusion.52
  282.7 1.9 multiply_add_fusion.50
  293.5 1.9 multiply_add_fusion.51
  304.4 1.9 multiply_add_fusion.52
  328.8 1.9 multiply_add_fusion.50
  339.6 1.9 multiply_add_fusion.51
  350.5 1.9 multiply_add_fusion.52
  375.0 1.9 multiply_add_fusion.50
  385.8 1.9 multiply_add_fusion.51
  396.7 1.9 multiply_add_fusion.52
  421.1 1.9 multiply_add_fusion.50
  431.9 1.9 multiply_add_fusion.51
  442.8 1.9 multiply_add_fusion.52
  467.3 1.9 multiply_add_fusion.50
  478.1 1.9 multiply_add_fusion.51
  489.0 1.9 multiply_add_fusion.52
  513.5 1.9 multiply_add_fusion.50
  524.2 1.9 multiply_add_fusion.51
  535.1 1.9 multiply_add_fusion.52
  559.6 1.9 multiply_add_fusion.50
  570.4 1.9 multiply_add_fusion.51
  581.3 1.9 multiply_add_fusion.52
  605.8 1.9 multiply_add_fusion.50
  616.6 1.9 multiply_add_fusion.51
  627.5 1.9 multiply_add_fusion.52
  651.9 1.9 multiply_add_fusion.50
  662.7 1.9 multiply_add_fusion.51
  673.6 1.9 multiply_add_fusion.52
  698.1 1.9 multiply_add_fusion.50
  708.9 1.9 multiply_add_fusion.51
  719.8 1.9 multiply_add_fusion.52
  744.3 1.9 multiply_add_fusion.50
  755.0 1.9 multiply_add_fusion.51
  765.9 1.9 multiply_add_fusion.52
  774.2 72.1 %all-gather.16.cloned.1.call-done = bf16[512,1024]{1,0:T(8,128)(2,1)} async-done(((bf16[16,1024]{1,0:T(8,128)(2,1)}), bf16[512,1024]{1,0:T(8,128)(2,1)}) %all-gather.16.cloned.1.call-update) | async-done | bytes 1048592 | tf_op jit(solution)/shard_map/all_gather | solution.py:16
  846.3 76.3 %all-gather.18.cloned.1.call-done = bf16[512,1024]{1,0:T(8,128)(2,1)} async-done(((bf16[16,1024]{1,0:T(8,128)(2,1)}), bf16[512,1024]{1,0:T(8,128)(2,1)}) %all-gather.18.cloned.1.call-update) | async-done | bytes 1048592 | tf_op jit(solution)/shard_map/all_gather | solution.py:16
  922.7 183.2 %while.45 = (s32[]{:T(128)}, f32[16,1024]{1,0:T(8,128)S(1)}, f32[16,1024]{1,0:T(8,128)S(1)}, f32[16,16,1024]{2,1,0:T(8,128)S(1)}, f32[16,1024]{1,0:T(8,128)S(1)}...) while((s32[]{:T(128)}, f32[16,1024]{1,0:T(8,128)S(1)}, ...), condition=%wide.region_40.41_spmd, body=%wide.region_23.40_spmd.sunk | while | flops 3899394 | bytes 1769893 | solution.py:100
  1106.1 1.7 copy-done.3
  1108.3 11.8 convolution_convert_fusion
  1120.2 65.6 %reduce-scatter.2.cloned.1.call-done = bf16[256,1024]{1,0:T(8,128)(2,1)} async-done(((bf16[256,8192]{1,0:T(8,128)(2,1)}), bf16[256,1024]{1,0:T(8,128)(2,1)}) %reduce-scatter.2.cloned.1.call-update) | async-done | bytes 524304 | tf_op jit(solution)/shard_map/reduce_scatter | solution.py:169
  (500 shorter events, 352.8 us)
Async XLA Ops:
  6.5 19.0 %copy-start.4 = (bf16[3,256,1024]{2,1,0:T(8,128)(2,1)S(1)}, bf16[3,256,1024]{2,1,0:T(8,128)(2,1)}, u32[]{:S(2)}) copy-start(bf16[3,256,1024]{2,1,0:T(8,128)(2,1)} %param.16) | copy-start | bytes 4718596
  6.5 767.6 %all-gather.12.cloned.1.call-start = ((), (), s32[]{:S(2)}) async-start(), calls=%async_computation.3 | async-start | bytes 1081344 | tf_op jit(solution)/shard_map/all_gather | solution.py:16
  10.9 763.3 %all-gather.14.cloned.1.call-start = ((), (), s32[]{:S(2)}) async-start(), calls=%async_computation.4 | async-start | bytes 1081344 | tf_op jit(solution)/shard_map/all_gather | solution.py:16
  11.7 13.8 %collective-permute-start = (bf16[3,6,1024]{2,1,0:T(8,128)(2,1)S(1)}, bf16[3,6,1024]{2,1,0:T(8,128)(2,1)S(1)}, u32[]{:S(2)}, u32[]{:S(2)}) collective-permute-start(bf16[3,6,1024]{2,1,0:T(8,128)(2,1)S(1)} %slice.586), channel_id=1, source_target_pairs={{0,8},{8,16},{16,24},{24,32},{32,40},{40,48},{48,56},{56,64},{64,7... | collective-permute-start | bytes 110600 | tf_op jit(solution)/shard_map/ppermute | solution.py:10
  16.2 830.1 %all-gather.16.cloned.1.call-start = ((), (), s32[]{:S(2)}) async-start(), calls=%async_computation.5 | async-start | bytes 1081344 | tf_op jit(solution)/shard_map/all_gather | solution.py:16
  29.4 1.7 copy-start.2
  31.1 1.6 copy-start
  31.1 1.6 copy-start.1
  772.0 150.6 %all-gather.18.cloned.1.call-start = ((), (), s32[]{:S(2)}) async-start(), calls=%async_computation.6 | async-start | bytes 1081344 | tf_op jit(solution)/shard_map/all_gather | solution.py:16
  772.7 335.6 %all-gather.10.cloned.1.call-start = ((), (), s32[]{:S(2)}) async-start(), calls=%async_computation.1 | async-start | bytes 17301504 | tf_op jit(solution)/shard_map/all_gather | solution.py:166
  773.3 412.5 %reduce-scatter.2.cloned.1.call-start = ((), (), s32[]{:S(2)}) async-start(), calls=%async_computation.2 | async-start | bytes 4718592 | tf_op jit(solution)/shard_map/reduce_scatter | solution.py:169
  922.7 183.4 %copy-start.5 = (f32[1024]{0:T(1024)S(1)}, f32[1024]{0:T(1024)}, u32[]{:S(2)}) copy-start(f32[1024]{0:T(1024)} %param.21) | copy-start | bytes 12292
  1106.0 1.9 copy-start.3
Sparse Core Ops, SparseCore 0:
  11.0 75.6 all-gather.11
  89.2 73.7 all-gather.13
  772.1 74.1 all-gather.15
  848.7 73.7 all-gather.17
  924.9 150.4 all-gather.9
  1120.3 65.4 reduce-scatter.1
where the time goes:
time: 1210 us; the launch traced here: 1190 us
  loops' own time  483 us (40%)
  other arithmetic  394 us (33%)
  waiting for transfers between devices  215 us (18%)
  local copies, waits for them, and re-layouts  71.1 us (6%)
  between operations  13.7 us (1%)
    another operation x1, loops' own time, local_modes(): lax.scan(local_block_step, (zeros, zeros), (product_f.reshape(blocks, ste...  481 us
    mul x128, other arithmetic, carried_block_step(): flags[offset]  157 us
    all_gather x4, waiting for transfers between devices, entering_2(): lax.all_gather(a.astype(kind), axis)  148 us
    reduce_sum x80, other arithmetic, local_block_step(): jnp.sum(residues[0] * state_re - residues[1] * state_im, axis=0)  98.6 us
    add x48, other arithmetic, local_block_step(): state_im = pole_re * before_im + pole_im * before_re  92.3 us
    reduce_scatter x1, waiting for transfers between devices, shards(): lax.psum_scatter(terms.astype(jnp.bfloat16), 'chan', scatter_dimension=1,...  65.6 us
  transfers between devices with their start and end apart: 7, of which 3 were waited for; matrix products, arithmetic and copies ran while one was open for 38% of the time, Pallas kernels for 0%

commit v1 on v0

v1 whole, which is shorter than its diff:
```python
import functools

import jax
import jax.numpy as jnp
from jax import lax
from jax.experimental import pallas as pl
from jax.experimental.pallas import tpu as pltpu
from jax.sharding import Mesh
from jax.sharding import PartitionSpec as P

F32 = jnp.float32
BF16 = jnp.bfloat16
ROWS = 256
CH = 1024
LANES = 128
TILES = CH // LANES
MODES = 16
TAPS = 7
GAP = 9
BLOCK = GAP * TILES
VMEM_LIMIT = 56 * 1024 * 1024


def spread(scratch, base, value):
    for j in range(TILES):
        scratch[pl.ds(base + j * GAP, 8), :] = value[:, j * LANES : (j + 1) * LANES]


def row(scratch, base, r):
    return scratch[pl.ds(base + r, TILES, stride=GAP), :]


def record_of(ids, position):
    return jnp.where(position < 0, -1, ids[jnp.maximum(position, 0)])


def scan_kernel(
    dev_ref, ids, picks, feat, border, filt, decay, angle, res, skip, entry,
    final_out, pole_out, power_out, query_out, base_out,
    streams, tables, product, states, small,
):
    position = dev_ref[0] * ROWS
    for half in range(2):
        rows = slice(8 * half, 8 * half + 8)
        mag = jnp.exp(-decay[rows, :])
        ang = angle[rows, :]
        parts = (mag * jnp.cos(ang), mag * jnp.sin(ang), res[0, rows, :], res[1, rows, :])
        for n, part in enumerate(parts):
            spread(small, n * BLOCK, part)
        for n in range(4):
            for r in range(8):
                tables[n, 8 * half + r] = row(small, n * BLOCK, r)
    for m in range(MODES):
        pole_out[0, m] = tables[0, m]
        pole_out[1, m] = tables[1, m]
        re, im = tables[0, m], tables[1, m]
        for _ in range(8):
            re, im = re * re - im * im, 2.0 * re * im
        power_out[0, m] = re
        power_out[1, m] = im
    spread(small, 0, jnp.broadcast_to(skip[...], (8, CH)))
    skip_row = row(small, 0, 0)

    for i in range(3):
        spread(streams.at[i], 0, border[i].astype(F32))

    def relayout(b, carry):
        for i in range(3):
            value = feat[i, pl.ds(pl.multiple_of(b * 16, 16), 16), :].astype(F32)
            spread(streams.at[i], (2 * b + 1) * BLOCK, value[:8])
            spread(streams.at[i], (2 * b + 2) * BLOCK, value[8:])
        return carry

    lax.fori_loop(0, ROWS // 16, relayout, 0)

    def featurize(b, carry):
        first = position + 8 * b
        plain = record_of(ids, first - 6) == ids[first + 7]

        def outputs(results):
            for t in range(8):
                query_out[8 * b + t] = results[0][t]
                product[8 * b + t] = (results[1][t] * results[2][t]).astype(BF16).astype(F32)

        def rows_of(i):
            return [row(streams.at[i], b * BLOCK, 2 + r) for r in range(6)] + [
                row(streams.at[i], (b + 1) * BLOCK, r) for r in range(8)
            ]

        @pl.when(plain)
        def _():
            results = []
            for i in range(3):
                values = rows_of(i)
                taps = [filt[j, i] for j in range(TAPS)]
                results.append(
                    [sum(taps[j] * values[6 + t - j] for j in range(TAPS)) for t in range(8)]
                )
            outputs(results)

        @pl.when(jnp.logical_not(plain))
        def _():
            same = [
                [
                    (record_of(ids, first + t - j) == ids[first + t]).astype(F32)
                    for j in range(TAPS)
                ]
                for t in range(8)
            ]
            results = []
            for i in range(3):
                values = rows_of(i)
                taps = [filt[j, i] for j in range(TAPS)]
                results.append(
                    [
                        sum(
                            taps[j] * jnp.where(same[t][j] > 0.5, values[6 + t - j], 0.0)
                            for j in range(TAPS)
                        )
                        for t in range(8)
                    ]
                )
            outputs(results)

        return carry

    lax.fori_loop(0, ROWS // 8, featurize, 0)

    for group in range(2):
        modes = range(8 * group, 8 * group + 8)
        for m in range(8):
            states[0, m] = jnp.zeros((8, LANES), F32)
            states[1, m] = jnp.zeros((8, LANES), F32)

        def step(value, re, im, group=group, modes=modes):
            out = None
            for m in range(8):
                pr, pi = tables[0, modes[m]], tables[1, modes[m]]
                new_re = pr * re[m] - pi * im[m] + value
                new_im = pr * im[m] + pi * re[m]
                re[m], im[m] = new_re, new_im
                term = tables[2, modes[m]] * new_re - tables[3, modes[m]] * new_im
                out = term if out is None else out + term
            return out

        def emit(t, value, out, group=group):
            if group == 0:
                base_out[t] = skip_row * value + out
            else:
                base_out[t] = base_out[t] + out

        def block(b, carry, group=group, step=step, emit=emit):
            first = position + 8 * b
            plain = record_of(ids, first - 1) == ids[first + 7]

            @pl.when(plain)
            def _():
                re = [states[0, m] for m in range(8)]
                im = [states[1, m] for m in range(8)]
                for t in range(8):
                    value = product[8 * b + t]
                    emit(8 * b + t, value, step(value, re, im))
                for m in range(8):
                    states[0, m] = re[m]
                    states[1, m] = im[m]

            @pl.when(jnp.logical_not(plain))
            def _():
                def one(t, carry):
                    here = first + t

                    @pl.when(record_of(ids, here - 1) != ids[here])
                    def _():
                        pick = picks[ids[here]]
                        for part in range(2):
                            spread(small, 0, entry[pick, part, 8 * group : 8 * group + 8, :])
                            for m in range(8):
                                states[part, m] = row(small, 0, m)

                    re = [states[0, m] for m in range(8)]
                    im = [states[1, m] for m in range(8)]
                    value = product[8 * b + t]
                    emit(8 * b + t, value, step(value, re, im))
                    for m in range(8):
                        states[0, m] = re[m]
                        states[1, m] = im[m]
                    return carry

                lax.fori_loop(0, 8, one, 0)

            return carry

        lax.fori_loop(0, ROWS // 8, block, 0)
        for part in range(2):
            for m in range(0, 8, 2):
                pair = jnp.concatenate([states[part, m], states[part, m + 1]], axis=0)
                at = 64 * group + 8 * m
                final_out[part, at : at + 16, :] = pair.astype(BF16)


def scan(dev, ids, picks, feat, border, filt, decay, angle, res, skip, entry, interpret=False):
    smem = pl.BlockSpec(memory_space=pltpu.SMEM)
    vmem = pl.BlockSpec(memory_space=pltpu.VMEM)
    wide = (8, LANES)
    return pl.pallas_call(
        scan_kernel,
        out_shape=(
            jax.ShapeDtypeStruct((2, MODES * 8, LANES), BF16),
            jax.ShapeDtypeStruct((2, MODES) + wide, F32),
            jax.ShapeDtypeStruct((2, MODES) + wide, F32),
            jax.ShapeDtypeStruct((ROWS,) + wide, F32),
            jax.ShapeDtypeStruct((ROWS,) + wide, F32),
        ),
        in_specs=[smem, smem, smem] + [vmem] * 8,
        out_specs=(vmem,) * 5,
        scratch_shapes=[
            pltpu.VMEM((3, (ROWS // 8 + 1) * BLOCK, LANES), F32),
            pltpu.VMEM((4, MODES) + wide, F32),
            pltpu.VMEM((ROWS,) + wide, F32),
            pltpu.VMEM((2, 8) + wide, F32),
            pltpu.VMEM((4 * BLOCK, LANES), F32),
        ],
        compiler_params=pltpu.CompilerParams(vmem_limit_bytes=VMEM_LIMIT),
        name="modal_scan",
        interpret=interpret,
    )(dev, ids, picks, feat, border, filt, decay, angle, res, skip, entry)


def carry_kernel(dev_ref, ids, carry, pole, res, query, base, gated_out, tables, added, stage, small):
    position = dev_ref[0] * ROWS
    before = record_of(ids, position - 1)
    for part in range(2):
        for half in range(2):
            spread(small, 0, res[part, 8 * half : 8 * half + 8, :])
            for r in range(8):
                tables[part, 8 * half + r] = row(small, 0, r)
    for m in range(MODES):
        cr, ci = carry[0, m], carry[1, m]
        rr, ri = tables[0, m], tables[1, m]
        tables[0, m] = rr * cr - ri * ci
        tables[1, m] = rr * ci + ri * cr

    for group in range(2):
        modes = range(8 * group, 8 * group + 8)

        def block(b, carry, modes=modes, group=group):
            first = position + 8 * b

            @pl.when(ids[first] == before)
            def _():
                re = [tables[0, m] for m in modes]
                im = [tables[1, m] for m in modes]
                for t in range(8):
                    out = None
                    for m in range(8):
                        pr, pi = pole[0, modes[m]], pole[1, modes[m]]
                        re[m], im[m] = pr * re[m] - pi * im[m], pr * im[m] + pi * re[m]
                        out = re[m] if out is None else out + re[m]
                    out = jnp.where(ids[first + t] == before, out, 0.0)
                    if group == 0:
                        added[8 * b + t] = out
                    else:
                        added[8 * b + t] = added[8 * b + t] + out
                for m in range(8):
                    tables[0, modes[m]] = re[m]
                    tables[1, modes[m]] = im[m]

            if group == 0:

                @pl.when(ids[first] != before)
                def _():
                    for t in range(8):
                        added[8 * b + t] = jnp.zeros((8, LANES), F32)

            return carry

        lax.fori_loop(0, ROWS // 8, block, 0)

    def gate(b, carry):
        for half in range(2):
            for t in range(8):
                at = 16 * b + 8 * half + t
                value = query[at] * (base[at] + added[at])
                stage[pl.ds((2 * b + half) * BLOCK + t, TILES, stride=GAP), :] = value
        for j in range(TILES):
            low = stage[pl.ds(2 * b * BLOCK + j * GAP, 8), :]
            high = stage[pl.ds((2 * b + 1) * BLOCK + j * GAP, 8), :]
            both = jnp.concatenate([low, high], axis=0).astype(BF16)
            gated_out[pl.ds(pl.multiple_of(16 * b, 16), 16), j * LANES : (j + 1) * LANES] = both
        return carry

    lax.fori_loop(0, ROWS // 16, gate, 0)


def carried(dev, ids, carry, pole, res, query, base, interpret=False):
    smem = pl.BlockSpec(memory_space=pltpu.SMEM)
    vmem = pl.BlockSpec(memory_space=pltpu.VMEM)
    wide = (8, LANES)
    return pl.pallas_call(
        carry_kernel,
        out_shape=jax.ShapeDtypeStruct((ROWS, CH), BF16),
        in_specs=[smem, smem] + [vmem] * 5,
        out_specs=vmem,
        scratch_shapes=[
            pltpu.VMEM((2, MODES) + wide, F32),
            pltpu.VMEM((ROWS,) + wide, F32),
            pltpu.VMEM((ROWS // 8 * BLOCK, LANES), F32),
            pltpu.VMEM((BLOCK, LANES), F32),
        ],
        compiler_params=pltpu.CompilerParams(vmem_limit_bytes=VMEM_LIMIT),
        name="carry_gate",
        interpret=interpret,
    )(dev, ids, carry, pole, res, query, base)


def product_kernel(core_ref, rows_ref, weight_ref, out_ref):
    out_ref[...] = jnp.dot(rows_ref[...], weight_ref[0], preferred_element_type=F32).astype(BF16)


def partial_products(core, rows, weight):
    return pl.pallas_call(
        product_kernel,
        out_shape=jax.ShapeDtypeStruct((2, 4 * ROWS, CH), BF16),
        grid_spec=pltpu.PrefetchScalarGridSpec(
            num_scalar_prefetch=1,
            grid=(8,),
            in_specs=[
                pl.BlockSpec((4 * ROWS, CH), lambda n, core: (0, 0)),
                pl.BlockSpec((1, CH, 256), lambda n, core: ((n + 4 * core[0]) % 8, 0, 0)),
            ],
            out_specs=pl.BlockSpec((None, 4 * ROWS, 256), lambda n, core: (n // 4, 0, n % 4)),
        ),
        compiler_params=pltpu.CompilerParams(vmem_limit_bytes=VMEM_LIMIT),
        name="partial_products",
    )(core, rows, weight)


def add_complex(own, other, power, keep):
    other = other.astype(F32)
    power = power * keep
    re = power[0] * other[0] - power[1] * other[1]
    im = power[0] * other[1] + power[1] * other[0]
    return own.astype(F32) + jnp.stack([re, im])


def square(power):
    return jnp.stack([power[0] * power[0] - power[1] * power[1], 2.0 * power[0] * power[1]])


def shift_records(value, steps):
    return lax.ppermute(value, ("y", "z"), [(i, i + steps) for i in range(32 - steps)])


def shards(
    features, short_filter, decay, angle_rate, residues, skip, entry_states, segment_ids, state_ids, out_weight
):
    y, z = lax.axis_index("y"), lax.axis_index("z")
    x, core = lax.axis_index("x"), lax.axis_index("core")
    device = y * 8 + z
    weight = lax.all_gather(out_weight, "z", axis=0)
    border = shift_records(features[:, ROWS - 8 :, :], 1)
    filt = jnp.repeat(short_filter.astype(F32), 16, axis=2).reshape(TAPS, 3, 8, LANES)
    dev = device.reshape(1).astype(jnp.int32)
    final, pole, power, query, base = scan(
        dev, segment_ids, state_ids, features, border, filt, decay, angle_rate, residues,
        skip.reshape(1, CH), entry_states,
    )
    power1 = power.reshape(2, MODES * 8, LANES)
    power2 = square(power1)
    power4 = square(power2)

    def keep(count):
        first = (device - count) * ROWS - 1
        last = device * ROWS - 1
        same = segment_ids[jnp.maximum(first, 0)] == segment_ids[jnp.maximum(last, 0)]
        return jnp.logical_and(first >= 0, same).astype(F32)

    e1 = shift_records(final, 1)
    e2 = add_complex(e1, shift_records(e1, 1), power1, keep(1))
    e4 = add_complex(e2, shift_records(e2.astype(BF16), 2), power2, keep(2))
    e8 = add_complex(e4, shift_records(e4.astype(BF16), 4), power4, keep(4))
    gated = carried(dev, segment_ids, e8.reshape(2, MODES, 8, LANES), pole, residues, query, base)

    def offset(owner, y):
        return owner

    rows = [
        lax.ppermute(
            gated,
            ("y", "x"),
            [
                (((b + offset((a + k) % 4, b)) % 4) * 4 + a, b * 4 + a)
                for b in range(4)
                for a in range(4)
            ],
        )
        for k in range(4)
    ]
    rows = jnp.concatenate(rows, axis=0)
    parts = partial_products(core.reshape(1).astype(jnp.int32), rows, weight)
    other = lax.ppermute(parts[1], "core", [(0, 1), (1, 0)])
    pair = (parts[0].astype(F32) + other.astype(F32)).astype(BF16).reshape(4, ROWS, CH)
    total = pair[0].astype(F32)
    for k in range(1, 4):
        total = total + lax.ppermute(pair[k], "x", [(a, (a + k) % 4) for a in range(4)]).astype(F32)
    moves = [
        (b * 4 + a, ((b + offset(a, b)) % 4) * 4 + b) for b in range(4) for a in range(4)
    ]
    return lax.ppermute(total.astype(BF16), ("y", "x"), moves)


def solution(mesh):
    fine = Mesh(mesh.devices.reshape(4, 8, 4, 2), ("y", "z", "x", "core"))
    seq, chan = ("y", "z"), ("x", "core")
    in_specs = (
        P(None, seq, chan),
        P(None, None, chan),
        P(None, chan),
        P(None, chan),
        P(None, None, chan),
        P(chan),
        P(None, None, None, chan),
        P(),
        P(),
        P(chan, seq),
    )
    return jax.shard_map(shards, mesh=fine, in_specs=in_specs, out_specs=P(seq, chan), check_vma=False)
```

time: 1210 us -> 197 us (0.16)
  the two profiles are of different devices: /device:TPU:1 before, /device:TPU:24 now
where the time goes in v1:
time: 197 us; the launch traced here: 196 us
  waiting for transfers between devices  95.3 us (48%)
  starting transfers between devices  38.7 us (20%)
  Pallas kernels  31.4 us (16%)
  between operations  17.4 us (9%)
  local copies, waits for them, and re-layouts  7.51 us (4%)
  other arithmetic  5.56 us (3%)
    ppermute x5, waiting for transfers between devices, shift_records(): lax.ppermute(value, ('y', 'z'), [(i, i + steps) for i in range(32 - steps)])  28.6 us
    ppermute x1, waiting for transfers between devices, shards(): return lax.ppermute(total.astype(BF16), ('y', 'x'), moves)  24.4 us
    ppermute x3, waiting for transfers between devices, shards(): lax.ppermute(pair[k], 'x', [(a, (a + k) % 4) for a in range(4)]).astype(F32)  21.4 us
    ppermute x5, starting transfers between devices, shift_records(): lax.ppermute(value, ('y', 'z'), [(i, i + steps) for i in range(32 - steps)])  16.4 us
    ppermute x4, waiting for transfers between devices, shards(): lax.ppermute(gated, ('y', 'x'), [((b + offset((a + k) % 4, b)) % 4 * 4 +...  16 us
    pallas_call x1, Pallas kernels, scan(): pl.pallas_call(scan_kernel, out_shape=(jax.ShapeDtypeStruct((2, MODES * 8...  14.1 us
    ppermute x4, starting transfers between devices, shards(): lax.ppermute(gated, ('y', 'x'), [((b + offset((a + k) % 4, b)) % 4 * 4 +...  10.9 us
    pallas_call x1, Pallas kernels, partial_products(): pl.pallas_call(product_kernel, out_shape=jax.ShapeDtypeStruct((2, 4 * ROW...  10.1 us
  transfers between devices with their start and end apart: 15, of which 12 were waited for; matrix products, arithmetic and copies ran while one was open for 4% of the time, Pallas kernels for 11%

profile of v1, /device:TPU:24, one launch (start us, length us, event | category | flops | bytes accessed | tf_op | source)
XLA Modules:
  0.0 196.0 jit_solution(654113756373588653)
XLA Ops:
  6.5 0.0 all-gather.3.cloned.1.call-start
  6.5 0.7 all-gather.3.cloned.1.call-update
  7.3 0.8 slice.91
  8.1 3.8 %collective-permute-start = (bf16[3,8,1024]{2,1,0:T(8,128)(2,1)S(1)}, bf16[3,8,1024]{2,1,0:T(8,128)(2,1)S(1)}, u32[]{:S(2)}, u32[]{:S(2)}) collective-permute-start(bf16[3,8,1024]{2,1,0:T(8,128)(2,1)S(1)} %slice.91), channel_id=1, source_target_pairs={{0,8},{8,16},{16,24},{24,32},{32,40},{40,48},{48,56},{56,64},{64,7... | collective-permute-start | bytes 147464 | tf_op jit(solution)/shard_map/ppermute | solution.py:351
  11.9 1.5 fusion.5
  17.2 0.7 copy.12
  17.9 0.2 broadcast_in_dim.3
  18.1 0.9 reshape_reshape.3.filt
  19.0 0.0 collective-permute-done.border
  19.0 0.0 copy-start.1
  19.0 0.6 copy-done.1
  19.6 14.1 %modal_scan.1 = (bf16[2,128,128]{2,1,0:T(8,128)(2,1)}, f32[2,16,8,128]{3,2,1,0:T(8,128)}, f32[2,16,8,128]{3,2,1,0:T(8,128)}, f32[256,8,128]{2,1,0:T(8,128)}, f32[256,8,128]{2,1,0:T(8,128)}) custom-call(s32[1]{0:T(128)} %bitcast.1.dev_ref, s32[8192]{0:T(1024)} %ids.3, s32[8]{0:T(128)} %picks.1, bf16[3,256,1024]{2,1,0:T(8,128)(2,1)} %feat.1, ...), custom_call_target="tpu_custom_call" | custom-call | tf_op jit(solution)/shard_map/modal_scan/pallas_call | solution.py:205
  33.7 3.4 %collective-permute-start.1 = (bf16[2,128,128]{2,1,0:T(8,128)(2,1)}, bf16[2,128,128]{2,1,0:T(8,128)(2,1)S(1)}, u32[]{:S(2)}, u32[]{:S(2)}) collective-permute-start(bf16[2,128,128]{2,1,0:T(8,128)(2,1)} %get-tuple-element.10), channel_id=1, source_target_pairs={{0,8},{8,16},{16,24},{24,32},{32,40},{40,48},{48,56},{56,64},{64,7... | collective-permute-start | bytes 196616 | tf_op jit(solution)/shard_map/ppermute | solution.py:351
  37.1 0.9 broadcast_multiply_fusion
  38.1 0.9 multiply_subtract_fusion.1
  39.0 4.9 %collective-permute-done.1 = bf16[2,128,128]{2,1,0:T(8,128)(2,1)S(1)} collective-permute-done((bf16[2,128,128]{2,1,0:T(8,128)(2,1)}, bf16[2,128,128]{2,1,0:T(8,128)(2,1)S(1)}, u32[]{:S(2)}, u32[]{:S(2)}) %collective-permute-start.1) | collective-permute-done | bytes 65568 | tf_op jit(solution)/shard_map/ppermute | solution.py:351
  43.8 1.9 collective-permute-start.2
  45.8 7.7 %collective-permute-done.2 = bf16[2,128,128]{2,1,0:T(8,128)(2,1)S(1)} collective-permute-done((bf16[2,128,128]{2,1,0:T(8,128)(2,1)S(1)}, bf16[2,128,128]{2,1,0:T(8,128)(2,1)S(1)}, u32[]{:S(2)}, u32[]{:S(2)}) %collective-permute-start.2) | collective-permute-done | bytes 65568 | tf_op jit(solution)/shard_map/ppermute | solution.py:351
  53.5 1.9 collective-permute-start.3
  55.5 8.6 %collective-permute-done.3 = bf16[2,128,128]{2,1,0:T(8,128)(2,1)S(1)} collective-permute-done((bf16[2,128,128]{2,1,0:T(8,128)(2,1)S(1)}, bf16[2,128,128]{2,1,0:T(8,128)(2,1)S(1)}, u32[]{:S(2)}, u32[]{:S(2)}) %collective-permute-start.3) | collective-permute-done | bytes 65568 | tf_op jit(solution)/shard_map/ppermute | solution.py:351
  64.2 5.3 %collective-permute-start.4 = (bf16[2,128,128]{2,1,0:T(8,128)(2,1)S(1)}, bf16[2,128,128]{2,1,0:T(8,128)(2,1)S(1)}, u32[]{:S(2)}, u32[]{:S(2)}) collective-permute-start(bf16[2,128,128]{2,1,0:T(8,128)(2,1)S(1)} %fusion.3), channel_id=1, source_target_pairs={{0,32},{8,40},{16,48},{24,56},{32,64},{40,72},{48,80},{56,88},{64,... | collective-permute-start | bytes 196616 | tf_op jit(solution)/shard_map/ppermute | solution.py:351
  69.5 7.4 %collective-permute-done.4 = bf16[2,128,128]{2,1,0:T(8,128)(2,1)S(1)} collective-permute-done((bf16[2,128,128]{2,1,0:T(8,128)(2,1)S(1)}, bf16[2,128,128]{2,1,0:T(8,128)(2,1)S(1)}, u32[]{:S(2)}, u32[]{:S(2)}) %collective-permute-start.4) | collective-permute-done | bytes 65568 | tf_op jit(solution)/shard_map/ppermute | solution.py:351
  76.9 0.7 fusion.1.carry
  77.6 7.2 %carry_gate.1 = bf16[256,1024]{1,0:T(8,128)(2,1)} custom-call(s32[1]{0:T(128)} %bitcast.1.dev_ref, s32[8192]{0:T(1024)} %ids.3, f32[2,16,8,128]{3,2,1,0:T(8,128)} %fusion.1.carry, f32[2,16,8,128]{3,2,1,0:T(8,128)} %get-tuple-element.12.pole, f32[2,16,1024]{2,1,0:T(8,128)} %res.3, f32[256,8,128]{2,1,0:T(8,128)} %get-tuple-element.13.query, ...), custom_call_target="tpu_custom_call" | custom-call | tf_op jit(solution)/shard_map/carry_gate/pallas_call | solution.py:299
  84.9 1.9 collective-permute-start.8
  86.8 4.6 %collective-permute-start.7 = (bf16[256,1024]{1,0:T(8,128)(2,1)}, bf16[256,1024]{1,0:T(8,128)(2,1)S(1)}, u32[]{:S(2)}, u32[]{:S(2)}) collective-permute-start(bf16[256,1024]{1,0:T(8,128)(2,1)} %carry_gate.1), channel_id=1, source_target_pairs={{128,0},{194,2},{4,4},{70,6},{192,64},{2,66},{68,68},{134,70},{0,1... | collective-permute-start | bytes 1572872 | tf_op jit(solution)/shard_map/ppermute | solution.py:388
  91.4 2.7 %collective-permute-start.6 = (bf16[256,1024]{1,0:T(8,128)(2,1)}, bf16[256,1024]{1,0:T(8,128)(2,1)S(1)}, u32[]{:S(2)}, u32[]{:S(2)}) collective-permute-start(bf16[256,1024]{1,0:T(8,128)(2,1)} %carry_gate.1), channel_id=1, source_target_pairs={{64,0},{130,2},{196,4},{6,6},{128,64},{194,66},{4,68},{70,70},{192... | collective-permute-start | bytes 1572872 | tf_op jit(solution)/shard_map/ppermute | solution.py:388
  94.1 1.7 collective-permute-start.5
  95.8 6.0 %collective-permute-done.8 = bf16[256,1024]{1,0:T(8,128)(2,1)S(1)} collective-permute-done((bf16[256,1024]{1,0:T(8,128)(2,1)}, bf16[256,1024]{1,0:T(8,128)(2,1)S(1)}, u32[]{:S(2)}, u32[]{:S(2)}) %collective-permute-start.8) | collective-permute-done | bytes 524320 | tf_op jit(solution)/shard_map/ppermute | solution.py:388
  101.8 3.5 %collective-permute-done.7 = bf16[256,1024]{1,0:T(8,128)(2,1)S(1)} collective-permute-done((bf16[256,1024]{1,0:T(8,128)(2,1)}, bf16[256,1024]{1,0:T(8,128)(2,1)S(1)}, u32[]{:S(2)}, u32[]{:S(2)}) %collective-permute-start.7) | collective-permute-done | bytes 524320 | tf_op jit(solution)/shard_map/ppermute | solution.py:388
  105.3 6.5 %collective-permute-done.6 = bf16[256,1024]{1,0:T(8,128)(2,1)S(1)} collective-permute-done((bf16[256,1024]{1,0:T(8,128)(2,1)}, bf16[256,1024]{1,0:T(8,128)(2,1)S(1)}, u32[]{:S(2)}, u32[]{:S(2)}) %collective-permute-start.6) | collective-permute-done | bytes 524320 | tf_op jit(solution)/shard_map/ppermute | solution.py:388
  111.8 0.0 collective-permute-done.5
  111.8 1.6 pad_maximum_fusion.rows_ref
  113.4 0.0 all-gather.3.cloned.1.call-done
  113.4 10.1 %partial_products.1 = bf16[2,1024,1024]{2,1,0:T(8,128)(2,1)} custom-call(s32[1]{0:T(128)} %bitcast.core_ref, bf16[1024,1024]{1,0:T(8,128)(2,1)} %pad_maximum_fusion.rows_ref, bf16[8,1024,256]{2,1,0:T(8,128)(2,1)} %bitcast.36), custom_call_target="tpu_custom_call" | custom-call | tf_op jit(solution)/shard_map/partial_products/pallas_call | solution.py:321
  123.4 0.0 copy-start
  123.4 1.9 slice_bitcast_fusion
  125.4 0.1 collective-permute-start.9
  125.5 4.1 %collective-permute-done.9 = bf16[1024,1024]{1,0:T(8,128)(2,1)S(1)} collective-permute-done((bf16[1024,1024]{1,0:T(8,128)(2,1)S(1)}, bf16[1024,1024]{1,0:T(8,128)(2,1)S(1)}, u32[]{:S(2)}, u32[]{:S(2)}) %collective-permute-start.9) | collective-permute-done | bytes 2097184 | tf_op jit(solution)/shard_map/ppermute | solution.py:401
  129.6 0.0 copy-done
  129.6 1.0 fusion
  130.6 0.1 fusion.4
  130.7 3.3 %collective-permute-start.10 = (bf16[256,1024]{1,0:T(8,128)(2,1)S(1)}, bf16[256,1024]{1,0:T(8,128)(2,1)S(1)}, u32[]{:S(2)}, u32[]{:S(2)}) collective-permute-start(bf16[256,1024]{1,0:T(8,128)(2,1)S(1)} %get-tuple-element.18), channel_id=1, source_target_pairs={{0,2},{2,4},{4,6},{6,0},{1,3},{3,5},{5,7},{7,1},{8,10},{10,12},{12... | collective-permute-start | bytes 1572872 | tf_op jit(solution)/shard_map/ppermute | solution.py:405
  134.0 0.0 collective-permute-start.12
  134.0 2.6 %collective-permute-start.11 = (bf16[256,1024]{1,0:T(8,128)(2,1)S(1)}, bf16[256,1024]{1,0:T(8,128)(2,1)S(1)}, u32[]{:S(2)}, u32[]{:S(2)}) collective-permute-start(bf16[256,1024]{1,0:T(8,128)(2,1)S(1)} %get-tuple-element.20), channel_id=1, source_target_pairs={{0,4},{2,6},{4,0},{6,2},{1,5},{3,7},{5,1},{7,3},{8,12},{10,14},{12... | collective-permute-start | bytes 1572872 | tf_op jit(solution)/shard_map/ppermute | solution.py:405
  136.6 9.7 %collective-permute-done.10 = bf16[256,1024]{1,0:T(8,128)(2,1)S(1)} collective-permute-done((bf16[256,1024]{1,0:T(8,128)(2,1)S(1)}, bf16[256,1024]{1,0:T(8,128)(2,1)S(1)}, u32[]{:S(2)}, u32[]{:S(2)}) %collective-permute-start.10) | collective-permute-done | bytes 524320 | tf_op jit(solution)/shard_map/ppermute | solution.py:405
  146.3 2.5 %collective-permute-done.12 = bf16[256,1024]{1,0:T(8,128)(2,1)S(1)} collective-permute-done((bf16[256,1024]{1,0:T(8,128)(2,1)S(1)}, bf16[256,1024]{1,0:T(8,128)(2,1)S(1)}, u32[]{:S(2)}, u32[]{:S(2)}) %collective-permute-start.12) | collective-permute-done | bytes 524320 | tf_op jit(solution)/shard_map/ppermute | solution.py:405
  148.8 9.2 %collective-permute-done.11 = bf16[256,1024]{1,0:T(8,128)(2,1)S(1)} collective-permute-done((bf16[256,1024]{1,0:T(8,128)(2,1)S(1)}, bf16[256,1024]{1,0:T(8,128)(2,1)S(1)}, u32[]{:S(2)}, u32[]{:S(2)}) %collective-permute-start.11) | collective-permute-done | bytes 524320 | tf_op jit(solution)/shard_map/ppermute | solution.py:405
  158.1 0.4 add_convert_fusion
  158.4 5.4 %collective-permute-start.13 = (bf16[256,1024]{1,0:T(8,128)(2,1)S(1)}, bf16[256,1024]{1,0:T(8,128)(2,1)S(1)}, u32[]{:S(2)}, u32[]{:S(2)}) collective-permute-start(bf16[256,1024]{1,0:T(8,128)(2,1)S(1)} %add_convert_fusion), channel_id=1, source_target_pairs={{0,0},{2,64},{4,128},{6,192},{64,66},{66,130},{68,194},{70,2},{128... | collective-permute-start | bytes 1572872 | tf_op jit(solution)/shard_map/ppermute | solution.py:409
  163.9 24.4 %collective-permute-done.13 = bf16[256,1024]{1,0:T(8,128)(2,1)S(1)} collective-permute-done((bf16[256,1024]{1,0:T(8,128)(2,1)S(1)}, bf16[256,1024]{1,0:T(8,128)(2,1)S(1)}, u32[]{:S(2)}, u32[]{:S(2)}) %collective-permute-start.13) | collective-permute-done | bytes 524320 | tf_op jit(solution)/shard_map/ppermute | solution.py:409
  188.3 0.8 copy.14
  (11 shorter events, 0.2 us)
Async XLA Ops:
  6.5 106.8 %all-gather.3.cloned.1.call-start = ((), (), s32[]{:S(2)}) async-start(), calls=%async_computation | async-start | bytes 4718592 | tf_op jit(solution)/shard_map/all_gather | solution.py:360
  8.1 10.9 %collective-permute-start = (bf16[3,8,1024]{2,1,0:T(8,128)(2,1)S(1)}, bf16[3,8,1024]{2,1,0:T(8,128)(2,1)S(1)}, u32[]{:S(2)}, u32[]{:S(2)}) collective-permute-start(bf16[3,8,1024]{2,1,0:T(8,128)(2,1)S(1)} %slice.91), channel_id=1, source_target_pairs={{0,8},{8,16},{16,24},{24,32},{32,40},{40,48},{48,56},{56,64},{64,7... | collective-permute-start | bytes 147464 | tf_op jit(solution)/shard_map/ppermute | solution.py:351
  19.0 0.6 copy-start.1
  33.7 10.1 %collective-permute-start.1 = (bf16[2,128,128]{2,1,0:T(8,128)(2,1)}, bf16[2,128,128]{2,1,0:T(8,128)(2,1)S(1)}, u32[]{:S(2)}, u32[]{:S(2)}) collective-permute-start(bf16[2,128,128]{2,1,0:T(8,128)(2,1)} %get-tuple-element.10), channel_id=1, source_target_pairs={{0,8},{8,16},{16,24},{24,32},{32,40},{40,48},{48,56},{56,64},{64,7... | collective-permute-start | bytes 196616 | tf_op jit(solution)/shard_map/ppermute | solution.py:351
  43.8 9.6 %collective-permute-start.2 = (bf16[2,128,128]{2,1,0:T(8,128)(2,1)S(1)}, bf16[2,128,128]{2,1,0:T(8,128)(2,1)S(1)}, u32[]{:S(2)}, u32[]{:S(2)}) collective-permute-start(bf16[2,128,128]{2,1,0:T(8,128)(2,1)S(1)} %collective-permute-done.1), channel_id=1, source_target_pairs={{0,8},{8,16},{16,24},{24,32},{32,40},{40,48},{48,56},{56,64},{64,7... | collective-permute-start | bytes 196616 | tf_op jit(solution)/shard_map/ppermute | solution.py:351
  53.5 10.5 %collective-permute-start.3 = (bf16[2,128,128]{2,1,0:T(8,128)(2,1)S(1)}, bf16[2,128,128]{2,1,0:T(8,128)(2,1)S(1)}, u32[]{:S(2)}, u32[]{:S(2)}) collective-permute-start(bf16[2,128,128]{2,1,0:T(8,128)(2,1)S(1)} %fusion.2), channel_id=1, source_target_pairs={{0,16},{8,24},{16,32},{24,40},{32,48},{40,56},{48,64},{56,72},{64,... | collective-permute-start | bytes 196616 | tf_op jit(solution)/shard_map/ppermute | solution.py:351
  64.2 12.7 %collective-permute-start.4 = (bf16[2,128,128]{2,1,0:T(8,128)(2,1)S(1)}, bf16[2,128,128]{2,1,0:T(8,128)(2,1)S(1)}, u32[]{:S(2)}, u32[]{:S(2)}) collective-permute-start(bf16[2,128,128]{2,1,0:T(8,128)(2,1)S(1)} %fusion.3), channel_id=1, source_target_pairs={{0,32},{8,40},{16,48},{24,56},{32,64},{40,72},{48,80},{56,88},{64,... | collective-permute-start | bytes 196616 | tf_op jit(solution)/shard_map/ppermute | solution.py:351
  84.9 17.0 %collective-permute-start.8 = (bf16[256,1024]{1,0:T(8,128)(2,1)}, bf16[256,1024]{1,0:T(8,128)(2,1)S(1)}, u32[]{:S(2)}, u32[]{:S(2)}) collective-permute-start(bf16[256,1024]{1,0:T(8,128)(2,1)} %carry_gate.1), channel_id=1, source_target_pairs={{192,0},{2,2},{68,4},{134,6},{0,64},{66,66},{132,68},{198,70},{64,... | collective-permute-start | bytes 1572872 | tf_op jit(solution)/shard_map/ppermute | solution.py:388
  86.8 18.5 %collective-permute-start.7 = (bf16[256,1024]{1,0:T(8,128)(2,1)}, bf16[256,1024]{1,0:T(8,128)(2,1)S(1)}, u32[]{:S(2)}, u32[]{:S(2)}) collective-permute-start(bf16[256,1024]{1,0:T(8,128)(2,1)} %carry_gate.1), channel_id=1, source_target_pairs={{128,0},{194,2},{4,4},{70,6},{192,64},{2,66},{68,68},{134,70},{0,1... | collective-permute-start | bytes 1572872 | tf_op jit(solution)/shard_map/ppermute | solution.py:388
  91.4 20.4 %collective-permute-start.6 = (bf16[256,1024]{1,0:T(8,128)(2,1)}, bf16[256,1024]{1,0:T(8,128)(2,1)S(1)}, u32[]{:S(2)}, u32[]{:S(2)}) collective-permute-start(bf16[256,1024]{1,0:T(8,128)(2,1)} %carry_gate.1), channel_id=1, source_target_pairs={{64,0},{130,2},{196,4},{6,6},{128,64},{194,66},{4,68},{70,70},{192... | collective-permute-start | bytes 1572872 | tf_op jit(solution)/shard_map/ppermute | solution.py:388
  94.1 17.7 %collective-permute-start.5 = (bf16[256,1024]{1,0:T(8,128)(2,1)}, bf16[256,1024]{1,0:T(8,128)(2,1)S(1)}, u32[]{:S(2)}, u32[]{:S(2)}) collective-permute-start(bf16[256,1024]{1,0:T(8,128)(2,1)} %carry_gate.1), channel_id=1, source_target_pairs={{0,0},{66,2},{132,4},{198,6},{64,64},{130,66},{196,68},{6,70},{128... | collective-permute-start | bytes 1572872 | tf_op jit(solution)/shard_map/ppermute | solution.py:388
  123.4 6.2 %copy-start = (bf16[2,1024,1024]{2,1,0:T(8,128)(2,1)S(1)}, bf16[2,1024,1024]{2,1,0:T(8,128)(2,1)}, u32[]{:S(2)}) copy-start(bf16[2,1024,1024]{2,1,0:T(8,128)(2,1)} %partial_products.1) | copy-start | bytes 12582916
  125.4 4.2 %collective-permute-start.9 = (bf16[1024,1024]{1,0:T(8,128)(2,1)S(1)}, bf16[1024,1024]{1,0:T(8,128)(2,1)S(1)}, u32[]{:S(2)}, u32[]{:S(2)}) collective-permute-start(bf16[1024,1024]{1,0:T(8,128)(2,1)S(1)} %slice_bitcast_fusion), channel_id=1, source_target_pairs={{0,1},{1,0},{2,3},{3,2},{4,5},{5,4},{6,7},{7,6},{8,9},{9,8},{10,11... | collective-permute-start | bytes 6291464 | tf_op jit(solution)/shard_map/ppermute | solution.py:401
  130.7 15.6 %collective-permute-start.10 = (bf16[256,1024]{1,0:T(8,128)(2,1)S(1)}, bf16[256,1024]{1,0:T(8,128)(2,1)S(1)}, u32[]{:S(2)}, u32[]{:S(2)}) collective-permute-start(bf16[256,1024]{1,0:T(8,128)(2,1)S(1)} %get-tuple-element.18), channel_id=1, source_target_pairs={{0,2},{2,4},{4,6},{6,0},{1,3},{3,5},{5,7},{7,1},{8,10},{10,12},{12... | collective-permute-start | bytes 1572872 | tf_op jit(solution)/shard_map/ppermute | solution.py:405
  134.0 14.8 %collective-permute-start.12 = (bf16[256,1024]{1,0:T(8,128)(2,1)S(1)}, bf16[256,1024]{1,0:T(8,128)(2,1)S(1)}, u32[]{:S(2)}, u32[]{:S(2)}) collective-permute-start(bf16[256,1024]{1,0:T(8,128)(2,1)S(1)} %get-tuple-element.19), channel_id=1, source_target_pairs={{0,6},{2,0},{4,2},{6,4},{1,7},{3,1},{5,3},{7,5},{8,14},{10,8},{12,... | collective-permute-start | bytes 1572872 | tf_op jit(solution)/shard_map/ppermute | solution.py:405
  134.0 24.0 %collective-permute-start.11 = (bf16[256,1024]{1,0:T(8,128)(2,1)S(1)}, bf16[256,1024]{1,0:T(8,128)(2,1)S(1)}, u32[]{:S(2)}, u32[]{:S(2)}) collective-permute-start(bf16[256,1024]{1,0:T(8,128)(2,1)S(1)} %get-tuple-element.20), channel_id=1, source_target_pairs={{0,4},{2,6},{4,0},{6,2},{1,5},{3,7},{5,1},{7,3},{8,12},{10,14},{12... | collective-permute-start | bytes 1572872 | tf_op jit(solution)/shard_map/ppermute | solution.py:405
  158.4 29.9 %collective-permute-start.13 = (bf16[256,1024]{1,0:T(8,128)(2,1)S(1)}, bf16[256,1024]{1,0:T(8,128)(2,1)S(1)}, u32[]{:S(2)}, u32[]{:S(2)}) collective-permute-start(bf16[256,1024]{1,0:T(8,128)(2,1)S(1)} %add_convert_fusion), channel_id=1, source_target_pairs={{0,0},{2,64},{4,128},{6,192},{64,66},{66,130},{68,194},{70,2},{128... | collective-permute-start | bytes 1572872 | tf_op jit(solution)/shard_map/ppermute | solution.py:409
Sparse Core Ops, SparseCore 0:
  9.1 60.2 all-gather.2

commit v2 on v0

v2 whole, which is shorter than its diff:
```python
import jax
import jax.numpy as jnp
from jax import lax
from jax.experimental import pallas as pl
from jax.experimental.pallas import tpu as pltpu
from jax.sharding import Mesh
from jax.sharding import PartitionSpec as P

F32 = jnp.float32
BF16 = jnp.bfloat16
ROWS = 256
CH = 1024
LANES = 128
TILES = CH // LANES
MODES = 16
TAPS = 7
GROUP = 16
GAP = 9
BLOCK = GAP * TILES
COLS = 256
WIDE = (8, LANES)
MIB = 1024 * 1024
SMEM_SPEC = pl.BlockSpec(memory_space=pltpu.SMEM)
VMEM_SPEC = pl.BlockSpec(memory_space=pltpu.VMEM)


def call(kernel, outs, in_specs, scratch, limit, name, cycles, interpret=False):
    return pl.pallas_call(
        kernel,
        out_shape=outs,
        in_specs=in_specs,
        out_specs=jax.tree.map(lambda out: VMEM_SPEC, outs),
        scratch_shapes=scratch,
        compiler_params=pltpu.CompilerParams(vmem_limit_bytes=limit * MIB),
        cost_estimate=pl.CostEstimate(flops=cycles, transcendentals=0, bytes_accessed=MIB),
        name=name,
        interpret=interpret,
    )


def first_position():
    device = (lax.axis_index("y") * 4 + lax.axis_index("zh")) * 2 + lax.axis_index("zl")
    return device * ROWS


def spread(scratch, base, value):
    for j in range(TILES):
        scratch[pl.ds(base + j * GAP, value.shape[0]), :] = value[:, j * LANES : (j + 1) * LANES]


def row(scratch, base, r):
    return scratch[pl.ds(base + r, TILES, stride=GAP), :]


def record_of(ids, position):
    return jnp.where(position < 0, -1, ids[jnp.maximum(position, 0)])


def prepare_kernel(ids, feat, filt, decay, angle, pole_out, power_out, taps_out, streams_out, edge_out, small):
    position = first_position()
    edge_out[...] = feat[:, ROWS - 8 :, :]
    for half in range(2):
        rows = slice(8 * half, 8 * half + 8)
        mag = jnp.exp(-decay[rows, :])
        ang = angle[rows, :]
        spread(small, 0, mag * jnp.cos(ang))
        spread(small, BLOCK, mag * jnp.sin(ang))
        for r in range(8):
            pole_out[0, 8 * half + r] = row(small, 0, r)
            pole_out[1, 8 * half + r] = row(small, BLOCK, r)
    last = record_of(ids, position - 1)
    keeps = []
    for count in (1, 2, 4, 6):
        before = position - count * ROWS - 1
        keeps.append(jnp.where((before >= 0) & (record_of(ids, before) == last), 1.0, 0.0))
    for m in range(MODES):
        re, im = pole_out[0, m], pole_out[1, m]
        for doubling in range(8):
            re, im = re * re - im * im, 2.0 * re * im
        powers = [(re, im)]
        for doubling in range(2):
            re, im = re * re - im * im, 2.0 * re * im
            powers.append((re, im))
        two = powers[1]
        powers.append((re * two[0] - im * two[1], re * two[1] + im * two[0]))
        for n in range(4):
            power_out[n, 0, m] = powers[n][0] * keeps[n]
            power_out[n, 1, m] = powers[n][1] * keeps[n]
    groups = CH // GROUP
    group = lax.broadcasted_iota(jnp.int32, (groups, CH), 0)
    channel = lax.broadcasted_iota(jnp.int32, (groups, CH), 1)
    widen = jnp.where(channel // GROUP == group, 1.0, 0.0).astype(BF16)
    for i in range(3):
        spread(small, 0, jnp.dot(filt[i], widen, preferred_element_type=F32))
        for j in range(TAPS):
            taps_out[j, i] = row(small, 0, j)

    def lay_out(b, carry):
        for i in range(3):
            value = feat[i, pl.ds(pl.multiple_of(b * 16, 16), 16), :].astype(F32)
            spread(streams_out.at[i], 2 * b * BLOCK, value[:8])
            spread(streams_out.at[i], (2 * b + 1) * BLOCK, value[8:])
        return carry

    lax.fori_loop(0, ROWS // 16, lay_out, 0)


def prepare(ids, feat, filt, decay, angle):
    return call(
        prepare_kernel,
        (
            jax.ShapeDtypeStruct((2, MODES) + WIDE, F32),
            jax.ShapeDtypeStruct((4, 2, MODES) + WIDE, F32),
            jax.ShapeDtypeStruct((TAPS, 3) + WIDE, F32),
            jax.ShapeDtypeStruct((3, ROWS // 8 * BLOCK, LANES), F32),
            jax.ShapeDtypeStruct((3, 8, CH), BF16),
        ),
        [SMEM_SPEC] + [VMEM_SPEC] * 4,
        [pltpu.VMEM((2 * BLOCK, LANES), F32)],
        16,
        "prepare",
        3_000_000,
    )(ids, feat, filt, decay, angle)


def featurized(i, b, before, stream, taps_ref, same):
    values = [row(before[0], before[1], 2 + r) for r in range(6)]
    values += [row(stream, b * BLOCK, r) for r in range(8)]
    taps = [taps_ref[j, i] for j in range(TAPS)]
    outs = []
    for t in range(8):
        out = taps[0] * values[6 + t]
        for j in range(1, TAPS):
            value = values[6 + t - j]
            if same is not None:
                value = jnp.where(same[t][j], value, 0.0)
            out = out + taps[j] * value
        outs.append(out)
    return outs


def featurize(position, ids, which, streams, edge, taps, emit):
    def block(b, before):
        first = position + 8 * b
        plain = record_of(ids, first - 6) == ids[first + 7]

        def run(same):
            emit(b, [featurized(i, b, before(i), streams.at[i], taps, same) for i in which])

        @pl.when(plain)
        def _():
            run(None)

        @pl.when(jnp.logical_not(plain))
        def _():
            run([[record_of(ids, first + t - j) == ids[first + t] for j in range(TAPS)] for t in range(8)])

    block(0, lambda i: (edge, i * BLOCK))

    def step(b, carry):
        block(b, lambda i: (streams.at[i], (b - 1) * BLOCK))
        return carry

    lax.fori_loop(1, ROWS // 8, step, 0)


def run_modes(position, ids, picks, entry, states, small, product, group, step, emit, carry_in=None):
    for part in range(2):
        for m in range(8):
            states[part, m] = jnp.zeros(WIDE, F32) if carry_in is None else carry_in[part, 8 * group + m]

    def block(b, carry):
        first = position + 8 * b
        plain = record_of(ids, first - 1) == ids[first + 7]

        @pl.when(plain)
        def _():
            re = [states[0, m] for m in range(8)]
            im = [states[1, m] for m in range(8)]
            for t in range(8):
                value = product[8 * b + t]
                emit(8 * b + t, value, step(value, re, im))
            for m in range(8):
                states[0, m] = re[m]
                states[1, m] = im[m]

        @pl.when(jnp.logical_not(plain))
        def _():
            def one(t, carry):
                here = first + t

                @pl.when(record_of(ids, here - 1) != ids[here])
                def _():
                    pick = picks[ids[here]]
                    for part in range(2):
                        spread(small, 0, entry[pick, part, 8 * group : 8 * group + 8, :])
                        for m in range(8):
                            states[part, m] = row(small, 0, m)

                re = [states[0, m] for m in range(8)]
                im = [states[1, m] for m in range(8)]
                value = product[8 * b + t]
                emit(8 * b + t, value, step(value, re, im))
                for m in range(8):
                    states[0, m] = re[m]
                    states[1, m] = im[m]
                return carry

            lax.fori_loop(0, 8, one, 0)

        return carry

    lax.fori_loop(0, ROWS // 8, block, 0)


def final_kernel(ids, picks, streams, border, taps, pole, entry, final_out, product_out, edge, states, small):
    position = first_position()
    for i in (1, 2):
        spread(edge, i * BLOCK, border[i].astype(F32))

    def emit(b, outs):
        for t in range(8):
            product_out[8 * b + t] = (outs[0][t] * outs[1][t]).astype(BF16).astype(F32)

    featurize(position, ids, (1, 2), streams, edge, taps, emit)
    for group in range(2):

        def step(value, re, im, group=group):
            for m in range(8):
                pr, pi = pole[0, 8 * group + m], pole[1, 8 * group + m]
                re[m], im[m] = pr * re[m] - pi * im[m] + value, pr * im[m] + pi * re[m]

        run_modes(
            position, ids, picks, entry, states, small, product_out, group, step, lambda at, value, out: None
        )
        for part in range(2):
            for m in range(0, 8, 2):
                pair = jnp.concatenate([states[part, m], states[part, m + 1]], axis=0)
                at = 64 * group + 8 * m
                final_out[part, at : at + 16, :] = pair.astype(BF16)


def final_states(ids, picks, streams, border, taps, pole, entry):
    return call(
        final_kernel,
        (
            jax.ShapeDtypeStruct((2, MODES * 8, LANES), BF16),
            jax.ShapeDtypeStruct((ROWS,) + WIDE, F32),
        ),
        [SMEM_SPEC] * 2 + [VMEM_SPEC] * 5,
        [
            pltpu.VMEM((3 * BLOCK, LANES), F32),
            pltpu.VMEM((2, 8) + WIDE, F32),
            pltpu.VMEM((BLOCK, LANES), F32),
        ],
        16,
        "final_states",
        8_000_000,
    )(ids, picks, streams, border, taps, pole, entry)


def query_kernel(ids, streams, border, taps, query_out, edge):
    spread(edge, 0, border[0].astype(F32))

    def emit(b, outs):
        for t in range(8):
            query_out[8 * b + t] = outs[0][t]

    featurize(first_position(), ids, (0,), streams, edge, taps, emit)


def featured_query(ids, streams, border, taps):
    return call(
        query_kernel,
        jax.ShapeDtypeStruct((ROWS,) + WIDE, F32),
        [SMEM_SPEC] + [VMEM_SPEC] * 3,
        [pltpu.VMEM((BLOCK, LANES), F32)],
        16,
        "featured_query",
        2_000_000,
    )(ids, streams, border, taps)


def residue_tables(res, tables, small, halves):
    for part in range(2):
        for half in halves:
            spread(small, 0, res[part, 8 * half : 8 * half + 8, :])
            for r in range(8):
                tables[part, 8 * half + r] = row(small, 0, r)


def modal_kernel(
    ids, picks, near, two, four, six, power, pole, res, skip, entry, product, query,
    gated_out, tables, carry_in, states, base, stage, small,
):
    for pair in range(MODES // 2):
        rows = slice(16 * pair, 16 * pair + 16)
        re, im = near[0, rows, :], near[1, rows, :]
        for n, ref in ((1, two), (2, four), (3, six)):
            other_re, other_im = ref[0, rows, :].astype(F32), ref[1, rows, :].astype(F32)
            power_re, power_im = power[n, 0, rows, :], power[n, 1, rows, :]
            re = re + power_re * other_re - power_im * other_im
            im = im + power_re * other_im + power_im * other_re
        for part, value in enumerate((re, im)):
            carry_in[part, 2 * pair] = value[:8]
            carry_in[part, 2 * pair + 1] = value[8:]

    residue_tables(res, tables, small, (0, 1))
    spread(small, 0, skip[...])
    skip_row = row(small, 0, 0)
    for group in range(2):

        def step(value, re, im, group=group):
            out = None
            for m in range(8):
                mode = 8 * group + m
                pr, pi = pole[0, mode], pole[1, mode]
                new_re = pr * re[m] - pi * im[m] + value
                new_im = pr * im[m] + pi * re[m]
                re[m], im[m] = new_re, new_im
                term = tables[0, mode] * new_re - tables[1, mode] * new_im
                out = term if out is None else out + term
            return out

        def emit(at, value, out, group=group):
            if group == 0:
                base[at] = skip_row * value + out
            else:
                value = query[at] * (base[at] + out)
                stage[pl.ds(at // 8 * BLOCK + at % 8, TILES, stride=GAP), :] = value

        run_modes(first_position(), ids, picks, entry, states, small, product, group, step, emit, carry_in)

    def gather(b, carry):
        for j in range(TILES):
            low = stage[pl.ds(2 * b * BLOCK + j * GAP, 8), :]
            high = stage[pl.ds((2 * b + 1) * BLOCK + j * GAP, 8), :]
            both = jnp.concatenate([low, high], axis=0).astype(BF16)
            gated_out[pl.ds(pl.multiple_of(16 * b, 16), 16), j * LANES : (j + 1) * LANES] = both
        return carry

    lax.fori_loop(0, ROWS // 16, gather, 0)


def gated_rows(ids, picks, near, two, four, six, power, pole, res, skip, entry, product, query):
    return call(
        modal_kernel,
        jax.ShapeDtypeStruct((ROWS, CH), BF16),
        [SMEM_SPEC] * 2 + [VMEM_SPEC] * 11,
        [
            pltpu.VMEM((2, MODES) + WIDE, F32),
            pltpu.VMEM((2, MODES) + WIDE, F32),
            pltpu.VMEM((2, 8) + WIDE, F32),
            pltpu.VMEM((ROWS,) + WIDE, F32),
            pltpu.VMEM((ROWS // 8 * BLOCK, LANES), F32),
            pltpu.VMEM((BLOCK, LANES), F32),
        ],
        20,
        "gated_rows",
        12_000_000,
    )(ids, picks, near, two, four, six, power, pole, res, skip, entry, product, query)


def partial_products(blocks, places, weights, name):
    rows = sum(part.stop - part.start for place in places for part, core in place) // 2

    def kernel(*refs):
        block_refs, weight_refs = refs[: len(blocks)], refs[len(blocks) : -2]
        out_ref, all_rows = refs[-2:]
        y, x = lax.axis_index("y"), lax.axis_index("x")
        zl, core = lax.axis_index("zl"), lax.axis_index("core")
        at = [0, rows]
        for ref, place in zip(block_refs, places):
            for part, owner in place:
                count = part.stop - part.start
                all_rows[at[owner] : at[owner] + count] = ref[part, :]
                at[owner] += count
        for which in range(2):
            own_y, next_y, last_y = [ref[which] for ref in weight_refs[:3]]
            for shift, weight in enumerate((own_y, next_y, weight_refs[3 + which][...], last_y)):
                slot = (y + shift - x + 4) % 4
                to = pl.multiple_of((zl + which) % 2 * COLS, COLS)
                part = jnp.dot(all_rows[...], weight, preferred_element_type=F32).astype(BF16)
                out_ref[core, slot, :, pl.ds(to, COLS)] = part[:rows]
                out_ref[1 - core, slot, :, pl.ds(to, COLS)] = part[rows:]

    return call(
        kernel,
        jax.ShapeDtypeStruct((2, 4, rows, 2 * COLS), BF16),
        [VMEM_SPEC] * (len(blocks) + 5),
        [pltpu.VMEM((2 * rows, CH), BF16)],
        24,
        name,
        1_000_000_000,
    )(*blocks, *weights)


def assemble_kernel(near_own, near_other, far_top, far_bottom, side, out_ref):
    zh, core = lax.axis_index("zh"), lax.axis_index("core")
    half = ROWS // 2
    same = pl.ds(pl.multiple_of(zh % 2 * 2 * COLS, 2 * COLS), 2 * COLS)
    other = pl.ds(pl.multiple_of((zh + 1) % 2 * 2 * COLS, 2 * COLS), 2 * COLS)

    @pl.when(zh // 2 == core)
    def _():
        out_ref[pl.ds(pl.multiple_of(core * half, half), half), same] = near_own[...]
        out_ref[pl.ds(pl.multiple_of((1 - core) * half, half), half), same] = near_other[...]

    @pl.when(zh // 2 != core)
    def _():
        out_ref[:half, same] = far_top[...]
        out_ref[half:, same] = far_bottom[...]

    out_ref[:, other] = side[...]


def add_complex(own, other, power):
    other = other.astype(F32)
    re = power[0] * other[0] - power[1] * other[1]
    im = power[0] * other[1] + power[1] * other[0]
    return own.astype(F32) + jnp.stack([re, im])


def shift_records(value, steps):
    return lax.ppermute(value, ("y", "zh", "zl"), [(i, i + steps) for i in range(32 - steps)])


def turn(value, axis, steps):
    return lax.ppermute(value, axis, [(i, (i + steps) % 4) for i in range(4)])


def tie(*values):
    return lax.optimization_barrier(values)


def shards(
    features, short_filter, decay, angle_rate, residues, skip, entry_states, segment_ids, state_ids, out_weight
):
    skip_row = skip.reshape(1, CH)
    pole, power, taps, streams, edge = prepare(
        segment_ids, features, short_filter.transpose(1, 0, 2), decay, angle_rate
    )
    power = power.reshape(4, 2, MODES * 8, LANES)
    border = shift_records(edge, 1)
    border, out_weight = tie(border, out_weight)
    paired = lax.ppermute(out_weight, "zl", [(0, 1), (1, 0)])
    final, product = final_states(segment_ids, state_ids, streams, border, taps, pole, entry_states)

    final, product = tie(final, product)
    last = shift_records(final, 1), shift_records(final, 2)
    query = featured_query(segment_ids, streams, border, taps)
    last, query, product, paired = tie(last, query, product, paired)
    near = add_complex(last[0], last[1], power[0])
    sent = near.astype(BF16)
    here = jnp.stack([out_weight, paired])
    lower, upper = turn(here, "y", 1), turn(here, "y", -1)
    gated = gated_rows(
        segment_ids, state_ids, near, *[shift_records(sent, steps) for steps in (2, 4, 6)],
        power, pole, residues, skip_row, entry_states, product, query,
    )

    gated, lower, upper = tie(gated, lower, upper)
    after, before = turn(gated, "zh", -1), turn(gated, "zh", 1)
    across, paired_across = turn(lower[0], "y", 1), turn(upper[1], "y", -1)
    weights = (here, upper, lower, across, paired_across)
    half = ROWS // 2
    top, bottom, whole = slice(0, half), slice(half, ROWS), slice(0, ROWS)
    after, before, weights = tie(after, before, weights)
    far = turn(after[top], "zh", -1), turn(before[bottom], "zh", 1)

    def over_cores(parts):
        other = lax.ppermute(parts[1], "core", [(0, 1), (1, 0)])
        return (parts[0].astype(F32) + other.astype(F32)).astype(BF16)

    def from_x(both, k):
        return turn(both[k], "x", k)

    def home(sums, moves):
        pairs = [(2 * zh + core, 2 * ((zh + step) % 4) + zh // 2) for zh in range(4) for core, step in moves]
        return lax.ppermute(sums, ("zh", "core"), pairs)

    def add(values):
        total = values[0].astype(F32)
        for value in values[1:]:
            total = total + value.astype(F32)
        return total.astype(BF16)

    places = [[(top, 0), (bottom, 1)], [(whole, 0)], [(whole, 1)]]
    one = over_cores(partial_products([gated, after, before], places, weights, "products_near"))
    one_1, one_3 = from_x(one, 1), from_x(one, 3)
    far, one, one_1, one_3 = tie(far, one, one_1, one_3)
    two = over_cores(partial_products(far, [[(top, 0)], [(top, 1)]], weights, "products_far"))
    one = add([one[0], one_1, from_x(one, 2), one_3])
    two = add([two[0]] + [from_x(two, k) for k in range(1, 4)])
    near_own = one[:half]
    near_other = lax.ppermute(near_own, "core", [(0, 1), (1, 0)])
    side = home(one[half:], [(0, 1), (1, 3)])
    far_top, far_bottom = home(two, [(0, 2)]), home(two, [(1, 2)])
    return call(
        assemble_kernel, jax.ShapeDtypeStruct((ROWS, CH), BF16), [VMEM_SPEC] * 5, [], 8, "assemble", 1_000_000
    )(near_own, near_other, far_top, far_bottom, side)


def solution(mesh):
    fine = Mesh(mesh.devices.reshape(4, 4, 2, 4, 2), ("y", "zh", "zl", "x", "core"))
    seq, chan = ("y", "zh", "zl"), ("x", "core")
    in_specs = (
        P(None, seq, chan),
        P(None, None, chan),
        P(None, chan),
        P(None, chan),
        P(None, None, chan),
        P(chan),
        P(None, None, None, chan),
        P(),
        P(),
        P(chan, seq),
    )
    return jax.shard_map(shards, mesh=fine, in_specs=in_specs, out_specs=P(seq, chan), check_vma=False)
```

time: 1210 us -> 160 us (0.13); the launches traced: 1190 us -> 160 us
  loops' own time: 483 us -> 0 us
  other arithmetic: 394 us -> 1.01 us
  waiting for transfers between devices: 215 us -> 54.4 us
  starting transfers between devices: 4.59 us -> 71.2 us
  local copies, waits for them, and re-layouts: 71.1 us -> 5.04 us
  Pallas kernels: 0 us -> 27.6 us
  between operations: 13.7 us -> 0.35 us
    another operation x3 -> x0, loops' own time: 483 us -> none  [the longest x1 481 us: local_modes(): lax.scan(local_block_step, (zeros, zeros), (product_f.reshape(blocks, ste...]
    mul x128 -> x0, other arithmetic: 157 us -> none  [carried_block_step(): flags[offset]]
    all_gather x5 -> x0, waiting for transfers between devices: 148 us -> none  [the longest x4 148 us: entering_2(): lax.all_gather(a.astype(kind), axis)]
    add x66 -> x0, other arithmetic: 116 us -> none  [the longest x48 92.3 us: local_block_step(): state_im = pole_re * before_im + pole_im * before_re]
    reduce_sum x112 -> x0, other arithmetic: 109 us -> none  [the longest x80 98.6 us: local_block_step(): jnp.sum(residues[0] * state_re - residues[1] * state_im, axis=0)]
    ppermute x1 -> x27, starting transfers between devices: 4.38 us -> 71.2 us  [the longest x14 25.1 us: turn(): return lax.ppermute(value, axis, [(i, (i + steps) % 4) for i in range(4)])]
    reduce_scatter x1 -> x0, waiting for transfers between devices: 65.6 us -> none  [shards(): lax.psum_scatter(terms.astype(jnp.bfloat16), 'chan', scatter_dimension=1,...]
    slice x67 -> x4, local copies, waits for them, and re-layouts: 57.8 us -> 0.07 us  [the longest x2 0.04 us: shards(): far = (turn(after[top], 'zh', -1), turn(before[bottom], 'zh', 1))]
  transfers between devices with their start and end apart: 7 -> 27, of which waited for: 3 -> 12; matrix products, arithmetic and copies ran while one was open for 38% -> 0% of each run, Pallas kernels for 0% -> 13%
where the time goes in v2:
time: 160 us
  starting transfers between devices  71.2 us (44%)
  waiting for transfers between devices  54.4 us (34%)
  Pallas kernels  27.6 us (17%)
  local copies, waits for them, and re-layouts  5.04 us (3%)
    ppermute x14, waiting for transfers between devices, turn(): return lax.ppermute(value, axis, [(i, (i + steps) % 4) for i in range(4)])  37.8 us
    ppermute x14, starting transfers between devices, turn(): return lax.ppermute(value, axis, [(i, (i + steps) % 4) for i in range(4)])  25.1 us
    ppermute x6, starting transfers between devices, shift_records(): lax.ppermute(value, ('y', 'zh', 'zl'), [(i, i + steps) for i in range(32...  22.2 us
    ppermute x3, starting transfers between devices, home(): return lax.ppermute(sums, ('zh', 'core'), pairs)  10.9 us
    ppermute x3, waiting for transfers between devices, home(): return lax.ppermute(sums, ('zh', 'core'), pairs)  10.9 us
    ppermute x2, starting transfers between devices, over_cores(): other = lax.ppermute(parts[1], 'core', [(0, 1), (1, 0)])  9.99 us
    pallas_call x1, Pallas kernels, gated_rows(): call(modal_kernel, jax.ShapeDtypeStruct((ROWS, CH), BF16), [SMEM_SPEC] *...  9.14 us
    pallas_call x1, Pallas kernels, final_states(): call(final_kernel, (jax.ShapeDtypeStruct((2, MODES * 8, LANES), BF16), ja...  8.68 us
  transfers between devices with their start and end apart: 27, of which 12 were waited for; matrix products, arithmetic and copies ran while one was open for 0% of the time, Pallas kernels for 13%

profile of v2, /device:TPU:1, one launch (start us, length us, event | category | flops | bytes accessed | tf_op | source)
XLA Modules:
  0.0 159.5 jit_solution(115762312878778496)
XLA Ops:
  0.0 1.5 copy-done.1
  1.5 0.8 copy-done.2
  2.3 0.8 copy-done.5
  3.1 0.8 copy-done.6
  3.9 0.7 copy-done.7
  4.6 1.7 %prepare.1 = (f32[2,16,8,128]{3,2,1,0:T(8,128)S(1)}, f32[4,2,16,8,128]{4,3,2,1,0:T(8,128)S(1)}, f32[7,3,8,128]{3,2,1,0:T(8,128)S(1)}, f32[3,2304,128]{2,1,0:T(8,128)S(1)}, bf16[3,8,1024]{2,1,0:T(8,128)(2,1)S(1)}) custom-call(s32[8192]{0:T(1024)S(1)} %copy-done.2, bf16[3,256,1024]{2,1,0:T(8,128)(2,1)S(1)} %copy-done.1, bf16[3,7,64]{2,1,0:T(8,128)(2,1)S(1)} %bitcast.58, ...), custom_call_target="tpu_custom_call" | custom-call | flops 3000000 | bytes 1048576 | tf_op jit(solution)/shard_map/prepare/pallas_call | solution.py:109
  6.4 4.4 %collective-permute-start = (bf16[3,8,1024]{2,1,0:T(8,128)(2,1)S(1)}, bf16[3,8,1024]{2,1,0:T(8,128)(2,1)S(1)}, u32[]{:S(2)}, u32[]{:S(2)}) collective-permute-start(bf16[3,8,1024]{2,1,0:T(8,128)(2,1)S(1)} %get-tuple-element.35), channel_id=1, source_target_pairs={{0,8},{8,16},{16,24},{24,32},{32,40},{40,48},{48,56},{56,64},{64,7... | collective-permute-start | bytes 147464 | tf_op jit(solution)/shard_map/ppermute | solution.py:425
  10.8 1.2 collective-permute-done.border
  11.9 1.8 %collective-permute-start.3 = (bf16[1024,256]{1,0:T(8,128)(2,1)S(1)}, bf16[1024,256]{1,0:T(8,128)(2,1)S(1)}, u32[]{:S(2)}, u32[]{:S(2)}) collective-permute-start(bf16[1024,256]{1,0:T(8,128)(2,1)S(1)} %copy-done.10), channel_id=1, source_target_pairs={{0,8},{8,0},{1,9},{9,1},{2,10},{10,2},{3,11},{11,3},{4,12},{12,4},... | collective-permute-start | bytes 1572872 | tf_op jit(solution)/shard_map/ppermute | solution.py:446
  13.7 8.7 %final_states.1 = (bf16[2,128,128]{2,1,0:T(8,128)(2,1)S(1)}, f32[256,8,128]{2,1,0:T(8,128)S(1)}) custom-call(s32[8192]{0:T(1024)S(1)} %copy-done.2, s32[8]{0:T(128)S(1)} %copy-done.9, f32[3,2304,128]{2,1,0:T(8,128)S(1)} %get-tuple-element.34.streams, bf16[3,8,1024]{2,1,0:T(8,128)(2,1)S(1)} %collective-permute-done.border, ...), custom_call_target="tpu_custom_call" | custom-call | flops 8000000 | bytes 1048576 | tf_op jit(solution)/shard_map/final_states/pallas_call | solution.py:244
  22.4 6.0 %collective-permute-start.2 = (bf16[2,128,128]{2,1,0:T(8,128)(2,1)S(1)}, bf16[2,128,128]{2,1,0:T(8,128)(2,1)S(1)}, u32[]{:S(2)}, u32[]{:S(2)}) collective-permute-start(bf16[2,128,128]{2,1,0:T(8,128)(2,1)S(1)} %get-tuple-element.39), channel_id=1, source_target_pairs={{0,16},{8,24},{16,32},{24,40},{32,48},{40,56},{48,64},{56,72},{64,... | collective-permute-start | bytes 196616 | tf_op jit(solution)/shard_map/ppermute | solution.py:425
  28.4 1.6 %collective-permute-start.1 = (bf16[2,128,128]{2,1,0:T(8,128)(2,1)S(1)}, bf16[2,128,128]{2,1,0:T(8,128)(2,1)S(1)}, u32[]{:S(2)}, u32[]{:S(2)}) collective-permute-start(bf16[2,128,128]{2,1,0:T(8,128)(2,1)S(1)} %get-tuple-element.39), channel_id=1, source_target_pairs={{0,8},{8,16},{16,24},{24,32},{32,40},{40,48},{48,56},{56,64},{64,7... | collective-permute-start | bytes 196616 | tf_op jit(solution)/shard_map/ppermute | solution.py:425
  30.0 2.3 %featured_query.1.query = f32[256,8,128]{2,1,0:T(8,128)S(1)} custom-call(s32[8192]{0:T(1024)S(1)} %copy-done.2, f32[3,2304,128]{2,1,0:T(8,128)S(1)} %get-tuple-element.34.streams, bf16[3,8,1024]{2,1,0:T(8,128)(2,1)S(1)} %collective-permute-done.border, f32[7,3,8,128]{3,2,1,0:T(8,128)S(1)} %get-tuple-element.37.taps), custom_call_target="tpu_custom_call" | custom-call | flops 2000000 | bytes 1048576 | tf_op jit(solution)/shard_map/featured_query/pallas_call | solution.py:273
  32.3 0.0 copy-start.3
  32.3 0.0 copy-start.4
  32.4 0.0 copy-start.8
  32.4 0.0 collective-permute-done.2
  32.4 0.0 collective-permute-done.3
  32.4 0.1 pad_maximum_fusion.refs_3_.refs_2_
  32.5 6.9 %collective-permute-start.8 = (bf16[2,1024,256]{2,1,0:T(8,128)(2,1)S(1)}, bf16[2,1024,256]{2,1,0:T(8,128)(2,1)S(1)}, u32[]{:S(2)}, u32[]{:S(2)}) collective-permute-start(bf16[2,1024,256]{2,1,0:T(8,128)(2,1)S(1)} %pad_maximum_fusion.refs_3_.refs_2_), channel_id=1, source_target_pairs={{0,192},{64,0},{128,64},{192,128},{1,193},{65,1},{129,65},{193,129... | collective-permute-start | bytes 3145736 | tf_op jit(solution)/shard_map/ppermute | solution.py:429
  39.4 0.0 collective-permute-start.7
  39.5 1.3 collective-permute-start.6
  40.8 5.7 %collective-permute-start.5 = (bf16[2,128,128]{2,1,0:T(8,128)(2,1)S(1)}, bf16[2,128,128]{2,1,0:T(8,128)(2,1)S(1)}, u32[]{:S(2)}, u32[]{:S(2)}) collective-permute-start(bf16[2,128,128]{2,1,0:T(8,128)(2,1)S(1)} %get-tuple-element.63), channel_id=1, source_target_pairs={{0,32},{8,40},{16,48},{24,56},{32,64},{40,72},{48,80},{56,88},{64,... | collective-permute-start | bytes 196616 | tf_op jit(solution)/shard_map/ppermute | solution.py:425
  46.5 3.3 %collective-permute-start.4 = (bf16[2,128,128]{2,1,0:T(8,128)(2,1)S(1)}, bf16[2,128,128]{2,1,0:T(8,128)(2,1)S(1)}, u32[]{:S(2)}, u32[]{:S(2)}) collective-permute-start(bf16[2,128,128]{2,1,0:T(8,128)(2,1)S(1)} %get-tuple-element.63), channel_id=1, source_target_pairs={{0,16},{8,24},{16,32},{24,40},{32,48},{40,56},{48,64},{56,72},{64,... | collective-permute-start | bytes 196616 | tf_op jit(solution)/shard_map/ppermute | solution.py:425
  49.7 0.0 collective-permute-done.6.six
  49.8 0.0 collective-permute-done.5.four
  49.8 1.5 collective-permute-done.4.two
  51.2 9.1 %gated_rows.1.refs_0_ = bf16[256,1024]{1,0:T(8,128)(2,1)S(1)} custom-call(s32[8192]{0:T(1024)S(1)} %copy-done.3, s32[8]{0:T(128)S(1)} %copy-done.9, f32[2,128,128]{2,1,0:T(8,128)S(1)} %get-tuple-element.64.near, bf16[2,128,128]{2,1,0:T(8,128)(2,1)S(1)} %collective-permute-done.4.two, bf16[2,128,128]{2,1,0:T(8,128)(2,1)S(1)} %collective-permute-done.5.four, ...), custom_call_target="tpu_custom_call" | custom-call | flops 12000000 | bytes 1048576 | tf_op jit(solution)/shard_map/gated_rows/pallas_call | solution.py:346
  60.4 3.7 %collective-permute-done.7.refs_5_.refs_4_ = bf16[2,1024,256]{2,1,0:T(8,128)(2,1)S(1)} collective-permute-done((bf16[2,1024,256]{2,1,0:T(8,128)(2,1)S(1)}, bf16[2,1024,256]{2,1,0:T(8,128)(2,1)S(1)}, u32[]{:S(2)}, u32[]{:S(2)}) %collective-permute-start.7) | collective-permute-done | bytes 1048608 | tf_op jit(solution)/shard_map/ppermute | solution.py:429
  64.2 2.3 %collective-permute-start.11 = (bf16[1024,256]{1,0:T(8,128)(2,1)S(1)}, bf16[1024,256]{1,0:T(8,128)(2,1)S(1)}, u32[]{:S(2)}, u32[]{:S(2)}) collective-permute-start(bf16[1024,256]{1,0:T(8,128)(2,1)S(1)} %slice_bitcast_fusion.5), channel_id=1, source_target_pairs={{0,64},{64,128},{128,192},{192,0},{1,65},{65,129},{129,193},{193,1... | collective-permute-start | bytes 1572872 | tf_op jit(solution)/shard_map/ppermute | solution.py:429
  66.5 0.5 collective-permute-start.12
  67.0 3.6 %collective-permute-start.9 = (bf16[256,1024]{1,0:T(8,128)(2,1)S(1)}, bf16[256,1024]{1,0:T(8,128)(2,1)S(1)}, u32[]{:S(2)}, u32[]{:S(2)}) collective-permute-start(bf16[256,1024]{1,0:T(8,128)(2,1)S(1)} %gated_rows.1.refs_0_), channel_id=1, source_target_pairs={{0,48},{16,0},{32,16},{48,32},{1,49},{17,1},{33,17},{49,33},{2,50}... | collective-permute-start | bytes 1572872 | tf_op jit(solution)/shard_map/ppermute | solution.py:429
  70.5 5.5 %collective-permute-done.11.refs_6_.refs_5_ = bf16[1024,256]{1,0:T(8,128)(2,1)S(1)} collective-permute-done((bf16[1024,256]{1,0:T(8,128)(2,1)S(1)}, bf16[1024,256]{1,0:T(8,128)(2,1)S(1)}, u32[]{:S(2)}, u32[]{:S(2)}) %collective-permute-start.11) | collective-permute-done | bytes 524320 | tf_op jit(solution)/shard_map/ppermute | solution.py:429
  76.1 3.8 %collective-permute-done.10.refs_2_ = bf16[256,1024]{1,0:T(8,128)(2,1)S(1)} collective-permute-done((bf16[256,1024]{1,0:T(8,128)(2,1)S(1)}, bf16[256,1024]{1,0:T(8,128)(2,1)S(1)}, u32[]{:S(2)}, u32[]{:S(2)}) %collective-permute-start.10) | collective-permute-done | bytes 524320 | tf_op jit(solution)/shard_map/ppermute | solution.py:429
  79.9 5.4 %collective-permute-done.9.refs_1_ = bf16[256,1024]{1,0:T(8,128)(2,1)S(1)} collective-permute-done((bf16[256,1024]{1,0:T(8,128)(2,1)S(1)}, bf16[256,1024]{1,0:T(8,128)(2,1)S(1)}, u32[]{:S(2)}, u32[]{:S(2)}) %collective-permute-start.9) | collective-permute-done | bytes 524320 | tf_op jit(solution)/shard_map/ppermute | solution.py:429
  85.2 3.6 %products_near.1 = bf16[2,4,384,512]{3,2,1,0:T(8,128)(2,1)S(1)} custom-call(bf16[256,1024]{1,0:T(8,128)(2,1)S(1)} %gated_rows.1.refs_0_, bf16[256,1024]{1,0:T(8,128)(2,1)S(1)} %collective-permute-done.9.refs_1_, bf16[256,1024]{1,0:T(8,128)(2,1)S(1)} %collective-permute-done.10.refs_2_, bf16[2,1024,256]{2,1,0:T(8,128)(2,1)S(1)} %pad_maximum_fusion.refs_3_.refs_2_, ...), custom_call_target="tpu_custom_call" | custom-call | flops 1000000000 | bytes 1048576 | tf_op jit(solution)/shard_map/products_near/pallas_call | solution.py:387
  88.8 0.1 slice_bitcast_fusion
  88.9 9.4 %collective-permute-start.15 = (bf16[4,384,512]{2,1,0:T(8,128)(2,1)S(1)}, bf16[4,384,512]{2,1,0:T(8,128)(2,1)S(1)}, u32[]{:S(2)}, u32[]{:S(2)}) collective-permute-start(bf16[4,384,512]{2,1,0:T(8,128)(2,1)S(1)} %slice_bitcast_fusion), channel_id=1, source_target_pairs={{0,1},{1,0},{2,3},{3,2},{4,5},{5,4},{6,7},{7,6},{8,9},{9,8},{10,11... | collective-permute-start | bytes 4718600 | tf_op jit(solution)/shard_map/ppermute | solution.py:472
  98.4 3.0 %collective-permute-done.15 = bf16[4,384,512]{2,1,0:T(8,128)(2,1)S(1)} collective-permute-done((bf16[4,384,512]{2,1,0:T(8,128)(2,1)S(1)}, bf16[4,384,512]{2,1,0:T(8,128)(2,1)S(1)}, u32[]{:S(2)}, u32[]{:S(2)}) %collective-permute-start.15) | collective-permute-done | bytes 1572896 | tf_op jit(solution)/shard_map/ppermute | solution.py:472
  101.4 0.4 fusion
  101.9 0.1 slice_bitcast_fusion.6
  101.9 2.6 %collective-permute-start.17 = (bf16[384,512]{1,0:T(8,128)(2,1)S(1)}, bf16[384,512]{1,0:T(8,128)(2,1)S(1)}, u32[]{:S(2)}, u32[]{:S(2)}) collective-permute-start(bf16[384,512]{1,0:T(8,128)(2,1)S(1)} %get-tuple-element.65), channel_id=1, source_target_pairs={{0,6},{2,0},{4,2},{6,4},{1,7},{3,1},{5,3},{7,5},{8,14},{10,8},{12,... | collective-permute-start | bytes 1179656 | tf_op jit(solution)/shard_map/ppermute | solution.py:429
  104.5 0.0 collective-permute-start.16
  104.5 0.1 collective-permute-start.14
  104.6 3.8 %collective-permute-start.13 = (bf16[128,1024]{1,0:T(8,128)(2,1)S(1)}, bf16[128,1024]{1,0:T(8,128)(2,1)S(1)}, u32[]{:S(2)}, u32[]{:S(2)}) collective-permute-start(bf16[128,1024]{1,0:T(8,128)(2,1)S(1)} %slice.82), channel_id=1, source_target_pairs={{0,48},{16,0},{32,16},{48,32},{1,49},{17,1},{33,17},{49,33},{2,50}... | collective-permute-start | bytes 786440 | tf_op jit(solution)/shard_map/ppermute | solution.py:429
  108.4 12.2 %collective-permute-done.14.refs_1_ = bf16[128,1024]{1,0:T(8,128)(2,1)S(1)} collective-permute-done((bf16[128,1024]{1,0:T(8,128)(2,1)S(1)}, bf16[128,1024]{1,0:T(8,128)(2,1)S(1)}, u32[]{:S(2)}, u32[]{:S(2)}) %collective-permute-start.14) | collective-permute-done | bytes 262176 | tf_op jit(solution)/shard_map/ppermute | solution.py:429
  120.6 1.3 products_far.1
  121.9 0.6 collective-permute-start.20
  122.5 1.8 %collective-permute-start.18 = (bf16[384,512]{1,0:T(8,128)(2,1)S(1)}, bf16[384,512]{1,0:T(8,128)(2,1)S(1)}, u32[]{:S(2)}, u32[]{:S(2)}) collective-permute-start(bf16[384,512]{1,0:T(8,128)(2,1)S(1)} %slice_bitcast_fusion.8), channel_id=1, source_target_pairs={{0,4},{2,6},{4,0},{6,2},{1,5},{3,7},{5,1},{7,3},{8,12},{10,14},{12... | collective-permute-start | bytes 1179656 | tf_op jit(solution)/shard_map/ppermute | solution.py:429
  124.4 0.1 fusion.1
  124.5 1.6 collective-permute-start.21
  126.1 1.2 collective-permute-start.23
  127.3 0.9 collective-permute-start.22
  128.2 6.7 %collective-permute-done.18 = bf16[384,512]{1,0:T(8,128)(2,1)S(1)} collective-permute-done((bf16[384,512]{1,0:T(8,128)(2,1)S(1)}, bf16[384,512]{1,0:T(8,128)(2,1)S(1)}, u32[]{:S(2)}, u32[]{:S(2)}) %collective-permute-start.18) | collective-permute-done | bytes 393248 | tf_op jit(solution)/shard_map/ppermute | solution.py:429
  134.9 0.2 fusion.4
  135.2 1.3 collective-permute-start.19
  136.5 3.7 %collective-permute-start.26 = (bf16[256,512]{1,0:T(8,128)(2,1)S(1)}, bf16[256,512]{1,0:T(8,128)(2,1)S(1)}, u32[]{:S(2)}, u32[]{:S(2)}) collective-permute-start(bf16[256,512]{1,0:T(8,128)(2,1)S(1)} %slice.111), channel_id=1, source_target_pairs={{0,16},{1,48},{16,32},{17,0},{32,49},{33,17},{48,1},{49,33},{2,18}... | collective-permute-start | bytes 786440 | tf_op jit(solution)/shard_map/ppermute | solution.py:480
  140.1 0.4 collective-permute-done.22
  140.5 0.1 fusion.7
  140.6 5.9 %collective-permute-start.25 = (bf16[128,512]{1,0:T(8,128)(2,1)S(1)}, bf16[128,512]{1,0:T(8,128)(2,1)S(1)}, u32[]{:S(2)}, u32[]{:S(2)}) collective-permute-start(bf16[128,512]{1,0:T(8,128)(2,1)S(1)} %fusion.7), channel_id=1, source_target_pairs={{1,32},{17,48},{33,1},{49,17},{3,34},{19,50},{35,3},{51,19},{5,36}... | collective-permute-start | bytes 393224 | tf_op jit(solution)/shard_map/ppermute | solution.py:480
  146.5 1.3 collective-permute-start.24
  147.8 2.9 %collective-permute-done.25.far_bottom = bf16[128,512]{1,0:T(8,128)(2,1)S(1)} collective-permute-done((bf16[128,512]{1,0:T(8,128)(2,1)S(1)}, bf16[128,512]{1,0:T(8,128)(2,1)S(1)}, u32[]{:S(2)}, u32[]{:S(2)}) %collective-permute-start.25) | collective-permute-done | bytes 131104 | tf_op jit(solution)/shard_map/ppermute | solution.py:480
  150.7 8.0 %collective-permute-done.24.far_top = bf16[128,512]{1,0:T(8,128)(2,1)S(1)} collective-permute-done((bf16[128,512]{1,0:T(8,128)(2,1)S(1)}, bf16[128,512]{1,0:T(8,128)(2,1)S(1)}, u32[]{:S(2)}, u32[]{:S(2)}) %collective-permute-start.24) | collective-permute-done | bytes 131104 | tf_op jit(solution)/shard_map/ppermute | solution.py:480
  158.7 0.8 assemble.1
  (38 shorter events, 0.3 us)
Async XLA Ops:
  0.0 13.7 %copy-start = (f32[8,2,16,1024]{3,2,1,0:T(8,128)S(1)}, f32[8,2,16,1024]{3,2,1,0:T(8,128)}, u32[]{:S(2)}) copy-start(f32[8,2,16,1024]{3,2,1,0:T(8,128)} %entry.3) | copy-start | bytes 3145732
  0.0 1.5 copy-start.1
  1.5 0.8 copy-start.2
  2.3 0.8 copy-start.5
  3.1 0.8 copy-start.6
  3.9 0.7 copy-start.7
  4.6 7.3 %copy-start.10 = (bf16[1024,256]{1,0:T(8,128)(2,1)S(1)}, bf16[1024,256]{1,0:T(8,128)(2,1)}, u32[]{:S(2)}) copy-start(bf16[1024,256]{1,0:T(8,128)(2,1)} %param.19) | copy-start | bytes 1572868
  4.6 9.1 %copy-start.9 = (s32[8]{0:T(128)S(1)}, s32[8]{0:T(128)}, u32[]{:S(2)}) copy-start(s32[8]{0:T(128)} %picks.3) | copy-start | bytes 100
  6.4 5.5 %collective-permute-start = (bf16[3,8,1024]{2,1,0:T(8,128)(2,1)S(1)}, bf16[3,8,1024]{2,1,0:T(8,128)(2,1)S(1)}, u32[]{:S(2)}, u32[]{:S(2)}) collective-permute-start(bf16[3,8,1024]{2,1,0:T(8,128)(2,1)S(1)} %get-tuple-element.35), channel_id=1, source_target_pairs={{0,8},{8,16},{16,24},{24,32},{32,40},{40,48},{48,56},{56,64},{64,7... | collective-permute-start | bytes 147464 | tf_op jit(solution)/shard_map/ppermute | solution.py:425
  11.9 20.5 %collective-permute-start.3 = (bf16[1024,256]{1,0:T(8,128)(2,1)S(1)}, bf16[1024,256]{1,0:T(8,128)(2,1)S(1)}, u32[]{:S(2)}, u32[]{:S(2)}) collective-permute-start(bf16[1024,256]{1,0:T(8,128)(2,1)S(1)} %copy-done.10), channel_id=1, source_target_pairs={{0,8},{8,0},{1,9},{9,1},{2,10},{10,2},{3,11},{11,3},{4,12},{12,4},... | collective-permute-start | bytes 1572872 | tf_op jit(solution)/shard_map/ppermute | solution.py:446
  22.4 10.0 %collective-permute-start.2 = (bf16[2,128,128]{2,1,0:T(8,128)(2,1)S(1)}, bf16[2,128,128]{2,1,0:T(8,128)(2,1)S(1)}, u32[]{:S(2)}, u32[]{:S(2)}) collective-permute-start(bf16[2,128,128]{2,1,0:T(8,128)(2,1)S(1)} %get-tuple-element.39), channel_id=1, source_target_pairs={{0,16},{8,24},{16,32},{24,40},{32,48},{40,56},{48,64},{56,72},{64,... | collective-permute-start | bytes 196616 | tf_op jit(solution)/shard_map/ppermute | solution.py:425
  28.4 4.0 %collective-permute-start.1 = (bf16[2,128,128]{2,1,0:T(8,128)(2,1)S(1)}, bf16[2,128,128]{2,1,0:T(8,128)(2,1)S(1)}, u32[]{:S(2)}, u32[]{:S(2)}) collective-permute-start(bf16[2,128,128]{2,1,0:T(8,128)(2,1)S(1)} %get-tuple-element.39), channel_id=1, source_target_pairs={{0,8},{8,16},{16,24},{24,32},{32,40},{40,48},{48,56},{56,64},{64,7... | collective-permute-start | bytes 196616 | tf_op jit(solution)/shard_map/ppermute | solution.py:425
  32.3 18.9 %copy-start.3 = (s32[8192]{0:T(1024)S(1)}, s32[8192]{0:T(1024)}, u32[]{:S(2)}) copy-start(s32[8192]{0:T(1024)} %ids.7) | copy-start | bytes 98308
  32.3 18.9 %copy-start.4 = (f32[2,16,1024]{2,1,0:T(8,128)S(1)}, f32[2,16,1024]{2,1,0:T(8,128)}, u32[]{:S(2)}) copy-start(f32[2,16,1024]{2,1,0:T(8,128)} %res.1) | copy-start | bytes 393220
  32.4 18.9 %copy-start.8 = (f32[1024]{0:T(1024)S(1)}, f32[1024]{0:T(1024)}, u32[]{:S(2)}) copy-start(f32[1024]{0:T(1024)} %param.15) | copy-start | bytes 12292
  32.5 27.9 %collective-permute-start.8 = (bf16[2,1024,256]{2,1,0:T(8,128)(2,1)S(1)}, bf16[2,1024,256]{2,1,0:T(8,128)(2,1)S(1)}, u32[]{:S(2)}, u32[]{:S(2)}) collective-permute-start(bf16[2,1024,256]{2,1,0:T(8,128)(2,1)S(1)} %pad_maximum_fusion.refs_3_.refs_2_), channel_id=1, source_target_pairs={{0,192},{64,0},{128,64},{192,128},{1,193},{65,1},{129,65},{193,129... | collective-permute-start | bytes 3145736 | tf_op jit(solution)/shard_map/ppermute | solution.py:429
  39.4 24.7 %collective-permute-start.7 = (bf16[2,1024,256]{2,1,0:T(8,128)(2,1)S(1)}, bf16[2,1024,256]{2,1,0:T(8,128)(2,1)S(1)}, u32[]{:S(2)}, u32[]{:S(2)}) collective-permute-start(bf16[2,1024,256]{2,1,0:T(8,128)(2,1)S(1)} %pad_maximum_fusion.refs_3_.refs_2_), channel_id=1, source_target_pairs={{0,64},{64,128},{128,192},{192,0},{1,65},{65,129},{129,193},{193,1... | collective-permute-start | bytes 3145736 | tf_op jit(solution)/shard_map/ppermute | solution.py:429
  39.5 10.3 %collective-permute-start.6 = (bf16[2,128,128]{2,1,0:T(8,128)(2,1)S(1)}, bf16[2,128,128]{2,1,0:T(8,128)(2,1)S(1)}, u32[]{:S(2)}, u32[]{:S(2)}) collective-permute-start(bf16[2,128,128]{2,1,0:T(8,128)(2,1)S(1)} %get-tuple-element.63), channel_id=1, source_target_pairs={{0,48},{8,56},{16,64},{24,72},{32,80},{40,88},{48,96},{56,104},{64... | collective-permute-start | bytes 196616 | tf_op jit(solution)/shard_map/ppermute | solution.py:425
  40.8 9.0 %collective-permute-start.5 = (bf16[2,128,128]{2,1,0:T(8,128)(2,1)S(1)}, bf16[2,128,128]{2,1,0:T(8,128)(2,1)S(1)}, u32[]{:S(2)}, u32[]{:S(2)}) collective-permute-start(bf16[2,128,128]{2,1,0:T(8,128)(2,1)S(1)} %get-tuple-element.63), channel_id=1, source_target_pairs={{0,32},{8,40},{16,48},{24,56},{32,64},{40,72},{48,80},{56,88},{64,... | collective-permute-start | bytes 196616 | tf_op jit(solution)/shard_map/ppermute | solution.py:425
  46.5 4.8 %collective-permute-start.4 = (bf16[2,128,128]{2,1,0:T(8,128)(2,1)S(1)}, bf16[2,128,128]{2,1,0:T(8,128)(2,1)S(1)}, u32[]{:S(2)}, u32[]{:S(2)}) collective-permute-start(bf16[2,128,128]{2,1,0:T(8,128)(2,1)S(1)} %get-tuple-element.63), channel_id=1, source_target_pairs={{0,16},{8,24},{16,32},{24,40},{32,48},{40,56},{48,64},{56,72},{64,... | collective-permute-start | bytes 196616 | tf_op jit(solution)/shard_map/ppermute | solution.py:425
  64.2 11.8 %collective-permute-start.11 = (bf16[1024,256]{1,0:T(8,128)(2,1)S(1)}, bf16[1024,256]{1,0:T(8,128)(2,1)S(1)}, u32[]{:S(2)}, u32[]{:S(2)}) collective-permute-start(bf16[1024,256]{1,0:T(8,128)(2,1)S(1)} %slice_bitcast_fusion.5), channel_id=1, source_target_pairs={{0,64},{64,128},{128,192},{192,0},{1,65},{65,129},{129,193},{193,1... | collective-permute-start | bytes 1572872 | tf_op jit(solution)/shard_map/ppermute | solution.py:429
  66.5 9.6 %collective-permute-start.12 = (bf16[1024,256]{1,0:T(8,128)(2,1)S(1)}, bf16[1024,256]{1,0:T(8,128)(2,1)S(1)}, u32[]{:S(2)}, u32[]{:S(2)}) collective-permute-start(bf16[1024,256]{1,0:T(8,128)(2,1)S(1)} %slice_bitcast_fusion.4), channel_id=1, source_target_pairs={{0,192},{64,0},{128,64},{192,128},{1,193},{65,1},{129,65},{193,129... | collective-permute-start | bytes 1572872 | tf_op jit(solution)/shard_map/ppermute | solution.py:429
  67.0 12.9 %collective-permute-start.10 = (bf16[256,1024]{1,0:T(8,128)(2,1)S(1)}, bf16[256,1024]{1,0:T(8,128)(2,1)S(1)}, u32[]{:S(2)}, u32[]{:S(2)}) collective-permute-start(bf16[256,1024]{1,0:T(8,128)(2,1)S(1)} %gated_rows.1.refs_0_), channel_id=1, source_target_pairs={{0,16},{16,32},{32,48},{48,0},{1,17},{17,33},{33,49},{49,1},{2,18}... | collective-permute-start | bytes 1572872 | tf_op jit(solution)/shard_map/ppermute | solution.py:429
  67.0 18.3 %collective-permute-start.9 = (bf16[256,1024]{1,0:T(8,128)(2,1)S(1)}, bf16[256,1024]{1,0:T(8,128)(2,1)S(1)}, u32[]{:S(2)}, u32[]{:S(2)}) collective-permute-start(bf16[256,1024]{1,0:T(8,128)(2,1)S(1)} %gated_rows.1.refs_0_), channel_id=1, source_target_pairs={{0,48},{16,0},{32,16},{48,32},{1,49},{17,1},{33,17},{49,33},{2,50}... | collective-permute-start | bytes 1572872 | tf_op jit(solution)/shard_map/ppermute | solution.py:429
  88.9 12.4 %collective-permute-start.15 = (bf16[4,384,512]{2,1,0:T(8,128)(2,1)S(1)}, bf16[4,384,512]{2,1,0:T(8,128)(2,1)S(1)}, u32[]{:S(2)}, u32[]{:S(2)}) collective-permute-start(bf16[4,384,512]{2,1,0:T(8,128)(2,1)S(1)} %slice_bitcast_fusion), channel_id=1, source_target_pairs={{0,1},{1,0},{2,3},{3,2},{4,5},{5,4},{6,7},{7,6},{8,9},{9,8},{10,11... | collective-permute-start | bytes 4718600 | tf_op jit(solution)/shard_map/ppermute | solution.py:472
  101.9 18.7 %collective-permute-start.17 = (bf16[384,512]{1,0:T(8,128)(2,1)S(1)}, bf16[384,512]{1,0:T(8,128)(2,1)S(1)}, u32[]{:S(2)}, u32[]{:S(2)}) collective-permute-start(bf16[384,512]{1,0:T(8,128)(2,1)S(1)} %get-tuple-element.65), channel_id=1, source_target_pairs={{0,6},{2,0},{4,2},{6,4},{1,7},{3,1},{5,3},{7,5},{8,14},{10,8},{12,... | collective-permute-start | bytes 1179656 | tf_op jit(solution)/shard_map/ppermute | solution.py:429
  104.5 16.2 %collective-permute-start.16 = (bf16[384,512]{1,0:T(8,128)(2,1)S(1)}, bf16[384,512]{1,0:T(8,128)(2,1)S(1)}, u32[]{:S(2)}, u32[]{:S(2)}) collective-permute-start(bf16[384,512]{1,0:T(8,128)(2,1)S(1)} %get-tuple-element.66), channel_id=1, source_target_pairs={{0,2},{2,4},{4,6},{6,0},{1,3},{3,5},{5,7},{7,1},{8,10},{10,12},{12... | collective-permute-start | bytes 1179656 | tf_op jit(solution)/shard_map/ppermute | solution.py:429
  104.5 16.1 %collective-permute-start.14 = (bf16[128,1024]{1,0:T(8,128)(2,1)S(1)}, bf16[128,1024]{1,0:T(8,128)(2,1)S(1)}, u32[]{:S(2)}, u32[]{:S(2)}) collective-permute-start(bf16[128,1024]{1,0:T(8,128)(2,1)S(1)} %slice.83), channel_id=1, source_target_pairs={{0,16},{16,32},{32,48},{48,0},{1,17},{17,33},{33,49},{49,1},{2,18}... | collective-permute-start | bytes 786440 | tf_op jit(solution)/shard_map/ppermute | solution.py:429
  104.6 16.0 %collective-permute-start.13 = (bf16[128,1024]{1,0:T(8,128)(2,1)S(1)}, bf16[128,1024]{1,0:T(8,128)(2,1)S(1)}, u32[]{:S(2)}, u32[]{:S(2)}) collective-permute-start(bf16[128,1024]{1,0:T(8,128)(2,1)S(1)} %slice.82), channel_id=1, source_target_pairs={{0,48},{16,0},{32,16},{48,32},{1,49},{17,1},{33,17},{49,33},{2,50}... | collective-permute-start | bytes 786440 | tf_op jit(solution)/shard_map/ppermute | solution.py:429
  121.9 2.4 %collective-permute-start.20 = (bf16[4,128,512]{2,1,0:T(8,128)(2,1)S(1)}, bf16[4,128,512]{2,1,0:T(8,128)(2,1)S(1)}, u32[]{:S(2)}, u32[]{:S(2)}) collective-permute-start(bf16[4,128,512]{2,1,0:T(8,128)(2,1)S(1)} %slice_bitcast_fusion.2), channel_id=1, source_target_pairs={{0,1},{1,0},{2,3},{3,2},{4,5},{5,4},{6,7},{7,6},{8,9},{9,8},{10,11... | collective-permute-start | bytes 1572872 | tf_op jit(solution)/shard_map/ppermute | solution.py:472
  122.5 12.4 %collective-permute-start.18 = (bf16[384,512]{1,0:T(8,128)(2,1)S(1)}, bf16[384,512]{1,0:T(8,128)(2,1)S(1)}, u32[]{:S(2)}, u32[]{:S(2)}) collective-permute-start(bf16[384,512]{1,0:T(8,128)(2,1)S(1)} %slice_bitcast_fusion.8), channel_id=1, source_target_pairs={{0,4},{2,6},{4,0},{6,2},{1,5},{3,7},{5,1},{7,3},{8,12},{10,14},{12... | collective-permute-start | bytes 1179656 | tf_op jit(solution)/shard_map/ppermute | solution.py:429
  124.5 15.6 %collective-permute-start.21 = (bf16[128,512]{1,0:T(8,128)(2,1)S(1)}, bf16[128,512]{1,0:T(8,128)(2,1)S(1)}, u32[]{:S(2)}, u32[]{:S(2)}) collective-permute-start(bf16[128,512]{1,0:T(8,128)(2,1)S(1)} %get-tuple-element.69), channel_id=1, source_target_pairs={{0,2},{2,4},{4,6},{6,0},{1,3},{3,5},{5,7},{7,1},{8,10},{10,12},{12... | collective-permute-start | bytes 393224 | tf_op jit(solution)/shard_map/ppermute | solution.py:429
  126.1 14.0 %collective-permute-start.23 = (bf16[128,512]{1,0:T(8,128)(2,1)S(1)}, bf16[128,512]{1,0:T(8,128)(2,1)S(1)}, u32[]{:S(2)}, u32[]{:S(2)}) collective-permute-start(bf16[128,512]{1,0:T(8,128)(2,1)S(1)} %get-tuple-element.70), channel_id=1, source_target_pairs={{0,6},{2,0},{4,2},{6,4},{1,7},{3,1},{5,3},{7,5},{8,14},{10,8},{12,... | collective-permute-start | bytes 393224 | tf_op jit(solution)/shard_map/ppermute | solution.py:429
  127.3 13.2 %collective-permute-start.22 = (bf16[128,512]{1,0:T(8,128)(2,1)S(1)}, bf16[128,512]{1,0:T(8,128)(2,1)S(1)}, u32[]{:S(2)}, u32[]{:S(2)}) collective-permute-start(bf16[128,512]{1,0:T(8,128)(2,1)S(1)} %get-tuple-element.71), channel_id=1, source_target_pairs={{0,4},{2,6},{4,0},{6,2},{1,5},{3,7},{5,1},{7,3},{8,12},{10,14},{12... | collective-permute-start | bytes 393224 | tf_op jit(solution)/shard_map/ppermute | solution.py:429
  135.2 12.7 %collective-permute-start.19 = (bf16[128,512]{1,0:T(8,128)(2,1)S(1)}, bf16[128,512]{1,0:T(8,128)(2,1)S(1)}, u32[]{:S(2)}, u32[]{:S(2)}) collective-permute-start(bf16[128,512]{1,0:T(8,128)(2,1)S(1)} %slice.104.near_own), channel_id=1, source_target_pairs={{0,1},{1,0},{2,3},{3,2},{4,5},{5,4},{6,7},{7,6},{8,9},{9,8},{10,11... | collective-permute-start | bytes 393224 | tf_op jit(solution)/shard_map/ppermute | solution.py:496
  136.5 11.4 %collective-permute-start.26 = (bf16[256,512]{1,0:T(8,128)(2,1)S(1)}, bf16[256,512]{1,0:T(8,128)(2,1)S(1)}, u32[]{:S(2)}, u32[]{:S(2)}) collective-permute-start(bf16[256,512]{1,0:T(8,128)(2,1)S(1)} %slice.111), channel_id=1, source_target_pairs={{0,16},{1,48},{16,32},{17,0},{32,49},{33,17},{48,1},{49,33},{2,18}... | collective-permute-start | bytes 786440 | tf_op jit(solution)/shard_map/ppermute | solution.py:480
  140.6 10.1 %collective-permute-start.25 = (bf16[128,512]{1,0:T(8,128)(2,1)S(1)}, bf16[128,512]{1,0:T(8,128)(2,1)S(1)}, u32[]{:S(2)}, u32[]{:S(2)}) collective-permute-start(bf16[128,512]{1,0:T(8,128)(2,1)S(1)} %fusion.7), channel_id=1, source_target_pairs={{1,32},{17,48},{33,1},{49,17},{3,34},{19,50},{35,3},{51,19},{5,36}... | collective-permute-start | bytes 393224 | tf_op jit(solution)/shard_map/ppermute | solution.py:480
  146.5 12.2 %collective-permute-start.24 = (bf16[128,512]{1,0:T(8,128)(2,1)S(1)}, bf16[128,512]{1,0:T(8,128)(2,1)S(1)}, u32[]{:S(2)}, u32[]{:S(2)}) collective-permute-start(bf16[128,512]{1,0:T(8,128)(2,1)S(1)} %fusion.7), channel_id=1, source_target_pairs={{0,32},{16,48},{32,1},{48,17},{2,34},{18,50},{34,3},{50,19},{4,36}... | collective-permute-start | bytes 393224 | tf_op jit(solution)/shard_map/ppermute | solution.py:480

commit v3 on v2

--- a/solution.py
+++ b/solution.py
@@ -56,9 +56,8 @@
     return jnp.where(position < 0, -1, ids[jnp.maximum(position, 0)])
 
 
-def prepare_kernel(ids, feat, filt, decay, angle, pole_out, power_out, taps_out, streams_out, edge_out, small):
+def prepare_kernel(ids, filt, decay, angle, pole_out, power_out, taps_out, small):
     position = first_position()
-    edge_out[...] = feat[:, ROWS - 8 :, :]
     for half in range(2):
         rows = slice(8 * half, 8 * half + 8)
         mag = jnp.exp(-decay[rows, :])
@@ -66,23 +65,28 @@
         spread(small, 0, mag * jnp.cos(ang))
         spread(small, BLOCK, mag * jnp.sin(ang))
         for r in range(8):
-            pole_out[0, 8 * half + r] = row(small, 0, r)
-            pole_out[1, 8 * half + r] = row(small, BLOCK, r)
-    last = record_of(ids, position - 1)
+            pole_out[0, 0, 8 * half + r] = row(small, 0, r)
+            pole_out[0, 1, 8 * half + r] = row(small, BLOCK, r)
     keeps = []
-    for count in (1, 2, 4, 6):
-        before = position - count * ROWS - 1
-        keeps.append(jnp.where((before >= 0) & (record_of(ids, before) == last), 1.0, 0.0))
+    for count, last in ((1, position + ROWS - 1), (2, position + ROWS - 1), (3, position + ROWS - 1), (4, position - 1)):
+        before = last - count * ROWS
+        keeps.append(jnp.where((before >= 0) & (record_of(ids, before) == record_of(ids, last)), 1.0, 0.0))
     for m in range(MODES):
-        re, im = pole_out[0, m], pole_out[1, m]
-        for doubling in range(8):
+        re, im = pole_out[0, 0, m], pole_out[0, 1, m]
+        two_re, two_im = re * re - im * im, 2.0 * re * im
+        pole_out[1, 0, m], pole_out[1, 1, m] = two_re, two_im
+        pole_out[2, 0, m], pole_out[2, 1, m] = re * two_re - im * two_im, re * two_im + im * two_re
+        re, im = two_re * two_re - two_im * two_im, 2.0 * two_re * two_im
+        pole_out[3, 0, m], pole_out[3, 1, m] = re, im
+        for doubling in range(6):
             re, im = re * re - im * im, 2.0 * re * im
-        powers = [(re, im)]
-        for doubling in range(2):
-            re, im = re * re - im * im, 2.0 * re * im
-            powers.append((re, im))
-        two = powers[1]
-        powers.append((re * two[0] - im * two[1], re * two[1] + im * two[0]))
+        two_re, two_im = re * re - im * im, 2.0 * re * im
+        powers = (
+            (re, im),
+            (two_re, two_im),
+            (re * two_re - im * two_im, re * two_im + im * two_re),
+            (two_re * two_re - two_im * two_im, 2.0 * two_re * two_im),
+        )
         for n in range(4):
             power_out[n, 0, m] = powers[n][0] * keeps[n]
             power_out[n, 1, m] = powers[n][1] * keeps[n]
@@ -95,38 +99,35 @@
         for j in range(TAPS):
             taps_out[j, i] = row(small, 0, j)
 
-    def lay_out(b, carry):
-        for i in range(3):
-            value = feat[i, pl.ds(pl.multiple_of(b * 16, 16), 16), :].astype(F32)
-            spread(streams_out.at[i], 2 * b * BLOCK, value[:8])
-            spread(streams_out.at[i], (2 * b + 1) * BLOCK, value[8:])
-        return carry
-
-    lax.fori_loop(0, ROWS // 16, lay_out, 0)
-
-
-def prepare(ids, feat, filt, decay, angle):
+
+def prepare(ids, filt, decay, angle):
     return call(
         prepare_kernel,
         (
-            jax.ShapeDtypeStruct((2, MODES) + WIDE, F32),
+            jax.ShapeDtypeStruct((4, 2, MODES) + WIDE, F32),
             jax.ShapeDtypeStruct((4, 2, MODES) + WIDE, F32),
             jax.ShapeDtypeStruct((TAPS, 3) + WIDE, F32),
-            jax.ShapeDtypeStruct((3, ROWS // 8 * BLOCK, LANES), F32),
-            jax.ShapeDtypeStruct((3, 8, CH), BF16),
         ),
-        [SMEM_SPEC] + [VMEM_SPEC] * 4,
+        [SMEM_SPEC] + [VMEM_SPEC] * 3,
         [pltpu.VMEM((2 * BLOCK, LANES), F32)],
-        16,
+        58,
         "prepare",
         3_000_000,
-    )(ids, feat, filt, decay, angle)
-
-
-def featurized(i, b, before, stream, taps_ref, same):
-    values = [row(before[0], before[1], 2 + r) for r in range(6)]
-    values += [row(stream, b * BLOCK, r) for r in range(8)]
-    taps = [taps_ref[j, i] for j in range(TAPS)]
+    )(ids, filt, decay, angle)
+
+
+def lay_out(feat, which, streams):
+    def step(b, carry):
+        for n, i in enumerate(which):
+            value = feat[i, pl.ds(pl.multiple_of(b * 16, 16), 16), :].astype(F32)
+            spread(streams.at[n], 2 * b * BLOCK, value[:8])
+            spread(streams.at[n], (2 * b + 1) * BLOCK, value[8:])
+        return carry
+
+    lax.fori_loop(0, ROWS // 16, step, 0)
+
+
+def featurized(values, taps, same):
     outs = []
     for t in range(8):
         out = taps[0] * values[6 + t]
@@ -140,12 +141,19 @@
 
 
 def featurize(position, ids, which, streams, edge, taps, emit):
-    def block(b, before):
+    def step(b, before):
         first = position + 8 * b
         plain = record_of(ids, first - 6) == ids[first + 7]
+        rows = [[row(streams.at[n], b * BLOCK, r) for r in range(8)] for n in range(len(which))]
 
         def run(same):
-            emit(b, [featurized(i, b, before(i), streams.at[i], taps, same) for i in which])
+            emit(
+                b,
+                [
+                    featurized([*before[n], *rows[n]], [taps[j, i] for j in range(TAPS)], same)
+                    for n, i in enumerate(which)
+                ],
+            )
 
         @pl.when(plain)
         def _():
@@ -155,16 +163,12 @@
         def _():
             run([[record_of(ids, first + t - j) == ids[first + t] for j in range(TAPS)] for t in range(8)])
 
-    block(0, lambda i: (edge, i * BLOCK))
-
-    def step(b, carry):
-        block(b, lambda i: (streams.at[i], (b - 1) * BLOCK))
-        return carry
-
-    lax.fori_loop(1, ROWS // 8, step, 0)
-
-
-def run_modes(position, ids, picks, entry, states, small, product, group, step, emit, carry_in=None):
+        return tuple(tuple(eight[2:]) for eight in rows)
+
+    lax.fori_loop(0, ROWS // 8, step, tuple(tuple(row(edge, i * BLOCK, 2 + r) for r in range(6)) for i in which))
+
+
+def run_modes(position, ids, picks, entry, states, small, product, group, step, emit, carry_in=None, block_step=None):
     for part in range(2):
         for m in range(8):
             states[part, m] = jnp.zeros(WIDE, F32) if carry_in is None else carry_in[part, 8 * group + m]
@@ -177,9 +181,12 @@
         def _():
             re = [states[0, m] for m in range(8)]
             im = [states[1, m] for m in range(8)]
-            for t in range(8):
-                value = product[8 * b + t]
-                emit(8 * b + t, value, step(value, re, im))
+            if block_step is None:
+                for t in range(8):
+                    value = product[8 * b + t]
+                    emit(8 * b + t, value, step(value, re, im))
+            else:
+                block_step([product[8 * b + t] for t in range(8)], re, im)
             for m in range(8):
                 states[0, m] = re[m]
                 states[1, m] = im[m]
@@ -213,8 +220,9 @@
     lax.fori_loop(0, ROWS // 8, block, 0)
 
 
-def final_kernel(ids, picks, streams, border, taps, pole, entry, final_out, product_out, edge, states, small):
+def final_kernel(ids, picks, feat, border, taps, pole, entry, final_out, product_out, streams, edge, states, small):
     position = first_position()
+    lay_out(feat, (1, 2), streams)
     for i in (1, 2):
         spread(edge, i * BLOCK, border[i].astype(F32))
 
@@ -227,11 +235,25 @@
 
         def step(value, re, im, group=group):
             for m in range(8):
-                pr, pi = pole[0, 8 * group + m], pole[1, 8 * group + m]
+                pr, pi = pole[0, 0, 8 * group + m], pole[0, 1, 8 * group + m]
                 re[m], im[m] = pr * re[m] - pi * im[m] + value, pr * im[m] + pi * re[m]
 
+        def block_step(values, re, im, group=group):
+            for m in range(8):
+                power_re = [pole[n, 0, 8 * group + m] for n in range(4)]
+                power_im = [pole[n, 1, 8 * group + m] for n in range(4)]
+                for at in (0, 4):
+                    first, second, third, fourth = values[at : at + 4]
+                    new_re = power_re[2] * first + power_re[1] * second + power_re[0] * third + fourth
+                    new_im = power_im[2] * first + power_im[1] * second + power_im[0] * third
+                    re[m], im[m] = (
+                        power_re[3] * re[m] - power_im[3] * im[m] + new_re,
+                        power_re[3] * im[m] + power_im[3] * re[m] + new_im,
+                    )
+
         run_modes(
-            position, ids, picks, entry, states, small, product_out, group, step, lambda at, value, out: None
+            position, ids, picks, entry, states, small, product_out, group, step, lambda at, value, out: None,
+            block_step=block_step,
         )
         for part in range(2):
             for m in range(0, 8, 2):
@@ -240,7 +262,7 @@
                 final_out[part, at : at + 16, :] = pair.astype(BF16)
 
 
-def final_states(ids, picks, streams, border, taps, pole, entry):
+def final_states(ids, picks, feat, border, taps, pole, entry):
     return call(
         final_kernel,
         (
@@ -249,17 +271,19 @@
         ),
         [SMEM_SPEC] * 2 + [VMEM_SPEC] * 5,
         [
+            pltpu.VMEM((2, ROWS // 8 * BLOCK, LANES), F32),
             pltpu.VMEM((3 * BLOCK, LANES), F32),
             pltpu.VMEM((2, 8) + WIDE, F32),
             pltpu.VMEM((BLOCK, LANES), F32),
         ],
-        16,
+        58,
         "final_states",
         8_000_000,
-    )(ids, picks, streams, border, taps, pole, entry)
-
-
-def query_kernel(ids, streams, border, taps, query_out, edge):
+    )(ids, picks, feat, border, taps, pole, entry)
+
+
+def query_kernel(ids, feat, border, taps, query_out, streams, edge):
+    lay_out(feat, (0,), streams)
     spread(edge, 0, border[0].astype(F32))
 
     def emit(b, outs):
@@ -269,16 +293,16 @@
     featurize(first_position(), ids, (0,), streams, edge, taps, emit)
 
 
-def featured_query(ids, streams, border, taps):
+def featured_query(ids, feat, border, taps):
     return call(
         query_kernel,
         jax.ShapeDtypeStruct((ROWS,) + WIDE, F32),
         [SMEM_SPEC] + [VMEM_SPEC] * 3,
-        [pltpu.VMEM((BLOCK, LANES), F32)],
+        [pltpu.VMEM((1, ROWS // 8 * BLOCK, LANES), F32), pltpu.VMEM((BLOCK, LANES), F32)],
         16,
         "featured_query",
         2_000_000,
-    )(ids, streams, border, taps)
+    )(ids, feat, border, taps)
 
 
 def residue_tables(res, tables, small, halves):
@@ -290,17 +314,15 @@
 
 
 def modal_kernel(
-    ids, picks, near, two, four, six, power, pole, res, skip, entry, product, query,
+    ids, picks, near, far, power, pole, res, skip, entry, product, query,
     gated_out, tables, carry_in, states, base, stage, small,
 ):
     for pair in range(MODES // 2):
         rows = slice(16 * pair, 16 * pair + 16)
-        re, im = near[0, rows, :], near[1, rows, :]
-        for n, ref in ((1, two), (2, four), (3, six)):
-            other_re, other_im = ref[0, rows, :].astype(F32), ref[1, rows, :].astype(F32)
-            power_re, power_im = power[n, 0, rows, :], power[n, 1, rows, :]
-            re = re + power_re * other_re - power_im * other_im
-            im = im + power_re * other_im + power_im * other_re
+        far_re, far_im = far[0, rows, :].astype(F32), far[1, rows, :].astype(F32)
+        power_re, power_im = power[3, 0, rows, :], power[3, 1, rows, :]
+        re = near[0, rows, :].astype(F32) + power_re * far_re - power_im * far_im
+        im = near[1, rows, :].astype(F32) + power_re * far_im + power_im * far_re
         for part, value in enumerate((re, im)):
             carry_in[part, 2 * pair] = value[:8]
             carry_in[part, 2 * pair + 1] = value[8:]
@@ -314,7 +336,7 @@
             out = None
             for m in range(8):
                 mode = 8 * group + m
-                pr, pi = pole[0, mode], pole[1, mode]
+                pr, pi = pole[0, 0, mode], pole[0, 1, mode]
                 new_re = pr * re[m] - pi * im[m] + value
                 new_im = pr * im[m] + pi * re[m]
                 re[m], im[m] = new_re, new_im
@@ -342,11 +364,11 @@
     lax.fori_loop(0, ROWS // 16, gather, 0)
 
 
-def gated_rows(ids, picks, near, two, four, six, power, pole, res, skip, entry, product, query):
+def gated_rows(ids, picks, near, far, power, pole, res, skip, entry, product, query):
     return call(
         modal_kernel,
         jax.ShapeDtypeStruct((ROWS, CH), BF16),
-        [SMEM_SPEC] * 2 + [VMEM_SPEC] * 11,
+        [SMEM_SPEC] * 2 + [VMEM_SPEC] * 9,
         [
             pltpu.VMEM((2, MODES) + WIDE, F32),
             pltpu.VMEM((2, MODES) + WIDE, F32),
@@ -358,7 +380,7 @@
         20,
         "gated_rows",
         12_000_000,
-    )(ids, picks, near, two, four, six, power, pole, res, skip, entry, product, query)
+    )(ids, picks, near, far, power, pole, res, skip, entry, product, query)
 
 
 def partial_products(blocks, places, weights, name):
@@ -437,29 +459,29 @@
     features, short_filter, decay, angle_rate, residues, skip, entry_states, segment_ids, state_ids, out_weight
 ):
     skip_row = skip.reshape(1, CH)
-    pole, power, taps, streams, edge = prepare(
-        segment_ids, features, short_filter.transpose(1, 0, 2), decay, angle_rate
-    )
+    border = shift_records(features[:, ROWS - 8 :, :], 1)
+    pole, power, taps = prepare(segment_ids, short_filter.transpose(1, 0, 2), decay, angle_rate)
     power = power.reshape(4, 2, MODES * 8, LANES)
-    border = shift_records(edge, 1)
-    border, out_weight = tie(border, out_weight)
+    border, out_weight, pole = tie(border, out_weight, pole)
     paired = lax.ppermute(out_weight, "zl", [(0, 1), (1, 0)])
-    final, product = final_states(segment_ids, state_ids, streams, border, taps, pole, entry_states)
+    final, product = final_states(segment_ids, state_ids, features, border, taps, pole, entry_states)
 
     final, product = tie(final, product)
-    last = shift_records(final, 1), shift_records(final, 2)
-    query = featured_query(segment_ids, streams, border, taps)
+    last = [shift_records(final, steps) for steps in (3, 2, 1)][::-1]
+    query = featured_query(segment_ids, features, border, taps)
     last, query, product, paired = tie(last, query, product, paired)
-    near = add_complex(last[0], last[1], power[0])
-    sent = near.astype(BF16)
+    leaving = final
+    for n in range(3):
+        leaving = add_complex(leaving, last[n], power[n])
+    leaving = leaving.astype(BF16)
+    entering = [shift_records(leaving, steps) for steps in (5, 1)][::-1]
+    entering, out_weight, paired = tie(entering, out_weight, paired)
     here = jnp.stack([out_weight, paired])
     lower, upper = turn(here, "y", 1), turn(here, "y", -1)
     gated = gated_rows(
-        segment_ids, state_ids, near, *[shift_records(sent, steps) for steps in (2, 4, 6)],
-        power, pole, residues, skip_row, entry_states, product, query,
+        segment_ids, state_ids, *entering, power, pole, residues, skip_row, entry_states, product, query
     )
 
-    gated, lower, upper = tie(gated, lower, upper)
     after, before = turn(gated, "zh", -1), turn(gated, "zh", 1)
     across, paired_across = turn(lower[0], "y", 1), turn(upper[1], "y", -1)
     weights = (here, upper, lower, across, paired_across)
@@ -487,10 +509,10 @@
 
     places = [[(top, 0), (bottom, 1)], [(whole, 0)], [(whole, 1)]]
     one = over_cores(partial_products([gated, after, before], places, weights, "products_near"))
-    one_1, one_3 = from_x(one, 1), from_x(one, 3)
-    far, one, one_1, one_3 = tie(far, one, one_1, one_3)
+    one_x = [from_x(one, k) for k in (2, 1, 3)]
+    far, one, one_x = tie(far, one, one_x)
     two = over_cores(partial_products(far, [[(top, 0)], [(top, 1)]], weights, "products_far"))
-    one = add([one[0], one_1, from_x(one, 2), one_3])
+    one = add([one[0], *one_x])
     two = add([two[0]] + [from_x(two, k) for k in range(1, 4)])
     near_own = one[:half]
     near_other = lax.ppermute(near_own, "core", [(0, 1), (1, 0)])

time: 160 us -> 149 us (0.931)
  starting transfers between devices: 71.2 us -> 65.3 us
  waiting for transfers between devices: 54.4 us -> 49 us
  local copies, waits for them, and re-layouts: 5.04 us -> 2.6 us
  Pallas kernels: 27.6 us -> 29.4 us
    ppermute x2, starting transfers between devices: 9.99 us -> 3.64 us  [over_cores(): other = lax.ppermute(parts[1], 'core', [(0, 1), (1, 0)])]
    ppermute x14, waiting for transfers between devices: 37.8 us -> 33.9 us  [turn(): return lax.ppermute(value, axis, [(i, (i + steps) % 4) for i in range(4)])]
    ppermute x14, starting transfers between devices: 25.1 us -> 21.6 us  [turn(): return lax.ppermute(value, axis, [(i, (i + steps) % 4) for i in range(4)])]
    ppermute x6, starting transfers between devices: 22.2 us -> 25.5 us  [shift_records(): lax.ppermute(value, ('y', 'zh', 'zl'), [(i, i + steps) for i in range(32...]
    unnamed x22 -> x28, local copies, waits for them, and re-layouts: 4.65 us -> 1.42 us
    ppermute x3, waiting for transfers between devices: 10.9 us -> 9.16 us  [home(): return lax.ppermute(sums, ('zh', 'core'), pairs)]
  transfers between devices with their start and end apart: 27 -> 27, of which waited for: 12 -> 13; matrix products, arithmetic and copies ran while one was open for 0% -> 0% of each run, Pallas kernels for 13% -> 16%
where the time goes in v3:
time: 149 us; the launch traced here: 148 us
  starting transfers between devices  65.3 us (44%)
  waiting for transfers between devices  49 us (33%)
  Pallas kernels  29.4 us (20%)
  local copies, waits for them, and re-layouts  2.6 us (2%)
    ppermute x14, waiting for transfers between devices, turn(): return lax.ppermute(value, axis, [(i, (i + steps) % 4) for i in range(4)])  33.9 us
    ppermute x6, starting transfers between devices, shift_records(): lax.ppermute(value, ('y', 'zh', 'zl'), [(i, i + steps) for i in range(32...  25.5 us
    ppermute x14, starting transfers between devices, turn(): return lax.ppermute(value, axis, [(i, (i + steps) % 4) for i in range(4)])  21.6 us
    ppermute x3, starting transfers between devices, home(): return lax.ppermute(sums, ('zh', 'core'), pairs)  11.8 us
    pallas_call x1, Pallas kernels, final_states(): call(final_kernel, (jax.ShapeDtypeStruct((2, MODES * 8, LANES), BF16), ja...  9.44 us
    ppermute x3, waiting for transfers between devices, home(): return lax.ppermute(sums, ('zh', 'core'), pairs)  9.16 us
    pallas_call x1, Pallas kernels, gated_rows(): call(modal_kernel, jax.ShapeDtypeStruct((ROWS, CH), BF16), [SMEM_SPEC] *...  9.11 us
    pallas_call x2, Pallas kernels, partial_products(): call(kernel, jax.ShapeDtypeStruct((2, 4, rows, 2 * COLS), BF16), [VMEM_SP...  4.84 us
  transfers between devices with their start and end apart: 27, of which 13 were waited for; matrix products, arithmetic and copies ran while one was open for 0% of the time, Pallas kernels for 16%

profile of v3, /device:TPU:1, one launch (start us, length us, event | category | flops | bytes accessed | tf_op | source)
XLA Modules:
  0.0 147.8 jit_solution(2833297084657359764)
XLA Ops:
  0.0 0.8 slice.123
  0.8 4.4 %collective-permute-start = (bf16[3,8,1024]{2,1,0:T(8,128)(2,1)S(1)}, bf16[3,8,1024]{2,1,0:T(8,128)(2,1)S(1)}, u32[]{:S(2)}, u32[]{:S(2)}) collective-permute-start(bf16[3,8,1024]{2,1,0:T(8,128)(2,1)S(1)} %slice.123), channel_id=1, source_target_pairs={{0,8},{8,16},{16,24},{24,32},{32,40},{40,48},{48,56},{56,64},{64,7... | collective-permute-start | bytes 147464 | tf_op jit(solution)/shard_map/ppermute | solution.py:447
  5.2 2.7 %prepare.1 = (f32[4,2,16,8,128]{4,3,2,1,0:T(8,128)}, f32[4,2,16,8,128]{4,3,2,1,0:T(8,128)}, f32[7,3,8,128]{3,2,1,0:T(8,128)}) custom-call(s32[8192]{0:T(1024)} %ids.7, bf16[3,7,64]{2,1,0:T(8,128)(2,1)} %bitcast.89, f32[16,1024]{1,0:T(8,128)} %decay.1, f32[16,1024]{1,0:T(8,128)} %angle.1), custom_call_target="tpu_custom_call" | custom-call | flops 3000000 | bytes 1048576 | tf_op jit(solution)/shard_map/prepare/pallas_call | solution.py:104
  7.9 1.7 %collective-permute-start.4 = (bf16[1024,256]{1,0:T(8,128)(2,1)}, bf16[1024,256]{1,0:T(8,128)(2,1)S(1)}, u32[]{:S(2)}, u32[]{:S(2)}) collective-permute-start(bf16[1024,256]{1,0:T(8,128)(2,1)} %param.19), channel_id=1, source_target_pairs={{0,8},{8,0},{1,9},{9,1},{2,10},{10,2},{3,11},{11,3},{4,12},{12,4},... | collective-permute-start | bytes 1572872 | tf_op jit(solution)/shard_map/ppermute | solution.py:466
  9.6 9.4 %final_states.1 = (bf16[2,128,128]{2,1,0:T(8,128)(2,1)}, f32[256,8,128]{2,1,0:T(8,128)}) custom-call(s32[8192]{0:T(1024)} %ids.7, s32[8]{0:T(128)} %picks.3, bf16[3,256,1024]{2,1,0:T(8,128)(2,1)} %feat.3, bf16[3,8,1024]{2,1,0:T(8,128)(2,1)} %copy-done.7, f32[7,3,8,128]{3,2,1,0:T(8,128)} %get-tuple-element.38.taps, ...), custom_call_target="tpu_custom_call" | custom-call | flops 8000000 | bytes 1048576 | tf_op jit(solution)/shard_map/final_states/pallas_call | solution.py:266
  19.0 6.5 %collective-permute-start.3 = (bf16[2,128,128]{2,1,0:T(8,128)(2,1)}, bf16[2,128,128]{2,1,0:T(8,128)(2,1)S(1)}, u32[]{:S(2)}, u32[]{:S(2)}) collective-permute-start(bf16[2,128,128]{2,1,0:T(8,128)(2,1)} %get-tuple-element.40), channel_id=1, source_target_pairs={{0,24},{8,32},{16,40},{24,48},{32,56},{40,64},{48,72},{56,80},{64,... | collective-permute-start | bytes 196616 | tf_op jit(solution)/shard_map/ppermute | solution.py:447
  25.5 3.5 %collective-permute-start.2 = (bf16[2,128,128]{2,1,0:T(8,128)(2,1)}, bf16[2,128,128]{2,1,0:T(8,128)(2,1)S(1)}, u32[]{:S(2)}, u32[]{:S(2)}) collective-permute-start(bf16[2,128,128]{2,1,0:T(8,128)(2,1)} %get-tuple-element.40), channel_id=1, source_target_pairs={{0,16},{8,24},{16,32},{24,40},{32,48},{40,56},{48,64},{56,72},{64,... | collective-permute-start | bytes 196616 | tf_op jit(solution)/shard_map/ppermute | solution.py:447
  29.1 2.3 %collective-permute-start.1 = (bf16[2,128,128]{2,1,0:T(8,128)(2,1)}, bf16[2,128,128]{2,1,0:T(8,128)(2,1)S(1)}, u32[]{:S(2)}, u32[]{:S(2)}) collective-permute-start(bf16[2,128,128]{2,1,0:T(8,128)(2,1)} %get-tuple-element.40), channel_id=1, source_target_pairs={{0,8},{8,16},{16,24},{24,32},{32,40},{40,48},{48,56},{56,64},{64,7... | collective-permute-start | bytes 196616 | tf_op jit(solution)/shard_map/ppermute | solution.py:447
  31.4 0.8 copy-done.8
  32.2 2.4 %featured_query.1.query = f32[256,8,128]{2,1,0:T(8,128)S(1)} custom-call(s32[8192]{0:T(1024)S(1)} %copy-done.5, bf16[3,256,1024]{2,1,0:T(8,128)(2,1)S(1)} %copy-done, bf16[3,8,1024]{2,1,0:T(8,128)(2,1)S(1)} %copy-done.8, f32[7,3,8,128]{3,2,1,0:T(8,128)S(1)} %copy-done.6), custom_call_target="tpu_custom_call" | custom-call | flops 2000000 | bytes 1048576 | tf_op jit(solution)/shard_map/featured_query/pallas_call | solution.py:297
  34.6 0.0 copy-start.12
  34.6 0.0 collective-permute-done.3
  34.6 0.0 collective-permute-done.2
  34.7 0.0 collective-permute-done.4
  34.8 0.0 copy-start.1
  34.8 0.0 copy-start.2
  34.8 0.0 copy-start.9
  34.8 0.0 copy-start.10
  34.8 0.0 copy-start.11
  34.9 0.6 copy-done.13
  35.5 5.4 %collective-permute-start.6 = (bf16[2,128,128]{2,1,0:T(8,128)(2,1)S(1)}, bf16[2,128,128]{2,1,0:T(8,128)(2,1)S(1)}, u32[]{:S(2)}, u32[]{:S(2)}) collective-permute-start(bf16[2,128,128]{2,1,0:T(8,128)(2,1)S(1)} %fusion.10), channel_id=1, source_target_pairs={{0,40},{8,48},{16,56},{24,64},{32,72},{40,80},{48,88},{56,96},{64,... | collective-permute-start | bytes 196616 | tf_op jit(solution)/shard_map/ppermute | solution.py:447
  40.9 3.4 %collective-permute-start.5 = (bf16[2,128,128]{2,1,0:T(8,128)(2,1)S(1)}, bf16[2,128,128]{2,1,0:T(8,128)(2,1)S(1)}, u32[]{:S(2)}, u32[]{:S(2)}) collective-permute-start(bf16[2,128,128]{2,1,0:T(8,128)(2,1)S(1)} %fusion.10), channel_id=1, source_target_pairs={{0,8},{8,16},{16,24},{24,32},{32,40},{40,48},{48,56},{56,64},{64,7... | collective-permute-start | bytes 196616 | tf_op jit(solution)/shard_map/ppermute | solution.py:447
  44.4 1.3 collective-permute-done.5.near
  45.7 0.1 pad_maximum_fusion.refs_3_.refs_2_
  45.8 4.5 %collective-permute-start.10 = (bf16[2,1024,256]{2,1,0:T(8,128)(2,1)S(1)}, bf16[2,1024,256]{2,1,0:T(8,128)(2,1)S(1)}, u32[]{:S(2)}, u32[]{:S(2)}) collective-permute-start(bf16[2,1024,256]{2,1,0:T(8,128)(2,1)S(1)} %pad_maximum_fusion.refs_3_.refs_2_), channel_id=1, source_target_pairs={{0,64},{64,128},{128,192},{192,0},{1,65},{65,129},{129,193},{193,1... | collective-permute-start | bytes 3145736 | tf_op jit(solution)/shard_map/ppermute | solution.py:451
  50.3 9.1 %gated_rows.1.refs_0_ = bf16[256,1024]{1,0:T(8,128)(2,1)S(1)} custom-call(s32[8192]{0:T(1024)S(1)} %copy-done.5, s32[8]{0:T(128)S(1)} %copy-done.11, bf16[2,128,128]{2,1,0:T(8,128)(2,1)S(1)} %collective-permute-done.5.near, bf16[2,128,128]{2,1,0:T(8,128)(2,1)S(1)} %collective-permute-done.6.far, f32[4,2,128,128]{3,2,1,0:T(8,128)S(1)} %bitcast.85, ...), custom_call_target="tpu_custom_call" | custom-call | flops 12000000 | bytes 1048576 | tf_op jit(solution)/shard_map/gated_rows/pallas_call | solution.py:368
  59.4 0.3 collective-permute-start.8
  59.7 3.4 %collective-permute-start.7 = (bf16[256,1024]{1,0:T(8,128)(2,1)S(1)}, bf16[256,1024]{1,0:T(8,128)(2,1)S(1)}, u32[]{:S(2)}, u32[]{:S(2)}) collective-permute-start(bf16[256,1024]{1,0:T(8,128)(2,1)S(1)} %gated_rows.1.refs_0_), channel_id=1, source_target_pairs={{0,48},{16,0},{32,16},{48,32},{1,49},{17,1},{33,17},{49,33},{2,50}... | collective-permute-start | bytes 1572872 | tf_op jit(solution)/shard_map/ppermute | solution.py:451
  63.1 6.7 %collective-permute-done.10.refs_5_.refs_4_ = bf16[2,1024,256]{2,1,0:T(8,128)(2,1)S(1)} collective-permute-done((bf16[2,1024,256]{2,1,0:T(8,128)(2,1)S(1)}, bf16[2,1024,256]{2,1,0:T(8,128)(2,1)S(1)}, u32[]{:S(2)}, u32[]{:S(2)}) %collective-permute-start.10) | collective-permute-done | bytes 1048608 | tf_op jit(solution)/shard_map/ppermute | solution.py:451
  69.8 2.3 %collective-permute-start.11 = (bf16[1024,256]{1,0:T(8,128)(2,1)S(1)}, bf16[1024,256]{1,0:T(8,128)(2,1)S(1)}, u32[]{:S(2)}, u32[]{:S(2)}) collective-permute-start(bf16[1024,256]{1,0:T(8,128)(2,1)S(1)} %slice_bitcast_fusion.5), channel_id=1, source_target_pairs={{0,64},{64,128},{128,192},{192,0},{1,65},{65,129},{129,193},{193,1... | collective-permute-start | bytes 1572872 | tf_op jit(solution)/shard_map/ppermute | solution.py:451
  72.1 0.6 collective-permute-start.12
  72.7 11.2 %collective-permute-done.8.refs_2_ = bf16[256,1024]{1,0:T(8,128)(2,1)S(1)} collective-permute-done((bf16[256,1024]{1,0:T(8,128)(2,1)S(1)}, bf16[256,1024]{1,0:T(8,128)(2,1)S(1)}, u32[]{:S(2)}, u32[]{:S(2)}) %collective-permute-start.8) | collective-permute-done | bytes 524320 | tf_op jit(solution)/shard_map/ppermute | solution.py:451
  83.9 2.1 %collective-permute-done.7.refs_1_ = bf16[256,1024]{1,0:T(8,128)(2,1)S(1)} collective-permute-done((bf16[256,1024]{1,0:T(8,128)(2,1)S(1)}, bf16[256,1024]{1,0:T(8,128)(2,1)S(1)}, u32[]{:S(2)}, u32[]{:S(2)}) %collective-permute-start.7) | collective-permute-done | bytes 524320 | tf_op jit(solution)/shard_map/ppermute | solution.py:451
  86.0 3.6 %products_near.1 = bf16[2,4,384,512]{3,2,1,0:T(8,128)(2,1)S(1)} custom-call(bf16[256,1024]{1,0:T(8,128)(2,1)S(1)} %gated_rows.1.refs_0_, bf16[256,1024]{1,0:T(8,128)(2,1)S(1)} %collective-permute-done.7.refs_1_, bf16[256,1024]{1,0:T(8,128)(2,1)S(1)} %collective-permute-done.8.refs_2_, bf16[2,1024,256]{2,1,0:T(8,128)(2,1)S(1)} %pad_maximum_fusion.refs_3_.refs_2_, ...), custom_call_target="tpu_custom_call" | custom-call | flops 1000000000 | bytes 1048576 | tf_op jit(solution)/shard_map/products_near/pallas_call | solution.py:409
  89.6 0.1 slice_bitcast_fusion
  89.7 1.1 collective-permute-start.15
  90.8 3.0 %collective-permute-done.15 = bf16[4,384,512]{2,1,0:T(8,128)(2,1)S(1)} collective-permute-done((bf16[4,384,512]{2,1,0:T(8,128)(2,1)S(1)}, bf16[4,384,512]{2,1,0:T(8,128)(2,1)S(1)}, u32[]{:S(2)}, u32[]{:S(2)}) %collective-permute-start.15) | collective-permute-done | bytes 1572896 | tf_op jit(solution)/shard_map/ppermute | solution.py:494
  93.9 0.4 fusion
  94.3 0.1 slice_bitcast_fusion.6
  94.4 2.6 %collective-permute-start.18 = (bf16[384,512]{1,0:T(8,128)(2,1)S(1)}, bf16[384,512]{1,0:T(8,128)(2,1)S(1)}, u32[]{:S(2)}, u32[]{:S(2)}) collective-permute-start(bf16[384,512]{1,0:T(8,128)(2,1)S(1)} %get-tuple-element.67), channel_id=1, source_target_pairs={{0,6},{2,0},{4,2},{6,4},{1,7},{3,1},{5,3},{7,5},{8,14},{10,8},{12,... | collective-permute-start | bytes 1179656 | tf_op jit(solution)/shard_map/ppermute | solution.py:451
  97.0 0.0 collective-permute-start.17
  97.0 1.7 %collective-permute-start.16 = (bf16[384,512]{1,0:T(8,128)(2,1)S(1)}, bf16[384,512]{1,0:T(8,128)(2,1)S(1)}, u32[]{:S(2)}, u32[]{:S(2)}) collective-permute-start(bf16[384,512]{1,0:T(8,128)(2,1)S(1)} %get-tuple-element.69), channel_id=1, source_target_pairs={{0,4},{2,6},{4,0},{6,2},{1,5},{3,7},{5,1},{7,3},{8,12},{10,14},{12... | collective-permute-start | bytes 1179656 | tf_op jit(solution)/shard_map/ppermute | solution.py:451
  98.7 2.5 %collective-permute-start.14 = (bf16[128,1024]{1,0:T(8,128)(2,1)S(1)}, bf16[128,1024]{1,0:T(8,128)(2,1)S(1)}, u32[]{:S(2)}, u32[]{:S(2)}) collective-permute-start(bf16[128,1024]{1,0:T(8,128)(2,1)S(1)} %slice.139), channel_id=1, source_target_pairs={{0,16},{16,32},{32,48},{48,0},{1,17},{17,33},{33,49},{49,1},{2,18}... | collective-permute-start | bytes 786440 | tf_op jit(solution)/shard_map/ppermute | solution.py:451
  101.3 1.1 collective-permute-start.13
  102.4 10.3 %collective-permute-done.14.refs_1_ = bf16[128,1024]{1,0:T(8,128)(2,1)S(1)} collective-permute-done((bf16[128,1024]{1,0:T(8,128)(2,1)S(1)}, bf16[128,1024]{1,0:T(8,128)(2,1)S(1)}, u32[]{:S(2)}, u32[]{:S(2)}) %collective-permute-start.14) | collective-permute-done | bytes 262176 | tf_op jit(solution)/shard_map/ppermute | solution.py:451
  112.7 1.5 collective-permute-done.13.refs_0_
  114.2 1.5 %collective-permute-done.16 = bf16[384,512]{1,0:T(8,128)(2,1)S(1)} collective-permute-done((bf16[384,512]{1,0:T(8,128)(2,1)S(1)}, bf16[384,512]{1,0:T(8,128)(2,1)S(1)}, u32[]{:S(2)}, u32[]{:S(2)}) %collective-permute-start.16) | collective-permute-done | bytes 393248 | tf_op jit(solution)/shard_map/ppermute | solution.py:451
  115.7 1.3 products_far.1
  117.0 2.5 %collective-permute-start.20 = (bf16[4,128,512]{2,1,0:T(8,128)(2,1)S(1)}, bf16[4,128,512]{2,1,0:T(8,128)(2,1)S(1)}, u32[]{:S(2)}, u32[]{:S(2)}) collective-permute-start(bf16[4,128,512]{2,1,0:T(8,128)(2,1)S(1)} %slice_bitcast_fusion.2), channel_id=1, source_target_pairs={{0,1},{1,0},{2,3},{3,2},{4,5},{5,4},{6,7},{7,6},{8,9},{9,8},{10,11... | collective-permute-start | bytes 1572872 | tf_op jit(solution)/shard_map/ppermute | solution.py:494
  119.5 1.5 %collective-permute-done.20 = bf16[4,128,512]{2,1,0:T(8,128)(2,1)S(1)} collective-permute-done((bf16[4,128,512]{2,1,0:T(8,128)(2,1)S(1)}, bf16[4,128,512]{2,1,0:T(8,128)(2,1)S(1)}, u32[]{:S(2)}, u32[]{:S(2)}) %collective-permute-start.20) | collective-permute-done | bytes 524320 | tf_op jit(solution)/shard_map/ppermute | solution.py:494
  121.1 0.1 fusion.1
  121.2 0.1 collective-permute-start.21
  121.3 2.7 %collective-permute-start.23 = (bf16[128,512]{1,0:T(8,128)(2,1)S(1)}, bf16[128,512]{1,0:T(8,128)(2,1)S(1)}, u32[]{:S(2)}, u32[]{:S(2)}) collective-permute-start(bf16[128,512]{1,0:T(8,128)(2,1)S(1)} %get-tuple-element.77), channel_id=1, source_target_pairs={{0,6},{2,0},{4,2},{6,4},{1,7},{3,1},{5,3},{7,5},{8,14},{10,8},{12,... | collective-permute-start | bytes 393224 | tf_op jit(solution)/shard_map/ppermute | solution.py:451
  124.0 0.2 fusion.4
  124.2 1.0 collective-permute-start.19
  125.3 3.5 %collective-permute-start.26 = (bf16[256,512]{1,0:T(8,128)(2,1)S(1)}, bf16[256,512]{1,0:T(8,128)(2,1)S(1)}, u32[]{:S(2)}, u32[]{:S(2)}) collective-permute-start(bf16[256,512]{1,0:T(8,128)(2,1)S(1)} %slice.174), channel_id=1, source_target_pairs={{0,16},{1,48},{16,32},{17,0},{32,49},{33,17},{48,1},{49,33},{2,18}... | collective-permute-start | bytes 786440 | tf_op jit(solution)/shard_map/ppermute | solution.py:502
  128.7 0.4 collective-permute-done.23
  129.1 0.2 collective-permute-done.22
  129.3 0.1 fusion.7
  129.4 7.0 %collective-permute-start.25 = (bf16[128,512]{1,0:T(8,128)(2,1)S(1)}, bf16[128,512]{1,0:T(8,128)(2,1)S(1)}, u32[]{:S(2)}, u32[]{:S(2)}) collective-permute-start(bf16[128,512]{1,0:T(8,128)(2,1)S(1)} %fusion.7), channel_id=1, source_target_pairs={{1,32},{17,48},{33,1},{49,17},{3,34},{19,50},{35,3},{51,19},{5,36}... | collective-permute-start | bytes 393224 | tf_op jit(solution)/shard_map/ppermute | solution.py:502
  136.4 1.3 collective-permute-start.24
  137.8 1.3 collective-permute-done.25.far_bottom
  139.1 7.8 %collective-permute-done.24.far_top = bf16[128,512]{1,0:T(8,128)(2,1)S(1)} collective-permute-done((bf16[128,512]{1,0:T(8,128)(2,1)S(1)}, bf16[128,512]{1,0:T(8,128)(2,1)S(1)}, u32[]{:S(2)}, u32[]{:S(2)}) %collective-permute-start.24) | collective-permute-done | bytes 131104 | tf_op jit(solution)/shard_map/ppermute | solution.py:502
  146.9 0.8 assemble.1
  (47 shorter events, 0.4 us)
Async XLA Ops:
  0.8 7.1 %collective-permute-start = (bf16[3,8,1024]{2,1,0:T(8,128)(2,1)S(1)}, bf16[3,8,1024]{2,1,0:T(8,128)(2,1)S(1)}, u32[]{:S(2)}, u32[]{:S(2)}) collective-permute-start(bf16[3,8,1024]{2,1,0:T(8,128)(2,1)S(1)} %slice.123), channel_id=1, source_target_pairs={{0,8},{8,16},{16,24},{24,32},{32,40},{40,48},{48,56},{56,64},{64,7... | collective-permute-start | bytes 147464 | tf_op jit(solution)/shard_map/ppermute | solution.py:447
  7.9 1.7 %copy-start.7 = (bf16[3,8,1024]{2,1,0:T(8,128)(2,1)}, bf16[3,8,1024]{2,1,0:T(8,128)(2,1)S(1)}, u32[]{:S(2)}) copy-start(bf16[3,8,1024]{2,1,0:T(8,128)(2,1)S(1)} %collective-permute-done.border) | copy-start | bytes 147460
  7.9 26.8 %collective-permute-start.4 = (bf16[1024,256]{1,0:T(8,128)(2,1)}, bf16[1024,256]{1,0:T(8,128)(2,1)S(1)}, u32[]{:S(2)}, u32[]{:S(2)}) collective-permute-start(bf16[1024,256]{1,0:T(8,128)(2,1)} %param.19), channel_id=1, source_target_pairs={{0,8},{8,0},{1,9},{9,1},{2,10},{10,2},{3,11},{11,3},{4,12},{12,4},... | collective-permute-start | bytes 1572872 | tf_op jit(solution)/shard_map/ppermute | solution.py:466
  9.6 21.8 %copy-start = (bf16[3,256,1024]{2,1,0:T(8,128)(2,1)S(1)}, bf16[3,256,1024]{2,1,0:T(8,128)(2,1)}, u32[]{:S(2)}) copy-start(bf16[3,256,1024]{2,1,0:T(8,128)(2,1)} %feat.3) | copy-start | bytes 4718596
  9.6 21.8 %copy-start.5 = (s32[8192]{0:T(1024)S(1)}, s32[8192]{0:T(1024)}, u32[]{:S(2)}) copy-start(s32[8192]{0:T(1024)} %ids.7) | copy-start | bytes 98308
  9.6 21.8 %copy-start.6 = (f32[7,3,8,128]{3,2,1,0:T(8,128)S(1)}, f32[7,3,8,128]{3,2,1,0:T(8,128)}, u32[]{:S(2)}) copy-start(f32[7,3,8,128]{3,2,1,0:T(8,128)} %get-tuple-element.38.taps) | copy-start | bytes 258052
  19.0 15.7 %copy-start.3 = (f32[4,2,16,8,128]{4,3,2,1,0:T(8,128)S(1)}, f32[4,2,16,8,128]{4,3,2,1,0:T(8,128)}, u32[]{:S(2)}) copy-start(f32[4,2,16,8,128]{4,3,2,1,0:T(8,128)} %get-tuple-element.41) | copy-start | bytes 1572868
  19.0 15.6 %collective-permute-start.3 = (bf16[2,128,128]{2,1,0:T(8,128)(2,1)}, bf16[2,128,128]{2,1,0:T(8,128)(2,1)S(1)}, u32[]{:S(2)}, u32[]{:S(2)}) collective-permute-start(bf16[2,128,128]{2,1,0:T(8,128)(2,1)} %get-tuple-element.40), channel_id=1, source_target_pairs={{0,24},{8,32},{16,40},{24,48},{32,56},{40,64},{48,72},{56,80},{64,... | collective-permute-start | bytes 196616 | tf_op jit(solution)/shard_map/ppermute | solution.py:447
  25.5 9.1 %collective-permute-start.2 = (bf16[2,128,128]{2,1,0:T(8,128)(2,1)}, bf16[2,128,128]{2,1,0:T(8,128)(2,1)S(1)}, u32[]{:S(2)}, u32[]{:S(2)}) collective-permute-start(bf16[2,128,128]{2,1,0:T(8,128)(2,1)} %get-tuple-element.40), channel_id=1, source_target_pairs={{0,16},{8,24},{16,32},{24,40},{32,48},{40,56},{48,64},{56,72},{64,... | collective-permute-start | bytes 196616 | tf_op jit(solution)/shard_map/ppermute | solution.py:447
  29.1 5.6 %collective-permute-start.1 = (bf16[2,128,128]{2,1,0:T(8,128)(2,1)}, bf16[2,128,128]{2,1,0:T(8,128)(2,1)S(1)}, u32[]{:S(2)}, u32[]{:S(2)}) collective-permute-start(bf16[2,128,128]{2,1,0:T(8,128)(2,1)} %get-tuple-element.40), channel_id=1, source_target_pairs={{0,8},{8,16},{16,24},{24,32},{32,40},{40,48},{48,56},{56,64},{64,7... | collective-permute-start | bytes 196616 | tf_op jit(solution)/shard_map/ppermute | solution.py:447
  31.4 0.8 copy-start.8
  34.6 0.8 copy-start.13
  34.6 11.0 %copy-start.12 = (bf16[1024,256]{1,0:T(8,128)(2,1)S(1)}, bf16[1024,256]{1,0:T(8,128)(2,1)}, u32[]{:S(2)}) copy-start(bf16[1024,256]{1,0:T(8,128)(2,1)} %param.19) | copy-start | bytes 1572868
  34.8 15.5 %copy-start.1 = (f32[8,2,16,1024]{3,2,1,0:T(8,128)S(1)}, f32[8,2,16,1024]{3,2,1,0:T(8,128)}, u32[]{:S(2)}) copy-start(f32[8,2,16,1024]{3,2,1,0:T(8,128)} %entry.3) | copy-start | bytes 3145732
  34.8 15.4 %copy-start.2 = (f32[4,2,16,8,128]{4,3,2,1,0:T(8,128)S(1)}, f32[4,2,16,8,128]{4,3,2,1,0:T(8,128)}, u32[]{:S(2)}) copy-start(f32[4,2,16,8,128]{4,3,2,1,0:T(8,128)} %get-tuple-element.39.pole) | copy-start | bytes 1572868
  34.8 15.4 %copy-start.4 = (f32[256,8,128]{2,1,0:T(8,128)S(1)}, f32[256,8,128]{2,1,0:T(8,128)}, u32[]{:S(2)}) copy-start(f32[256,8,128]{2,1,0:T(8,128)} %get-tuple-element.50.product) | copy-start | bytes 3145732
  34.8 15.4 %copy-start.9 = (f32[2,16,1024]{2,1,0:T(8,128)S(1)}, f32[2,16,1024]{2,1,0:T(8,128)}, u32[]{:S(2)}) copy-start(f32[2,16,1024]{2,1,0:T(8,128)} %res.1) | copy-start | bytes 393220
  34.8 15.4 %copy-start.10 = (f32[1024]{0:T(1024)S(1)}, f32[1024]{0:T(1024)}, u32[]{:S(2)}) copy-start(f32[1024]{0:T(1024)} %param.15) | copy-start | bytes 12292
  34.8 15.4 %copy-start.11 = (s32[8]{0:T(128)S(1)}, s32[8]{0:T(128)}, u32[]{:S(2)}) copy-start(s32[8]{0:T(128)} %picks.3) | copy-start | bytes 100
  35.5 8.9 %collective-permute-start.6 = (bf16[2,128,128]{2,1,0:T(8,128)(2,1)S(1)}, bf16[2,128,128]{2,1,0:T(8,128)(2,1)S(1)}, u32[]{:S(2)}, u32[]{:S(2)}) collective-permute-start(bf16[2,128,128]{2,1,0:T(8,128)(2,1)S(1)} %fusion.10), channel_id=1, source_target_pairs={{0,40},{8,48},{16,56},{24,64},{32,72},{40,80},{48,88},{56,96},{64,... | collective-permute-start | bytes 196616 | tf_op jit(solution)/shard_map/ppermute | solution.py:447
  40.9 4.7 %collective-permute-start.5 = (bf16[2,128,128]{2,1,0:T(8,128)(2,1)S(1)}, bf16[2,128,128]{2,1,0:T(8,128)(2,1)S(1)}, u32[]{:S(2)}, u32[]{:S(2)}) collective-permute-start(bf16[2,128,128]{2,1,0:T(8,128)(2,1)S(1)} %fusion.10), channel_id=1, source_target_pairs={{0,8},{8,16},{16,24},{24,32},{32,40},{40,48},{48,56},{56,64},{64,7... | collective-permute-start | bytes 196616 | tf_op jit(solution)/shard_map/ppermute | solution.py:447
  45.8 24.0 %collective-permute-start.10 = (bf16[2,1024,256]{2,1,0:T(8,128)(2,1)S(1)}, bf16[2,1024,256]{2,1,0:T(8,128)(2,1)S(1)}, u32[]{:S(2)}, u32[]{:S(2)}) collective-permute-start(bf16[2,1024,256]{2,1,0:T(8,128)(2,1)S(1)} %pad_maximum_fusion.refs_3_.refs_2_), channel_id=1, source_target_pairs={{0,64},{64,128},{128,192},{192,0},{1,65},{65,129},{129,193},{193,1... | collective-permute-start | bytes 3145736 | tf_op jit(solution)/shard_map/ppermute | solution.py:451
  50.2 21.8 %collective-permute-start.9 = (bf16[2,1024,256]{2,1,0:T(8,128)(2,1)S(1)}, bf16[2,1024,256]{2,1,0:T(8,128)(2,1)S(1)}, u32[]{:S(2)}, u32[]{:S(2)}) collective-permute-start(bf16[2,1024,256]{2,1,0:T(8,128)(2,1)S(1)} %pad_maximum_fusion.refs_3_.refs_2_), channel_id=1, source_target_pairs={{0,192},{64,0},{128,64},{192,128},{1,193},{65,1},{129,65},{193,129... | collective-permute-start | bytes 3145736 | tf_op jit(solution)/shard_map/ppermute | solution.py:451
  59.4 24.5 %collective-permute-start.8 = (bf16[256,1024]{1,0:T(8,128)(2,1)S(1)}, bf16[256,1024]{1,0:T(8,128)(2,1)S(1)}, u32[]{:S(2)}, u32[]{:S(2)}) collective-permute-start(bf16[256,1024]{1,0:T(8,128)(2,1)S(1)} %gated_rows.1.refs_0_), channel_id=1, source_target_pairs={{0,16},{16,32},{32,48},{48,0},{1,17},{17,33},{33,49},{49,1},{2,18}... | collective-permute-start | bytes 1572872 | tf_op jit(solution)/shard_map/ppermute | solution.py:451
  59.7 26.3 %collective-permute-start.7 = (bf16[256,1024]{1,0:T(8,128)(2,1)S(1)}, bf16[256,1024]{1,0:T(8,128)(2,1)S(1)}, u32[]{:S(2)}, u32[]{:S(2)}) collective-permute-start(bf16[256,1024]{1,0:T(8,128)(2,1)S(1)} %gated_rows.1.refs_0_), channel_id=1, source_target_pairs={{0,48},{16,0},{32,16},{48,32},{1,49},{17,1},{33,17},{49,33},{2,50}... | collective-permute-start | bytes 1572872 | tf_op jit(solution)/shard_map/ppermute | solution.py:451
  69.8 16.2 %collective-permute-start.11 = (bf16[1024,256]{1,0:T(8,128)(2,1)S(1)}, bf16[1024,256]{1,0:T(8,128)(2,1)S(1)}, u32[]{:S(2)}, u32[]{:S(2)}) collective-permute-start(bf16[1024,256]{1,0:T(8,128)(2,1)S(1)} %slice_bitcast_fusion.5), channel_id=1, source_target_pairs={{0,64},{64,128},{128,192},{192,0},{1,65},{65,129},{129,193},{193,1... | collective-permute-start | bytes 1572872 | tf_op jit(solution)/shard_map/ppermute | solution.py:451
  72.1 13.9 %collective-permute-start.12 = (bf16[1024,256]{1,0:T(8,128)(2,1)S(1)}, bf16[1024,256]{1,0:T(8,128)(2,1)S(1)}, u32[]{:S(2)}, u32[]{:S(2)}) collective-permute-start(bf16[1024,256]{1,0:T(8,128)(2,1)S(1)} %slice_bitcast_fusion.4), channel_id=1, source_target_pairs={{0,192},{64,0},{128,64},{192,128},{1,193},{65,1},{129,65},{193,129... | collective-permute-start | bytes 1572872 | tf_op jit(solution)/shard_map/ppermute | solution.py:451
  89.7 4.2 %collective-permute-start.15 = (bf16[4,384,512]{2,1,0:T(8,128)(2,1)S(1)}, bf16[4,384,512]{2,1,0:T(8,128)(2,1)S(1)}, u32[]{:S(2)}, u32[]{:S(2)}) collective-permute-start(bf16[4,384,512]{2,1,0:T(8,128)(2,1)S(1)} %slice_bitcast_fusion), channel_id=1, source_target_pairs={{0,1},{1,0},{2,3},{3,2},{4,5},{5,4},{6,7},{7,6},{8,9},{9,8},{10,11... | collective-permute-start | bytes 4718600 | tf_op jit(solution)/shard_map/ppermute | solution.py:494
  94.4 19.8 %collective-permute-start.18 = (bf16[384,512]{1,0:T(8,128)(2,1)S(1)}, bf16[384,512]{1,0:T(8,128)(2,1)S(1)}, u32[]{:S(2)}, u32[]{:S(2)}) collective-permute-start(bf16[384,512]{1,0:T(8,128)(2,1)S(1)} %get-tuple-element.67), channel_id=1, source_target_pairs={{0,6},{2,0},{4,2},{6,4},{1,7},{3,1},{5,3},{7,5},{8,14},{10,8},{12,... | collective-permute-start | bytes 1179656 | tf_op jit(solution)/shard_map/ppermute | solution.py:451
  97.0 17.2 %collective-permute-start.17 = (bf16[384,512]{1,0:T(8,128)(2,1)S(1)}, bf16[384,512]{1,0:T(8,128)(2,1)S(1)}, u32[]{:S(2)}, u32[]{:S(2)}) collective-permute-start(bf16[384,512]{1,0:T(8,128)(2,1)S(1)} %get-tuple-element.68), channel_id=1, source_target_pairs={{0,2},{2,4},{4,6},{6,0},{1,3},{3,5},{5,7},{7,1},{8,10},{10,12},{12... | collective-permute-start | bytes 1179656 | tf_op jit(solution)/shard_map/ppermute | solution.py:451
  97.0 18.7 %collective-permute-start.16 = (bf16[384,512]{1,0:T(8,128)(2,1)S(1)}, bf16[384,512]{1,0:T(8,128)(2,1)S(1)}, u32[]{:S(2)}, u32[]{:S(2)}) collective-permute-start(bf16[384,512]{1,0:T(8,128)(2,1)S(1)} %get-tuple-element.69), channel_id=1, source_target_pairs={{0,4},{2,6},{4,0},{6,2},{1,5},{3,7},{5,1},{7,3},{8,12},{10,14},{12... | collective-permute-start | bytes 1179656 | tf_op jit(solution)/shard_map/ppermute | solution.py:451
  98.7 14.0 %collective-permute-start.14 = (bf16[128,1024]{1,0:T(8,128)(2,1)S(1)}, bf16[128,1024]{1,0:T(8,128)(2,1)S(1)}, u32[]{:S(2)}, u32[]{:S(2)}) collective-permute-start(bf16[128,1024]{1,0:T(8,128)(2,1)S(1)} %slice.139), channel_id=1, source_target_pairs={{0,16},{16,32},{32,48},{48,0},{1,17},{17,33},{33,49},{49,1},{2,18}... | collective-permute-start | bytes 786440 | tf_op jit(solution)/shard_map/ppermute | solution.py:451
  101.3 12.9 %collective-permute-start.13 = (bf16[128,1024]{1,0:T(8,128)(2,1)S(1)}, bf16[128,1024]{1,0:T(8,128)(2,1)S(1)}, u32[]{:S(2)}, u32[]{:S(2)}) collective-permute-start(bf16[128,1024]{1,0:T(8,128)(2,1)S(1)} %slice.138), channel_id=1, source_target_pairs={{0,48},{16,0},{32,16},{48,32},{1,49},{17,1},{33,17},{49,33},{2,50}... | collective-permute-start | bytes 786440 | tf_op jit(solution)/shard_map/ppermute | solution.py:451
  117.0 4.0 %collective-permute-start.20 = (bf16[4,128,512]{2,1,0:T(8,128)(2,1)S(1)}, bf16[4,128,512]{2,1,0:T(8,128)(2,1)S(1)}, u32[]{:S(2)}, u32[]{:S(2)}) collective-permute-start(bf16[4,128,512]{2,1,0:T(8,128)(2,1)S(1)} %slice_bitcast_fusion.2), channel_id=1, source_target_pairs={{0,1},{1,0},{2,3},{3,2},{4,5},{5,4},{6,7},{7,6},{8,9},{9,8},{10,11... | collective-permute-start | bytes 1572872 | tf_op jit(solution)/shard_map/ppermute | solution.py:494
  121.2 7.5 %collective-permute-start.21 = (bf16[128,512]{1,0:T(8,128)(2,1)S(1)}, bf16[128,512]{1,0:T(8,128)(2,1)S(1)}, u32[]{:S(2)}, u32[]{:S(2)}) collective-permute-start(bf16[128,512]{1,0:T(8,128)(2,1)S(1)} %get-tuple-element.76), channel_id=1, source_target_pairs={{0,2},{2,4},{4,6},{6,0},{1,3},{3,5},{5,7},{7,1},{8,10},{10,12},{12... | collective-permute-start | bytes 393224 | tf_op jit(solution)/shard_map/ppermute | solution.py:451
  121.3 7.8 %collective-permute-start.23 = (bf16[128,512]{1,0:T(8,128)(2,1)S(1)}, bf16[128,512]{1,0:T(8,128)(2,1)S(1)}, u32[]{:S(2)}, u32[]{:S(2)}) collective-permute-start(bf16[128,512]{1,0:T(8,128)(2,1)S(1)} %get-tuple-element.77), channel_id=1, source_target_pairs={{0,6},{2,0},{4,2},{6,4},{1,7},{3,1},{5,3},{7,5},{8,14},{10,8},{12,... | collective-permute-start | bytes 393224 | tf_op jit(solution)/shard_map/ppermute | solution.py:451
  124.0 5.3 %collective-permute-start.22 = (bf16[128,512]{1,0:T(8,128)(2,1)S(1)}, bf16[128,512]{1,0:T(8,128)(2,1)S(1)}, u32[]{:S(2)}, u32[]{:S(2)}) collective-permute-start(bf16[128,512]{1,0:T(8,128)(2,1)S(1)} %get-tuple-element.78), channel_id=1, source_target_pairs={{0,4},{2,6},{4,0},{6,2},{1,5},{3,7},{5,1},{7,3},{8,12},{10,14},{12... | collective-permute-start | bytes 393224 | tf_op jit(solution)/shard_map/ppermute | solution.py:451
  124.2 13.5 %collective-permute-start.19 = (bf16[128,512]{1,0:T(8,128)(2,1)S(1)}, bf16[128,512]{1,0:T(8,128)(2,1)S(1)}, u32[]{:S(2)}, u32[]{:S(2)}) collective-permute-start(bf16[128,512]{1,0:T(8,128)(2,1)S(1)} %slice.167.near_own), channel_id=1, source_target_pairs={{0,1},{1,0},{2,3},{3,2},{4,5},{5,4},{6,7},{7,6},{8,9},{9,8},{10,11... | collective-permute-start | bytes 393224 | tf_op jit(solution)/shard_map/ppermute | solution.py:518
  125.3 12.5 %collective-permute-start.26 = (bf16[256,512]{1,0:T(8,128)(2,1)S(1)}, bf16[256,512]{1,0:T(8,128)(2,1)S(1)}, u32[]{:S(2)}, u32[]{:S(2)}) collective-permute-start(bf16[256,512]{1,0:T(8,128)(2,1)S(1)} %slice.174), channel_id=1, source_target_pairs={{0,16},{1,48},{16,32},{17,0},{32,49},{33,17},{48,1},{49,33},{2,18}... | collective-permute-start | bytes 786440 | tf_op jit(solution)/shard_map/ppermute | solution.py:502
  129.4 9.7 %collective-permute-start.25 = (bf16[128,512]{1,0:T(8,128)(2,1)S(1)}, bf16[128,512]{1,0:T(8,128)(2,1)S(1)}, u32[]{:S(2)}, u32[]{:S(2)}) collective-permute-start(bf16[128,512]{1,0:T(8,128)(2,1)S(1)} %fusion.7), channel_id=1, source_target_pairs={{1,32},{17,48},{33,1},{49,17},{3,34},{19,50},{35,3},{51,19},{5,36}... | collective-permute-start | bytes 393224 | tf_op jit(solution)/shard_map/ppermute | solution.py:502
  136.4 10.5 %collective-permute-start.24 = (bf16[128,512]{1,0:T(8,128)(2,1)S(1)}, bf16[128,512]{1,0:T(8,128)(2,1)S(1)}, u32[]{:S(2)}, u32[]{:S(2)}) collective-permute-start(bf16[128,512]{1,0:T(8,128)(2,1)S(1)} %fusion.7), channel_id=1, source_target_pairs={{0,32},{16,48},{32,1},{48,17},{2,34},{18,50},{34,3},{50,19},{4,36}... | collective-permute-start | bytes 393224 | tf_op jit(solution)/shard_map/ppermute | solution.py:502

commit v4 on v3

--- a/solution.py
+++ b/solution.py
@@ -384,7 +384,8 @@
 
 
 def partial_products(blocks, places, weights, name):
-    rows = sum(part.stop - part.start for place in places for part, core in place) // 2
+    counts = [sum(part.stop - part.start for place in places for part, core in place if core == n) for n in range(2)]
+    rows, total = counts[0], sum(counts)
 
     def kernel(*refs):
         block_refs, weight_refs = refs[: len(blocks)], refs[len(blocks) : -2]
@@ -403,21 +404,24 @@
                 slot = (y + shift - x + 4) % 4
                 to = pl.multiple_of((zl + which) % 2 * COLS, COLS)
                 part = jnp.dot(all_rows[...], weight, preferred_element_type=F32).astype(BF16)
-                out_ref[core, slot, :, pl.ds(to, COLS)] = part[:rows]
-                out_ref[1 - core, slot, :, pl.ds(to, COLS)] = part[rows:]
+                if counts[1]:
+                    out_ref[core, slot, :, pl.ds(to, COLS)] = part[:rows]
+                    out_ref[1 - core, slot, :, pl.ds(to, COLS)] = part[rows:]
+                else:
+                    out_ref[0, slot, :, pl.ds(to, COLS)] = part
 
     return call(
         kernel,
-        jax.ShapeDtypeStruct((2, 4, rows, 2 * COLS), BF16),
+        jax.ShapeDtypeStruct((2 if counts[1] else 1, 4, rows, 2 * COLS), BF16),
         [VMEM_SPEC] * (len(blocks) + 5),
-        [pltpu.VMEM((2 * rows, CH), BF16)],
+        [pltpu.VMEM((total, CH), BF16)],
         24,
         name,
         1_000_000_000,
     )(*blocks, *weights)
 
 
-def assemble_kernel(near_own, near_other, far_top, far_bottom, side, out_ref):
+def assemble_kernel(near_own, near_other, far, side, out_ref):
     zh, core = lax.axis_index("zh"), lax.axis_index("core")
     half = ROWS // 2
     same = pl.ds(pl.multiple_of(zh % 2 * 2 * COLS, 2 * COLS), 2 * COLS)
@@ -430,8 +434,7 @@
 
     @pl.when(zh // 2 != core)
     def _():
-        out_ref[:half, same] = far_top[...]
-        out_ref[half:, same] = far_bottom[...]
+        out_ref[:, same] = far[...]
 
     out_ref[:, other] = side[...]
 
@@ -511,16 +514,23 @@
     one = over_cores(partial_products([gated, after, before], places, weights, "products_near"))
     one_x = [from_x(one, k) for k in (2, 1, 3)]
     far, one, one_x = tie(far, one, one_x)
-    two = over_cores(partial_products(far, [[(top, 0)], [(top, 1)]], weights, "products_far"))
+    two = partial_products(far, [[(top, 0)], [(top, 0)]], weights, "products_far")[0]
+    pairs = [(2 * zh + 1 - zh // 2, 2 * zh + zh // 2) for zh in range(4)]
+    two = (two.astype(F32) + lax.ppermute(two, ("zh", "core"), pairs).astype(F32)).astype(BF16)
     one = add([one[0], *one_x])
-    two = add([two[0]] + [from_x(two, k) for k in range(1, 4)])
+    two_x = []
+    for k in (2, 1, 3):
+        pairs = [(8 * zh + 2 * x + zh // 2, 8 * zh + 2 * ((x + k) % 4) + zh // 2) for zh in range(4) for x in range(4)]
+        two_x.append(lax.ppermute(two[k], ("zh", "x", "core"), pairs))
+    two = add([two[0], *two_x])
     near_own = one[:half]
     near_other = lax.ppermute(near_own, "core", [(0, 1), (1, 0)])
     side = home(one[half:], [(0, 1), (1, 3)])
-    far_top, far_bottom = home(two, [(0, 2)]), home(two, [(1, 2)])
+    pairs = [(2 * zh + zh // 2, 2 * ((zh + 2) % 4) + zh // 2) for zh in range(4)]
+    far_sums = lax.ppermute(two, ("zh", "core"), pairs)
     return call(
-        assemble_kernel, jax.ShapeDtypeStruct((ROWS, CH), BF16), [VMEM_SPEC] * 5, [], 8, "assemble", 1_000_000
-    )(near_own, near_other, far_top, far_bottom, side)
+        assemble_kernel, jax.ShapeDtypeStruct((ROWS, CH), BF16), [VMEM_SPEC] * 4, [], 8, "assemble", 1_000_000
+    )(near_own, near_other, far_sums, side)
 
 
 def solution(mesh):

time: 149 us -> 148 us (level)
  waiting for transfers between devices: 49 us -> 44 us
  starting transfers between devices: 65.3 us -> 68.3 us
    ppermute x1, starting transfers between devices: 1.02 us -> 10.2 us  [shards(): near_other = lax.ppermute(near_own, 'core', [(0, 1), (1, 0)])]
    ppermute x3 -> x1, starting transfers between devices: 11.8 us -> 2.63 us  [home(): return lax.ppermute(sums, ('zh', 'core'), pairs)]
    ppermute x3 -> x1, waiting for transfers between devices: 9.16 us -> 0.01 us  [home(): return lax.ppermute(sums, ('zh', 'core'), pairs)]
    ppermute x0 -> x5, starting transfers between devices: none -> 7.73 us  [the longest x1 4.41 us: shards(): lax.ppermute(two, ('zh', 'core'), pairs).astype(F32)]
    ppermute x0 -> x5, waiting for transfers between devices: none -> 5.67 us  [the longest x1 3.46 us: shards(): far_sums = lax.ppermute(two, ('zh', 'core'), pairs)]
    ppermute x14 -> x11, starting transfers between devices: 21.6 us -> 18.8 us  [turn(): return lax.ppermute(value, axis, [(i, (i + steps) % 4) for i in range(4)])]
    ppermute x2 -> x1, starting transfers between devices: 3.64 us -> 1.81 us  [over_cores(): other = lax.ppermute(parts[1], 'core', [(0, 1), (1, 0)])]
    ppermute x2 -> x1, waiting for transfers between devices: 4.57 us -> 3.04 us  [over_cores(): other = lax.ppermute(parts[1], 'core', [(0, 1), (1, 0)])]
  transfers between devices with their start and end apart: 27 -> 26, of which waited for: 13 -> 11; matrix products, arithmetic and copies ran while one was open for 0% -> 0% of each run, Pallas kernels for 16% -> 16%
where the time goes in v4:
time: 148 us; the launch traced here: 146 us
  starting transfers between devices  68.3 us (46%)
  waiting for transfers between devices  44 us (30%)
  Pallas kernels  29.3 us (20%)
  local copies, waits for them, and re-layouts  2.59 us (2%)
    ppermute x11, waiting for transfers between devices, turn(): return lax.ppermute(value, axis, [(i, (i + steps) % 4) for i in range(4)])  33 us
    ppermute x6, starting transfers between devices, shift_records(): lax.ppermute(value, ('y', 'zh', 'zl'), [(i, i + steps) for i in range(32...  25.4 us
    ppermute x11, starting transfers between devices, turn(): return lax.ppermute(value, axis, [(i, (i + steps) % 4) for i in range(4)])  18.8 us
    ppermute x1, starting transfers between devices, shards(): near_other = lax.ppermute(near_own, 'core', [(0, 1), (1, 0)])  10.2 us
    pallas_call x1, Pallas kernels, final_states(): call(final_kernel, (jax.ShapeDtypeStruct((2, MODES * 8, LANES), BF16), ja...  9.41 us
    pallas_call x1, Pallas kernels, gated_rows(): call(modal_kernel, jax.ShapeDtypeStruct((ROWS, CH), BF16), [SMEM_SPEC] *...  9.11 us
    pallas_call x2, Pallas kernels, partial_products(): call(kernel, jax.ShapeDtypeStruct((2 if counts[1] else 1, 4, rows, 2 * CO...  4.84 us
    ppermute x1, starting transfers between devices, shards(): lax.ppermute(two, ('zh', 'core'), pairs).astype(F32)  4.41 us
  transfers between devices with their start and end apart: 26, of which 11 were waited for; matrix products, arithmetic and copies ran while one was open for 0% of the time, Pallas kernels for 16%

profile of v4, /device:TPU:1, one launch (start us, length us, event | category | flops | bytes accessed | tf_op | source)
XLA Modules:
  0.0 146.0 jit_solution(12778102384831727811)
XLA Ops:
  0.0 0.8 slice.117
  0.8 4.4 %collective-permute-start = (bf16[3,8,1024]{2,1,0:T(8,128)(2,1)S(1)}, bf16[3,8,1024]{2,1,0:T(8,128)(2,1)S(1)}, u32[]{:S(2)}, u32[]{:S(2)}) collective-permute-start(bf16[3,8,1024]{2,1,0:T(8,128)(2,1)S(1)} %slice.117), channel_id=1, source_target_pairs={{0,8},{8,16},{16,24},{24,32},{32,40},{40,48},{48,56},{56,64},{64,7... | collective-permute-start | bytes 147464 | tf_op jit(solution)/shard_map/ppermute | solution.py:450
  5.2 2.7 %prepare.1 = (f32[4,2,16,8,128]{4,3,2,1,0:T(8,128)}, f32[4,2,16,8,128]{4,3,2,1,0:T(8,128)}, f32[7,3,8,128]{3,2,1,0:T(8,128)}) custom-call(s32[8192]{0:T(1024)} %ids.7, bf16[3,7,64]{2,1,0:T(8,128)(2,1)} %bitcast.85, f32[16,1024]{1,0:T(8,128)} %decay.1, f32[16,1024]{1,0:T(8,128)} %angle.1), custom_call_target="tpu_custom_call" | custom-call | flops 3000000 | bytes 1048576 | tf_op jit(solution)/shard_map/prepare/pallas_call | solution.py:104
  7.9 0.0 collective-permute-done.border
  7.9 1.7 %collective-permute-start.4 = (bf16[1024,256]{1,0:T(8,128)(2,1)}, bf16[1024,256]{1,0:T(8,128)(2,1)S(1)}, u32[]{:S(2)}, u32[]{:S(2)}) collective-permute-start(bf16[1024,256]{1,0:T(8,128)(2,1)} %param.19), channel_id=1, source_target_pairs={{0,8},{8,0},{1,9},{9,1},{2,10},{10,2},{3,11},{11,3},{4,12},{12,4},... | collective-permute-start | bytes 1572872 | tf_op jit(solution)/shard_map/ppermute | solution.py:469
  9.6 9.4 %final_states.1 = (bf16[2,128,128]{2,1,0:T(8,128)(2,1)}, f32[256,8,128]{2,1,0:T(8,128)}) custom-call(s32[8192]{0:T(1024)} %ids.7, s32[8]{0:T(128)} %picks.3, bf16[3,256,1024]{2,1,0:T(8,128)(2,1)} %feat.3, bf16[3,8,1024]{2,1,0:T(8,128)(2,1)} %copy-done.7, f32[7,3,8,128]{3,2,1,0:T(8,128)} %get-tuple-element.38.taps, ...), custom_call_target="tpu_custom_call" | custom-call | flops 8000000 | bytes 1048576 | tf_op jit(solution)/shard_map/final_states/pallas_call | solution.py:266
  19.0 6.1 %collective-permute-start.3 = (bf16[2,128,128]{2,1,0:T(8,128)(2,1)}, bf16[2,128,128]{2,1,0:T(8,128)(2,1)S(1)}, u32[]{:S(2)}, u32[]{:S(2)}) collective-permute-start(bf16[2,128,128]{2,1,0:T(8,128)(2,1)} %get-tuple-element.40), channel_id=1, source_target_pairs={{0,24},{8,32},{16,40},{24,48},{32,56},{40,64},{48,72},{56,80},{64,... | collective-permute-start | bytes 196616 | tf_op jit(solution)/shard_map/ppermute | solution.py:450
  25.2 3.9 %collective-permute-start.2 = (bf16[2,128,128]{2,1,0:T(8,128)(2,1)}, bf16[2,128,128]{2,1,0:T(8,128)(2,1)S(1)}, u32[]{:S(2)}, u32[]{:S(2)}) collective-permute-start(bf16[2,128,128]{2,1,0:T(8,128)(2,1)} %get-tuple-element.40), channel_id=1, source_target_pairs={{0,16},{8,24},{16,32},{24,40},{32,48},{40,56},{48,64},{56,72},{64,... | collective-permute-start | bytes 196616 | tf_op jit(solution)/shard_map/ppermute | solution.py:450
  29.1 1.9 %collective-permute-start.1 = (bf16[2,128,128]{2,1,0:T(8,128)(2,1)}, bf16[2,128,128]{2,1,0:T(8,128)(2,1)S(1)}, u32[]{:S(2)}, u32[]{:S(2)}) collective-permute-start(bf16[2,128,128]{2,1,0:T(8,128)(2,1)} %get-tuple-element.40), channel_id=1, source_target_pairs={{0,8},{8,16},{16,24},{24,32},{32,40},{40,48},{48,56},{56,64},{64,7... | collective-permute-start | bytes 196616 | tf_op jit(solution)/shard_map/ppermute | solution.py:450
  31.0 0.8 copy-done.8
  31.7 2.4 %featured_query.1.query = f32[256,8,128]{2,1,0:T(8,128)S(1)} custom-call(s32[8192]{0:T(1024)S(1)} %copy-done.5, bf16[3,256,1024]{2,1,0:T(8,128)(2,1)S(1)} %copy-done, bf16[3,8,1024]{2,1,0:T(8,128)(2,1)S(1)} %copy-done.8, f32[7,3,8,128]{3,2,1,0:T(8,128)S(1)} %copy-done.6), custom_call_target="tpu_custom_call" | custom-call | flops 2000000 | bytes 1048576 | tf_op jit(solution)/shard_map/featured_query/pallas_call | solution.py:297
  34.2 0.0 copy-start.12
  34.2 0.0 collective-permute-done.3
  34.2 0.0 collective-permute-done.2
  34.3 0.0 copy-start.1
  34.4 0.0 copy-start.2
  34.4 0.0 copy-start.9
  34.4 0.0 copy-start.10
  34.4 0.0 copy-start.11
  34.5 0.6 copy-done.13
  35.1 5.8 %collective-permute-start.6 = (bf16[2,128,128]{2,1,0:T(8,128)(2,1)S(1)}, bf16[2,128,128]{2,1,0:T(8,128)(2,1)S(1)}, u32[]{:S(2)}, u32[]{:S(2)}) collective-permute-start(bf16[2,128,128]{2,1,0:T(8,128)(2,1)S(1)} %fusion.9), channel_id=1, source_target_pairs={{0,40},{8,48},{16,56},{24,64},{32,72},{40,80},{48,88},{56,96},{64,... | collective-permute-start | bytes 196616 | tf_op jit(solution)/shard_map/ppermute | solution.py:450
  40.9 3.3 %collective-permute-start.5 = (bf16[2,128,128]{2,1,0:T(8,128)(2,1)S(1)}, bf16[2,128,128]{2,1,0:T(8,128)(2,1)S(1)}, u32[]{:S(2)}, u32[]{:S(2)}) collective-permute-start(bf16[2,128,128]{2,1,0:T(8,128)(2,1)S(1)} %fusion.9), channel_id=1, source_target_pairs={{0,8},{8,16},{16,24},{24,32},{32,40},{40,48},{48,56},{56,64},{64,7... | collective-permute-start | bytes 196616 | tf_op jit(solution)/shard_map/ppermute | solution.py:450
  44.2 1.3 collective-permute-done.5.near
  45.5 0.1 pad_maximum_fusion.refs_3_.refs_2_
  45.6 3.9 %collective-permute-start.10 = (bf16[2,1024,256]{2,1,0:T(8,128)(2,1)S(1)}, bf16[2,1024,256]{2,1,0:T(8,128)(2,1)S(1)}, u32[]{:S(2)}, u32[]{:S(2)}) collective-permute-start(bf16[2,1024,256]{2,1,0:T(8,128)(2,1)S(1)} %pad_maximum_fusion.refs_3_.refs_2_), channel_id=1, source_target_pairs={{0,64},{64,128},{128,192},{192,0},{1,65},{65,129},{129,193},{193,1... | collective-permute-start | bytes 3145736 | tf_op jit(solution)/shard_map/ppermute | solution.py:454
  49.5 0.6 collective-permute-start.9
  50.1 9.1 %gated_rows.1.refs_0_ = bf16[256,1024]{1,0:T(8,128)(2,1)S(1)} custom-call(s32[8192]{0:T(1024)S(1)} %copy-done.5, s32[8]{0:T(128)S(1)} %copy-done.11, bf16[2,128,128]{2,1,0:T(8,128)(2,1)S(1)} %collective-permute-done.5.near, bf16[2,128,128]{2,1,0:T(8,128)(2,1)S(1)} %collective-permute-done.6.far, f32[4,2,128,128]{3,2,1,0:T(8,128)S(1)} %bitcast.81, ...), custom_call_target="tpu_custom_call" | custom-call | flops 12000000 | bytes 1048576 | tf_op jit(solution)/shard_map/gated_rows/pallas_call | solution.py:368
  59.2 0.8 collective-permute-start.8
  60.0 2.8 %collective-permute-start.7 = (bf16[256,1024]{1,0:T(8,128)(2,1)S(1)}, bf16[256,1024]{1,0:T(8,128)(2,1)S(1)}, u32[]{:S(2)}, u32[]{:S(2)}) collective-permute-start(bf16[256,1024]{1,0:T(8,128)(2,1)S(1)} %gated_rows.1.refs_0_), channel_id=1, source_target_pairs={{0,48},{16,0},{32,16},{48,32},{1,49},{17,1},{33,17},{49,33},{2,50}... | collective-permute-start | bytes 1572872 | tf_op jit(solution)/shard_map/ppermute | solution.py:454
  62.9 6.3 %collective-permute-done.10.refs_5_.refs_4_ = bf16[2,1024,256]{2,1,0:T(8,128)(2,1)S(1)} collective-permute-done((bf16[2,1024,256]{2,1,0:T(8,128)(2,1)S(1)}, bf16[2,1024,256]{2,1,0:T(8,128)(2,1)S(1)}, u32[]{:S(2)}, u32[]{:S(2)}) %collective-permute-start.10) | collective-permute-done | bytes 1048608 | tf_op jit(solution)/shard_map/ppermute | solution.py:454
  69.2 1.8 %collective-permute-start.11 = (bf16[1024,256]{1,0:T(8,128)(2,1)S(1)}, bf16[1024,256]{1,0:T(8,128)(2,1)S(1)}, u32[]{:S(2)}, u32[]{:S(2)}) collective-permute-start(bf16[1024,256]{1,0:T(8,128)(2,1)S(1)} %slice_bitcast_fusion.3), channel_id=1, source_target_pairs={{0,64},{64,128},{128,192},{192,0},{1,65},{65,129},{129,193},{193,1... | collective-permute-start | bytes 1572872 | tf_op jit(solution)/shard_map/ppermute | solution.py:454
  71.0 1.1 collective-permute-start.12
  72.1 9.7 %collective-permute-done.8.refs_2_ = bf16[256,1024]{1,0:T(8,128)(2,1)S(1)} collective-permute-done((bf16[256,1024]{1,0:T(8,128)(2,1)S(1)}, bf16[256,1024]{1,0:T(8,128)(2,1)S(1)}, u32[]{:S(2)}, u32[]{:S(2)}) %collective-permute-start.8) | collective-permute-done | bytes 524320 | tf_op jit(solution)/shard_map/ppermute | solution.py:454
  81.8 3.7 %collective-permute-done.7.refs_1_ = bf16[256,1024]{1,0:T(8,128)(2,1)S(1)} collective-permute-done((bf16[256,1024]{1,0:T(8,128)(2,1)S(1)}, bf16[256,1024]{1,0:T(8,128)(2,1)S(1)}, u32[]{:S(2)}, u32[]{:S(2)}) %collective-permute-start.7) | collective-permute-done | bytes 524320 | tf_op jit(solution)/shard_map/ppermute | solution.py:454
  85.5 3.6 %products_near.1 = bf16[2,4,384,512]{3,2,1,0:T(8,128)(2,1)S(1)} custom-call(bf16[256,1024]{1,0:T(8,128)(2,1)S(1)} %gated_rows.1.refs_0_, bf16[256,1024]{1,0:T(8,128)(2,1)S(1)} %collective-permute-done.7.refs_1_, bf16[256,1024]{1,0:T(8,128)(2,1)S(1)} %collective-permute-done.8.refs_2_, bf16[2,1024,256]{2,1,0:T(8,128)(2,1)S(1)} %pad_maximum_fusion.refs_3_.refs_2_, ...), custom_call_target="tpu_custom_call" | custom-call | flops 1000000000 | bytes 1048576 | tf_op jit(solution)/shard_map/products_near/pallas_call | solution.py:413
  89.1 0.1 slice_bitcast_fusion
  89.2 1.8 %collective-permute-start.15 = (bf16[4,384,512]{2,1,0:T(8,128)(2,1)S(1)}, bf16[4,384,512]{2,1,0:T(8,128)(2,1)S(1)}, u32[]{:S(2)}, u32[]{:S(2)}) collective-permute-start(bf16[4,384,512]{2,1,0:T(8,128)(2,1)S(1)} %slice_bitcast_fusion), channel_id=1, source_target_pairs={{0,1},{1,0},{2,3},{3,2},{4,5},{5,4},{6,7},{7,6},{8,9},{9,8},{10,11... | collective-permute-start | bytes 4718600 | tf_op jit(solution)/shard_map/ppermute | solution.py:497
  91.0 3.0 %collective-permute-done.15 = bf16[4,384,512]{2,1,0:T(8,128)(2,1)S(1)} collective-permute-done((bf16[4,384,512]{2,1,0:T(8,128)(2,1)S(1)}, bf16[4,384,512]{2,1,0:T(8,128)(2,1)S(1)}, u32[]{:S(2)}, u32[]{:S(2)}) %collective-permute-start.15) | collective-permute-done | bytes 1572896 | tf_op jit(solution)/shard_map/ppermute | solution.py:497
  94.0 0.4 fusion
  94.5 0.1 slice_bitcast_fusion.4
  94.6 2.6 %collective-permute-start.18 = (bf16[384,512]{1,0:T(8,128)(2,1)S(1)}, bf16[384,512]{1,0:T(8,128)(2,1)S(1)}, u32[]{:S(2)}, u32[]{:S(2)}) collective-permute-start(bf16[384,512]{1,0:T(8,128)(2,1)S(1)} %get-tuple-element.67), channel_id=1, source_target_pairs={{0,6},{2,0},{4,2},{6,4},{1,7},{3,1},{5,3},{7,5},{8,14},{10,8},{12,... | collective-permute-start | bytes 1179656 | tf_op jit(solution)/shard_map/ppermute | solution.py:454
  97.1 0.0 collective-permute-start.17
  97.1 1.7 %collective-permute-start.16 = (bf16[384,512]{1,0:T(8,128)(2,1)S(1)}, bf16[384,512]{1,0:T(8,128)(2,1)S(1)}, u32[]{:S(2)}, u32[]{:S(2)}) collective-permute-start(bf16[384,512]{1,0:T(8,128)(2,1)S(1)} %get-tuple-element.69), channel_id=1, source_target_pairs={{0,4},{2,6},{4,0},{6,2},{1,5},{3,7},{5,1},{7,3},{8,12},{10,14},{12... | collective-permute-start | bytes 1179656 | tf_op jit(solution)/shard_map/ppermute | solution.py:454
  98.9 2.8 %collective-permute-start.14 = (bf16[128,1024]{1,0:T(8,128)(2,1)S(1)}, bf16[128,1024]{1,0:T(8,128)(2,1)S(1)}, u32[]{:S(2)}, u32[]{:S(2)}) collective-permute-start(bf16[128,1024]{1,0:T(8,128)(2,1)S(1)} %slice.133), channel_id=1, source_target_pairs={{0,16},{16,32},{32,48},{48,0},{1,17},{17,33},{33,49},{49,1},{2,18}... | collective-permute-start | bytes 786440 | tf_op jit(solution)/shard_map/ppermute | solution.py:454
  101.7 0.8 collective-permute-start.13
  102.6 10.2 %collective-permute-done.14.refs_1_ = bf16[128,1024]{1,0:T(8,128)(2,1)S(1)} collective-permute-done((bf16[128,1024]{1,0:T(8,128)(2,1)S(1)}, bf16[128,1024]{1,0:T(8,128)(2,1)S(1)}, u32[]{:S(2)}, u32[]{:S(2)}) %collective-permute-start.14) | collective-permute-done | bytes 262176 | tf_op jit(solution)/shard_map/ppermute | solution.py:454
  112.8 1.0 collective-permute-done.13.refs_0_
  113.8 2.1 %collective-permute-done.16 = bf16[384,512]{1,0:T(8,128)(2,1)S(1)} collective-permute-done((bf16[384,512]{1,0:T(8,128)(2,1)S(1)}, bf16[384,512]{1,0:T(8,128)(2,1)S(1)}, u32[]{:S(2)}, u32[]{:S(2)}) %collective-permute-start.16) | collective-permute-done | bytes 393248 | tf_op jit(solution)/shard_map/ppermute | solution.py:454
  115.9 1.3 products_far.1
  117.1 4.4 %collective-permute-start.20 = (bf16[4,256,512]{2,1,0:T(8,128)(2,1)S(1)}, bf16[4,256,512]{2,1,0:T(8,128)(2,1)S(1)}, u32[]{:S(2)}, u32[]{:S(2)}) collective-permute-start(bf16[4,256,512]{2,1,0:T(8,128)(2,1)S(1)} %bitcast.80), channel_id=1, source_target_pairs={{1,0},{17,16},{32,33},{48,49},{3,2},{19,18},{34,35},{50,51},{5,4},... | collective-permute-start | bytes 3145736 | tf_op jit(solution)/shard_map/ppermute | solution.py:519
  121.6 2.2 %collective-permute-done.20 = bf16[4,256,512]{2,1,0:T(8,128)(2,1)S(1)} collective-permute-done((bf16[4,256,512]{2,1,0:T(8,128)(2,1)S(1)}, bf16[4,256,512]{2,1,0:T(8,128)(2,1)S(1)}, u32[]{:S(2)}, u32[]{:S(2)}) %collective-permute-start.20) | collective-permute-done | bytes 1048608 | tf_op jit(solution)/shard_map/ppermute | solution.py:519
  123.8 0.3 add_convert_fusion
  124.1 0.1 slice_bitcast_fusion.9
  124.1 0.7 collective-permute-start.21
  124.8 0.7 collective-permute-start.23
  125.5 0.7 collective-permute-start.22
  126.2 0.2 fusion.3
  126.4 2.6 %collective-permute-start.25 = (bf16[256,512]{1,0:T(8,128)(2,1)S(1)}, bf16[256,512]{1,0:T(8,128)(2,1)S(1)}, u32[]{:S(2)}, u32[]{:S(2)}) collective-permute-start(bf16[256,512]{1,0:T(8,128)(2,1)S(1)} %slice.164), channel_id=1, source_target_pairs={{0,16},{1,48},{16,32},{17,0},{32,49},{33,17},{48,1},{49,33},{2,18}... | collective-permute-start | bytes 786440 | tf_op jit(solution)/shard_map/ppermute | solution.py:505
  129.1 0.1 fusion.6
  129.2 1.3 collective-permute-start.24
  130.5 10.2 %collective-permute-start.19 = (bf16[128,512]{1,0:T(8,128)(2,1)S(1)}, bf16[128,512]{1,0:T(8,128)(2,1)S(1)}, u32[]{:S(2)}, u32[]{:S(2)}) collective-permute-start(bf16[128,512]{1,0:T(8,128)(2,1)S(1)} %slice.159.near_own), channel_id=1, source_target_pairs={{0,1},{1,0},{2,3},{3,2},{4,5},{5,4},{6,7},{7,6},{8,9},{9,8},{10,11... | collective-permute-start | bytes 393224 | tf_op jit(solution)/shard_map/ppermute | solution.py:527
  140.8 1.0 collective-permute-done.19.near_other
  141.7 3.5 %collective-permute-done.24.far = bf16[256,512]{1,0:T(8,128)(2,1)S(1)} collective-permute-done((bf16[256,512]{1,0:T(8,128)(2,1)S(1)}, bf16[256,512]{1,0:T(8,128)(2,1)S(1)}, u32[]{:S(2)}, u32[]{:S(2)}) %collective-permute-start.24) | collective-permute-done | bytes 262176 | tf_op jit(solution)/shard_map/ppermute | solution.py:530
  145.2 0.8 assemble.1
  (44 shorter events, 0.3 us)
Async XLA Ops:
  0.8 7.1 %collective-permute-start = (bf16[3,8,1024]{2,1,0:T(8,128)(2,1)S(1)}, bf16[3,8,1024]{2,1,0:T(8,128)(2,1)S(1)}, u32[]{:S(2)}, u32[]{:S(2)}) collective-permute-start(bf16[3,8,1024]{2,1,0:T(8,128)(2,1)S(1)} %slice.117), channel_id=1, source_target_pairs={{0,8},{8,16},{16,24},{24,32},{32,40},{40,48},{48,56},{56,64},{64,7... | collective-permute-start | bytes 147464 | tf_op jit(solution)/shard_map/ppermute | solution.py:450
  7.9 1.7 %copy-start.7 = (bf16[3,8,1024]{2,1,0:T(8,128)(2,1)}, bf16[3,8,1024]{2,1,0:T(8,128)(2,1)S(1)}, u32[]{:S(2)}) copy-start(bf16[3,8,1024]{2,1,0:T(8,128)(2,1)S(1)} %collective-permute-done.border) | copy-start | bytes 147460
  7.9 26.3 %collective-permute-start.4 = (bf16[1024,256]{1,0:T(8,128)(2,1)}, bf16[1024,256]{1,0:T(8,128)(2,1)S(1)}, u32[]{:S(2)}, u32[]{:S(2)}) collective-permute-start(bf16[1024,256]{1,0:T(8,128)(2,1)} %param.19), channel_id=1, source_target_pairs={{0,8},{8,0},{1,9},{9,1},{2,10},{10,2},{3,11},{11,3},{4,12},{12,4},... | collective-permute-start | bytes 1572872 | tf_op jit(solution)/shard_map/ppermute | solution.py:469
  9.6 21.3 %copy-start = (bf16[3,256,1024]{2,1,0:T(8,128)(2,1)S(1)}, bf16[3,256,1024]{2,1,0:T(8,128)(2,1)}, u32[]{:S(2)}) copy-start(bf16[3,256,1024]{2,1,0:T(8,128)(2,1)} %feat.3) | copy-start | bytes 4718596
  9.6 21.3 %copy-start.5 = (s32[8192]{0:T(1024)S(1)}, s32[8192]{0:T(1024)}, u32[]{:S(2)}) copy-start(s32[8192]{0:T(1024)} %ids.7) | copy-start | bytes 98308
  9.6 21.4 %copy-start.6 = (f32[7,3,8,128]{3,2,1,0:T(8,128)S(1)}, f32[7,3,8,128]{3,2,1,0:T(8,128)}, u32[]{:S(2)}) copy-start(f32[7,3,8,128]{3,2,1,0:T(8,128)} %get-tuple-element.38.taps) | copy-start | bytes 258052
  19.0 15.3 %copy-start.3 = (f32[4,2,16,8,128]{4,3,2,1,0:T(8,128)S(1)}, f32[4,2,16,8,128]{4,3,2,1,0:T(8,128)}, u32[]{:S(2)}) copy-start(f32[4,2,16,8,128]{4,3,2,1,0:T(8,128)} %get-tuple-element.41) | copy-start | bytes 1572868
  19.0 15.2 %collective-permute-start.3 = (bf16[2,128,128]{2,1,0:T(8,128)(2,1)}, bf16[2,128,128]{2,1,0:T(8,128)(2,1)S(1)}, u32[]{:S(2)}, u32[]{:S(2)}) collective-permute-start(bf16[2,128,128]{2,1,0:T(8,128)(2,1)} %get-tuple-element.40), channel_id=1, source_target_pairs={{0,24},{8,32},{16,40},{24,48},{32,56},{40,64},{48,72},{56,80},{64,... | collective-permute-start | bytes 196616 | tf_op jit(solution)/shard_map/ppermute | solution.py:450
  25.2 9.1 %collective-permute-start.2 = (bf16[2,128,128]{2,1,0:T(8,128)(2,1)}, bf16[2,128,128]{2,1,0:T(8,128)(2,1)S(1)}, u32[]{:S(2)}, u32[]{:S(2)}) collective-permute-start(bf16[2,128,128]{2,1,0:T(8,128)(2,1)} %get-tuple-element.40), channel_id=1, source_target_pairs={{0,16},{8,24},{16,32},{24,40},{32,48},{40,56},{48,64},{56,72},{64,... | collective-permute-start | bytes 196616 | tf_op jit(solution)/shard_map/ppermute | solution.py:450
  29.1 5.2 %collective-permute-start.1 = (bf16[2,128,128]{2,1,0:T(8,128)(2,1)}, bf16[2,128,128]{2,1,0:T(8,128)(2,1)S(1)}, u32[]{:S(2)}, u32[]{:S(2)}) collective-permute-start(bf16[2,128,128]{2,1,0:T(8,128)(2,1)} %get-tuple-element.40), channel_id=1, source_target_pairs={{0,8},{8,16},{16,24},{24,32},{32,40},{40,48},{48,56},{56,64},{64,7... | collective-permute-start | bytes 196616 | tf_op jit(solution)/shard_map/ppermute | solution.py:450
  30.9 0.8 copy-start.8
  34.2 0.8 copy-start.13
  34.2 11.3 %copy-start.12 = (bf16[1024,256]{1,0:T(8,128)(2,1)S(1)}, bf16[1024,256]{1,0:T(8,128)(2,1)}, u32[]{:S(2)}) copy-start(bf16[1024,256]{1,0:T(8,128)(2,1)} %param.19) | copy-start | bytes 1572868
  34.3 15.7 %copy-start.1 = (f32[8,2,16,1024]{3,2,1,0:T(8,128)S(1)}, f32[8,2,16,1024]{3,2,1,0:T(8,128)}, u32[]{:S(2)}) copy-start(f32[8,2,16,1024]{3,2,1,0:T(8,128)} %entry.3) | copy-start | bytes 3145732
  34.4 15.7 %copy-start.2 = (f32[4,2,16,8,128]{4,3,2,1,0:T(8,128)S(1)}, f32[4,2,16,8,128]{4,3,2,1,0:T(8,128)}, u32[]{:S(2)}) copy-start(f32[4,2,16,8,128]{4,3,2,1,0:T(8,128)} %get-tuple-element.39.pole) | copy-start | bytes 1572868
  34.4 15.7 %copy-start.4 = (f32[256,8,128]{2,1,0:T(8,128)S(1)}, f32[256,8,128]{2,1,0:T(8,128)}, u32[]{:S(2)}) copy-start(f32[256,8,128]{2,1,0:T(8,128)} %get-tuple-element.50.product) | copy-start | bytes 3145732
  34.4 15.7 %copy-start.9 = (f32[2,16,1024]{2,1,0:T(8,128)S(1)}, f32[2,16,1024]{2,1,0:T(8,128)}, u32[]{:S(2)}) copy-start(f32[2,16,1024]{2,1,0:T(8,128)} %res.1) | copy-start | bytes 393220
  34.4 15.7 %copy-start.10 = (f32[1024]{0:T(1024)S(1)}, f32[1024]{0:T(1024)}, u32[]{:S(2)}) copy-start(f32[1024]{0:T(1024)} %param.15) | copy-start | bytes 12292
  34.4 15.7 %copy-start.11 = (s32[8]{0:T(128)S(1)}, s32[8]{0:T(128)}, u32[]{:S(2)}) copy-start(s32[8]{0:T(128)} %picks.3) | copy-start | bytes 100
  35.1 9.2 %collective-permute-start.6 = (bf16[2,128,128]{2,1,0:T(8,128)(2,1)S(1)}, bf16[2,128,128]{2,1,0:T(8,128)(2,1)S(1)}, u32[]{:S(2)}, u32[]{:S(2)}) collective-permute-start(bf16[2,128,128]{2,1,0:T(8,128)(2,1)S(1)} %fusion.9), channel_id=1, source_target_pairs={{0,40},{8,48},{16,56},{24,64},{32,72},{40,80},{48,88},{56,96},{64,... | collective-permute-start | bytes 196616 | tf_op jit(solution)/shard_map/ppermute | solution.py:450
  40.9 4.6 %collective-permute-start.5 = (bf16[2,128,128]{2,1,0:T(8,128)(2,1)S(1)}, bf16[2,128,128]{2,1,0:T(8,128)(2,1)S(1)}, u32[]{:S(2)}, u32[]{:S(2)}) collective-permute-start(bf16[2,128,128]{2,1,0:T(8,128)(2,1)S(1)} %fusion.9), channel_id=1, source_target_pairs={{0,8},{8,16},{16,24},{24,32},{32,40},{40,48},{48,56},{56,64},{64,7... | collective-permute-start | bytes 196616 | tf_op jit(solution)/shard_map/ppermute | solution.py:450
  45.6 23.5 %collective-permute-start.10 = (bf16[2,1024,256]{2,1,0:T(8,128)(2,1)S(1)}, bf16[2,1024,256]{2,1,0:T(8,128)(2,1)S(1)}, u32[]{:S(2)}, u32[]{:S(2)}) collective-permute-start(bf16[2,1024,256]{2,1,0:T(8,128)(2,1)S(1)} %pad_maximum_fusion.refs_3_.refs_2_), channel_id=1, source_target_pairs={{0,64},{64,128},{128,192},{192,0},{1,65},{65,129},{129,193},{193,1... | collective-permute-start | bytes 3145736 | tf_op jit(solution)/shard_map/ppermute | solution.py:454
  49.5 21.5 %collective-permute-start.9 = (bf16[2,1024,256]{2,1,0:T(8,128)(2,1)S(1)}, bf16[2,1024,256]{2,1,0:T(8,128)(2,1)S(1)}, u32[]{:S(2)}, u32[]{:S(2)}) collective-permute-start(bf16[2,1024,256]{2,1,0:T(8,128)(2,1)S(1)} %pad_maximum_fusion.refs_3_.refs_2_), channel_id=1, source_target_pairs={{0,192},{64,0},{128,64},{192,128},{1,193},{65,1},{129,65},{193,129... | collective-permute-start | bytes 3145736 | tf_op jit(solution)/shard_map/ppermute | solution.py:454
  59.2 22.6 %collective-permute-start.8 = (bf16[256,1024]{1,0:T(8,128)(2,1)S(1)}, bf16[256,1024]{1,0:T(8,128)(2,1)S(1)}, u32[]{:S(2)}, u32[]{:S(2)}) collective-permute-start(bf16[256,1024]{1,0:T(8,128)(2,1)S(1)} %gated_rows.1.refs_0_), channel_id=1, source_target_pairs={{0,16},{16,32},{32,48},{48,0},{1,17},{17,33},{33,49},{49,1},{2,18}... | collective-permute-start | bytes 1572872 | tf_op jit(solution)/shard_map/ppermute | solution.py:454
  60.0 25.4 %collective-permute-start.7 = (bf16[256,1024]{1,0:T(8,128)(2,1)S(1)}, bf16[256,1024]{1,0:T(8,128)(2,1)S(1)}, u32[]{:S(2)}, u32[]{:S(2)}) collective-permute-start(bf16[256,1024]{1,0:T(8,128)(2,1)S(1)} %gated_rows.1.refs_0_), channel_id=1, source_target_pairs={{0,48},{16,0},{32,16},{48,32},{1,49},{17,1},{33,17},{49,33},{2,50}... | collective-permute-start | bytes 1572872 | tf_op jit(solution)/shard_map/ppermute | solution.py:454
  69.2 16.3 %collective-permute-start.11 = (bf16[1024,256]{1,0:T(8,128)(2,1)S(1)}, bf16[1024,256]{1,0:T(8,128)(2,1)S(1)}, u32[]{:S(2)}, u32[]{:S(2)}) collective-permute-start(bf16[1024,256]{1,0:T(8,128)(2,1)S(1)} %slice_bitcast_fusion.3), channel_id=1, source_target_pairs={{0,64},{64,128},{128,192},{192,0},{1,65},{65,129},{129,193},{193,1... | collective-permute-start | bytes 1572872 | tf_op jit(solution)/shard_map/ppermute | solution.py:454
  71.0 14.5 %collective-permute-start.12 = (bf16[1024,256]{1,0:T(8,128)(2,1)S(1)}, bf16[1024,256]{1,0:T(8,128)(2,1)S(1)}, u32[]{:S(2)}, u32[]{:S(2)}) collective-permute-start(bf16[1024,256]{1,0:T(8,128)(2,1)S(1)} %slice_bitcast_fusion.2), channel_id=1, source_target_pairs={{0,192},{64,0},{128,64},{192,128},{1,193},{65,1},{129,65},{193,129... | collective-permute-start | bytes 1572872 | tf_op jit(solution)/shard_map/ppermute | solution.py:454
  89.2 4.9 %collective-permute-start.15 = (bf16[4,384,512]{2,1,0:T(8,128)(2,1)S(1)}, bf16[4,384,512]{2,1,0:T(8,128)(2,1)S(1)}, u32[]{:S(2)}, u32[]{:S(2)}) collective-permute-start(bf16[4,384,512]{2,1,0:T(8,128)(2,1)S(1)} %slice_bitcast_fusion), channel_id=1, source_target_pairs={{0,1},{1,0},{2,3},{3,2},{4,5},{5,4},{6,7},{7,6},{8,9},{9,8},{10,11... | collective-permute-start | bytes 4718600 | tf_op jit(solution)/shard_map/ppermute | solution.py:497
  94.6 19.2 %collective-permute-start.18 = (bf16[384,512]{1,0:T(8,128)(2,1)S(1)}, bf16[384,512]{1,0:T(8,128)(2,1)S(1)}, u32[]{:S(2)}, u32[]{:S(2)}) collective-permute-start(bf16[384,512]{1,0:T(8,128)(2,1)S(1)} %get-tuple-element.67), channel_id=1, source_target_pairs={{0,6},{2,0},{4,2},{6,4},{1,7},{3,1},{5,3},{7,5},{8,14},{10,8},{12,... | collective-permute-start | bytes 1179656 | tf_op jit(solution)/shard_map/ppermute | solution.py:454
  97.1 16.7 %collective-permute-start.17 = (bf16[384,512]{1,0:T(8,128)(2,1)S(1)}, bf16[384,512]{1,0:T(8,128)(2,1)S(1)}, u32[]{:S(2)}, u32[]{:S(2)}) collective-permute-start(bf16[384,512]{1,0:T(8,128)(2,1)S(1)} %get-tuple-element.68), channel_id=1, source_target_pairs={{0,2},{2,4},{4,6},{6,0},{1,3},{3,5},{5,7},{7,1},{8,10},{10,12},{12... | collective-permute-start | bytes 1179656 | tf_op jit(solution)/shard_map/ppermute | solution.py:454
  97.1 18.7 %collective-permute-start.16 = (bf16[384,512]{1,0:T(8,128)(2,1)S(1)}, bf16[384,512]{1,0:T(8,128)(2,1)S(1)}, u32[]{:S(2)}, u32[]{:S(2)}) collective-permute-start(bf16[384,512]{1,0:T(8,128)(2,1)S(1)} %get-tuple-element.69), channel_id=1, source_target_pairs={{0,4},{2,6},{4,0},{6,2},{1,5},{3,7},{5,1},{7,3},{8,12},{10,14},{12... | collective-permute-start | bytes 1179656 | tf_op jit(solution)/shard_map/ppermute | solution.py:454
  98.9 13.9 %collective-permute-start.14 = (bf16[128,1024]{1,0:T(8,128)(2,1)S(1)}, bf16[128,1024]{1,0:T(8,128)(2,1)S(1)}, u32[]{:S(2)}, u32[]{:S(2)}) collective-permute-start(bf16[128,1024]{1,0:T(8,128)(2,1)S(1)} %slice.133), channel_id=1, source_target_pairs={{0,16},{16,32},{32,48},{48,0},{1,17},{17,33},{33,49},{49,1},{2,18}... | collective-permute-start | bytes 786440 | tf_op jit(solution)/shard_map/ppermute | solution.py:454
  101.7 12.1 %collective-permute-start.13 = (bf16[128,1024]{1,0:T(8,128)(2,1)S(1)}, bf16[128,1024]{1,0:T(8,128)(2,1)S(1)}, u32[]{:S(2)}, u32[]{:S(2)}) collective-permute-start(bf16[128,1024]{1,0:T(8,128)(2,1)S(1)} %slice.132), channel_id=1, source_target_pairs={{0,48},{16,0},{32,16},{48,32},{1,49},{17,1},{33,17},{49,33},{2,50}... | collective-permute-start | bytes 786440 | tf_op jit(solution)/shard_map/ppermute | solution.py:454
  117.1 6.6 %collective-permute-start.20 = (bf16[4,256,512]{2,1,0:T(8,128)(2,1)S(1)}, bf16[4,256,512]{2,1,0:T(8,128)(2,1)S(1)}, u32[]{:S(2)}, u32[]{:S(2)}) collective-permute-start(bf16[4,256,512]{2,1,0:T(8,128)(2,1)S(1)} %bitcast.80), channel_id=1, source_target_pairs={{1,0},{17,16},{32,33},{48,49},{3,2},{19,18},{34,35},{50,51},{5,4},... | collective-permute-start | bytes 3145736 | tf_op jit(solution)/shard_map/ppermute | solution.py:519
  124.1 4.9 %collective-permute-start.21 = (bf16[256,512]{1,0:T(8,128)(2,1)S(1)}, bf16[256,512]{1,0:T(8,128)(2,1)S(1)}, u32[]{:S(2)}, u32[]{:S(2)}) collective-permute-start(bf16[256,512]{1,0:T(8,128)(2,1)S(1)} %get-tuple-element.70), channel_id=1, source_target_pairs={{0,4},{2,6},{4,0},{6,2},{16,20},{18,22},{20,16},{22,18},{33,37},{3... | collective-permute-start | bytes 786440 | tf_op jit(solution)/shard_map/ppermute | solution.py:524
  124.8 4.2 %collective-permute-start.23 = (bf16[256,512]{1,0:T(8,128)(2,1)S(1)}, bf16[256,512]{1,0:T(8,128)(2,1)S(1)}, u32[]{:S(2)}, u32[]{:S(2)}) collective-permute-start(bf16[256,512]{1,0:T(8,128)(2,1)S(1)} %get-tuple-element.71), channel_id=1, source_target_pairs={{0,6},{2,0},{4,2},{6,4},{16,22},{18,16},{20,18},{22,20},{33,39},{3... | collective-permute-start | bytes 786440 | tf_op jit(solution)/shard_map/ppermute | solution.py:524
  125.5 3.6 %collective-permute-start.22 = (bf16[256,512]{1,0:T(8,128)(2,1)S(1)}, bf16[256,512]{1,0:T(8,128)(2,1)S(1)}, u32[]{:S(2)}, u32[]{:S(2)}) collective-permute-start(bf16[256,512]{1,0:T(8,128)(2,1)S(1)} %get-tuple-element.72), channel_id=1, source_target_pairs={{0,2},{2,4},{4,6},{6,0},{16,18},{18,20},{20,22},{22,16},{33,35},{3... | collective-permute-start | bytes 786440 | tf_op jit(solution)/shard_map/ppermute | solution.py:524
  126.4 15.3 %collective-permute-start.25 = (bf16[256,512]{1,0:T(8,128)(2,1)S(1)}, bf16[256,512]{1,0:T(8,128)(2,1)S(1)}, u32[]{:S(2)}, u32[]{:S(2)}) collective-permute-start(bf16[256,512]{1,0:T(8,128)(2,1)S(1)} %slice.164), channel_id=1, source_target_pairs={{0,16},{1,48},{16,32},{17,0},{32,49},{33,17},{48,1},{49,33},{2,18}... | collective-permute-start | bytes 786440 | tf_op jit(solution)/shard_map/ppermute | solution.py:505
  129.2 16.0 %collective-permute-start.24 = (bf16[256,512]{1,0:T(8,128)(2,1)S(1)}, bf16[256,512]{1,0:T(8,128)(2,1)S(1)}, u32[]{:S(2)}, u32[]{:S(2)}) collective-permute-start(bf16[256,512]{1,0:T(8,128)(2,1)S(1)} %fusion.6), channel_id=1, source_target_pairs={{0,32},{16,48},{33,1},{49,17},{2,34},{18,50},{35,3},{51,19},{4,36}... | collective-permute-start | bytes 786440 | tf_op jit(solution)/shard_map/ppermute | solution.py:530
  130.5 11.2 %collective-permute-start.19 = (bf16[128,512]{1,0:T(8,128)(2,1)S(1)}, bf16[128,512]{1,0:T(8,128)(2,1)S(1)}, u32[]{:S(2)}, u32[]{:S(2)}) collective-permute-start(bf16[128,512]{1,0:T(8,128)(2,1)S(1)} %slice.159.near_own), channel_id=1, source_target_pairs={{0,1},{1,0},{2,3},{3,2},{4,5},{5,4},{6,7},{7,6},{8,9},{9,8},{10,11... | collective-permute-start | bytes 393224 | tf_op jit(solution)/shard_map/ppermute | solution.py:527

commit v5 on v4

--- a/solution.py
+++ b/solution.py
@@ -18,6 +18,7 @@
 GAP = 9
 BLOCK = GAP * TILES
 COLS = 256
+SPARE = 16
 WIDE = (8, LANES)
 MIB = 1024 * 1024
 SMEM_SPEC = pl.BlockSpec(memory_space=pltpu.SMEM)
@@ -109,7 +110,7 @@
             jax.ShapeDtypeStruct((TAPS, 3) + WIDE, F32),
         ),
         [SMEM_SPEC] + [VMEM_SPEC] * 3,
-        [pltpu.VMEM((2 * BLOCK, LANES), F32)],
+        [pltpu.VMEM((2 * BLOCK + SPARE, LANES), F32)],
         58,
         "prepare",
         3_000_000,
@@ -271,10 +272,10 @@
         ),
         [SMEM_SPEC] * 2 + [VMEM_SPEC] * 5,
         [
-            pltpu.VMEM((2, ROWS // 8 * BLOCK, LANES), F32),
-            pltpu.VMEM((3 * BLOCK, LANES), F32),
+            pltpu.VMEM((2, ROWS // 8 * BLOCK + SPARE, LANES), F32),
+            pltpu.VMEM((3 * BLOCK + SPARE, LANES), F32),
             pltpu.VMEM((2, 8) + WIDE, F32),
-            pltpu.VMEM((BLOCK, LANES), F32),
+            pltpu.VMEM((BLOCK + SPARE, LANES), F32),
         ],
         58,
         "final_states",
@@ -298,7 +299,7 @@
         query_kernel,
         jax.ShapeDtypeStruct((ROWS,) + WIDE, F32),
         [SMEM_SPEC] + [VMEM_SPEC] * 3,
-        [pltpu.VMEM((1, ROWS // 8 * BLOCK, LANES), F32), pltpu.VMEM((BLOCK, LANES), F32)],
+        [pltpu.VMEM((1, ROWS // 8 * BLOCK + SPARE, LANES), F32), pltpu.VMEM((BLOCK + SPARE, LANES), F32)],
         16,
         "featured_query",
         2_000_000,
@@ -374,8 +375,8 @@
             pltpu.VMEM((2, MODES) + WIDE, F32),
             pltpu.VMEM((2, 8) + WIDE, F32),
             pltpu.VMEM((ROWS,) + WIDE, F32),
-            pltpu.VMEM((ROWS // 8 * BLOCK, LANES), F32),
-            pltpu.VMEM((BLOCK, LANES), F32),
+            pltpu.VMEM((ROWS // 8 * BLOCK + SPARE, LANES), F32),
+            pltpu.VMEM((BLOCK + SPARE, LANES), F32),
         ],
         20,
         "gated_rows",

time: 148 us -> 149 us (level)
  no operation moved by 1% of the time
where the time goes in v5:
time: 149 us; the launch traced here: 148 us
  starting transfers between devices  69.4 us (47%)
  waiting for transfers between devices  44.4 us (30%)
  Pallas kernels  29.5 us (20%)
  local copies, waits for them, and re-layouts  2.59 us (2%)
    ppermute x11, waiting for transfers between devices, turn(): return lax.ppermute(value, axis, [(i, (i + steps) % 4) for i in range(4)])  31.9 us
    ppermute x6, starting transfers between devices, shift_records(): lax.ppermute(value, ('y', 'zh', 'zl'), [(i, i + steps) for i in range(32...  25.5 us
    ppermute x11, starting transfers between devices, turn(): return lax.ppermute(value, axis, [(i, (i + steps) % 4) for i in range(4)])  19.1 us
    ppermute x1, starting transfers between devices, shards(): near_other = lax.ppermute(near_own, 'core', [(0, 1), (1, 0)])  10.2 us
    pallas_call x1, Pallas kernels, final_states(): call(final_kernel, (jax.ShapeDtypeStruct((2, MODES * 8, LANES), BF16), ja...  9.52 us
    pallas_call x1, Pallas kernels, gated_rows(): call(modal_kernel, jax.ShapeDtypeStruct((ROWS, CH), BF16), [SMEM_SPEC] *...  9.11 us
    ppermute x1, waiting for transfers between devices, shards(): far_sums = lax.ppermute(two, ('zh', 'core'), pairs)  4.91 us
    pallas_call x2, Pallas kernels, partial_products(): call(kernel, jax.ShapeDtypeStruct((2 if counts[1] else 1, 4, rows, 2 * CO...  4.84 us
  transfers between devices with their start and end apart: 26, of which 11 were waited for; matrix products, arithmetic and copies ran while one was open for 0% of the time, Pallas kernels for 16%

profile of v5, /device:TPU:1, one launch (start us, length us, event | category | flops | bytes accessed | tf_op | source)
XLA Modules:
  0.0 147.6 jit_solution(14372739226425277345)
XLA Ops:
  0.0 0.8 slice.117
  0.8 4.4 %collective-permute-start = (bf16[3,8,1024]{2,1,0:T(8,128)(2,1)S(1)}, bf16[3,8,1024]{2,1,0:T(8,128)(2,1)S(1)}, u32[]{:S(2)}, u32[]{:S(2)}) collective-permute-start(bf16[3,8,1024]{2,1,0:T(8,128)(2,1)S(1)} %slice.117), channel_id=1, source_target_pairs={{0,8},{8,16},{16,24},{24,32},{32,40},{40,48},{48,56},{56,64},{64,7... | collective-permute-start | bytes 147464 | tf_op jit(solution)/shard_map/ppermute | solution.py:451
  5.2 2.7 %prepare.1 = (f32[4,2,16,8,128]{4,3,2,1,0:T(8,128)}, f32[4,2,16,8,128]{4,3,2,1,0:T(8,128)}, f32[7,3,8,128]{3,2,1,0:T(8,128)}) custom-call(s32[8192]{0:T(1024)} %ids.7, bf16[3,7,64]{2,1,0:T(8,128)(2,1)} %bitcast.85, f32[16,1024]{1,0:T(8,128)} %decay.1, f32[16,1024]{1,0:T(8,128)} %angle.1), custom_call_target="tpu_custom_call" | custom-call | flops 3000000 | bytes 1048576 | tf_op jit(solution)/shard_map/prepare/pallas_call | solution.py:105
  7.9 0.0 collective-permute-done.border
  7.9 1.7 %collective-permute-start.4 = (bf16[1024,256]{1,0:T(8,128)(2,1)}, bf16[1024,256]{1,0:T(8,128)(2,1)S(1)}, u32[]{:S(2)}, u32[]{:S(2)}) collective-permute-start(bf16[1024,256]{1,0:T(8,128)(2,1)} %param.19), channel_id=1, source_target_pairs={{0,8},{8,0},{1,9},{9,1},{2,10},{10,2},{3,11},{11,3},{4,12},{12,4},... | collective-permute-start | bytes 1572872 | tf_op jit(solution)/shard_map/ppermute | solution.py:470
  9.6 9.5 %final_states.1 = (bf16[2,128,128]{2,1,0:T(8,128)(2,1)}, f32[256,8,128]{2,1,0:T(8,128)}) custom-call(s32[8192]{0:T(1024)} %ids.7, s32[8]{0:T(128)} %picks.3, bf16[3,256,1024]{2,1,0:T(8,128)(2,1)} %feat.3, bf16[3,8,1024]{2,1,0:T(8,128)(2,1)} %copy-done.7, f32[7,3,8,128]{3,2,1,0:T(8,128)} %get-tuple-element.38.taps, ...), custom_call_target="tpu_custom_call" | custom-call | flops 8000000 | bytes 1048576 | tf_op jit(solution)/shard_map/final_states/pallas_call | solution.py:267
  19.1 6.2 %collective-permute-start.3 = (bf16[2,128,128]{2,1,0:T(8,128)(2,1)}, bf16[2,128,128]{2,1,0:T(8,128)(2,1)S(1)}, u32[]{:S(2)}, u32[]{:S(2)}) collective-permute-start(bf16[2,128,128]{2,1,0:T(8,128)(2,1)} %get-tuple-element.40), channel_id=1, source_target_pairs={{0,24},{8,32},{16,40},{24,48},{32,56},{40,64},{48,72},{56,80},{64,... | collective-permute-start | bytes 196616 | tf_op jit(solution)/shard_map/ppermute | solution.py:451
  25.3 4.3 %collective-permute-start.2 = (bf16[2,128,128]{2,1,0:T(8,128)(2,1)}, bf16[2,128,128]{2,1,0:T(8,128)(2,1)S(1)}, u32[]{:S(2)}, u32[]{:S(2)}) collective-permute-start(bf16[2,128,128]{2,1,0:T(8,128)(2,1)} %get-tuple-element.40), channel_id=1, source_target_pairs={{0,16},{8,24},{16,32},{24,40},{32,48},{40,56},{48,64},{56,72},{64,... | collective-permute-start | bytes 196616 | tf_op jit(solution)/shard_map/ppermute | solution.py:451
  29.6 1.9 %collective-permute-start.1 = (bf16[2,128,128]{2,1,0:T(8,128)(2,1)}, bf16[2,128,128]{2,1,0:T(8,128)(2,1)S(1)}, u32[]{:S(2)}, u32[]{:S(2)}) collective-permute-start(bf16[2,128,128]{2,1,0:T(8,128)(2,1)} %get-tuple-element.40), channel_id=1, source_target_pairs={{0,8},{8,16},{16,24},{24,32},{32,40},{40,48},{48,56},{56,64},{64,7... | collective-permute-start | bytes 196616 | tf_op jit(solution)/shard_map/ppermute | solution.py:451
  31.5 0.8 copy-done.8
  32.3 2.4 %featured_query.1.query = f32[256,8,128]{2,1,0:T(8,128)S(1)} custom-call(s32[8192]{0:T(1024)S(1)} %copy-done.5, bf16[3,256,1024]{2,1,0:T(8,128)(2,1)S(1)} %copy-done, bf16[3,8,1024]{2,1,0:T(8,128)(2,1)S(1)} %copy-done.8, f32[7,3,8,128]{3,2,1,0:T(8,128)S(1)} %copy-done.6), custom_call_target="tpu_custom_call" | custom-call | flops 2000000 | bytes 1048576 | tf_op jit(solution)/shard_map/featured_query/pallas_call | solution.py:298
  34.7 0.0 copy-start.12
  34.7 0.0 collective-permute-done.2
  34.7 0.0 collective-permute-done.1
  34.9 0.0 copy-start.1
  34.9 0.0 copy-start.2
  34.9 0.0 copy-start.9
  34.9 0.0 copy-start.10
  34.9 0.0 copy-start.11
  35.0 0.6 copy-done.13
  35.6 5.9 %collective-permute-start.6 = (bf16[2,128,128]{2,1,0:T(8,128)(2,1)S(1)}, bf16[2,128,128]{2,1,0:T(8,128)(2,1)S(1)}, u32[]{:S(2)}, u32[]{:S(2)}) collective-permute-start(bf16[2,128,128]{2,1,0:T(8,128)(2,1)S(1)} %fusion.9), channel_id=1, source_target_pairs={{0,40},{8,48},{16,56},{24,64},{32,72},{40,80},{48,88},{56,96},{64,... | collective-permute-start | bytes 196616 | tf_op jit(solution)/shard_map/ppermute | solution.py:451
  41.5 3.0 %collective-permute-start.5 = (bf16[2,128,128]{2,1,0:T(8,128)(2,1)S(1)}, bf16[2,128,128]{2,1,0:T(8,128)(2,1)S(1)}, u32[]{:S(2)}, u32[]{:S(2)}) collective-permute-start(bf16[2,128,128]{2,1,0:T(8,128)(2,1)S(1)} %fusion.9), channel_id=1, source_target_pairs={{0,8},{8,16},{16,24},{24,32},{32,40},{40,48},{48,56},{56,64},{64,7... | collective-permute-start | bytes 196616 | tf_op jit(solution)/shard_map/ppermute | solution.py:451
  44.4 1.3 collective-permute-done.5.near
  45.7 0.1 pad_maximum_fusion.refs_3_.refs_2_
  45.9 3.8 %collective-permute-start.10 = (bf16[2,1024,256]{2,1,0:T(8,128)(2,1)S(1)}, bf16[2,1024,256]{2,1,0:T(8,128)(2,1)S(1)}, u32[]{:S(2)}, u32[]{:S(2)}) collective-permute-start(bf16[2,1024,256]{2,1,0:T(8,128)(2,1)S(1)} %pad_maximum_fusion.refs_3_.refs_2_), channel_id=1, source_target_pairs={{0,64},{64,128},{128,192},{192,0},{1,65},{65,129},{129,193},{193,1... | collective-permute-start | bytes 3145736 | tf_op jit(solution)/shard_map/ppermute | solution.py:455
  49.6 0.6 collective-permute-start.9
  50.2 9.1 %gated_rows.1.refs_0_ = bf16[256,1024]{1,0:T(8,128)(2,1)S(1)} custom-call(s32[8192]{0:T(1024)S(1)} %copy-done.5, s32[8]{0:T(128)S(1)} %copy-done.11, bf16[2,128,128]{2,1,0:T(8,128)(2,1)S(1)} %collective-permute-done.5.near, bf16[2,128,128]{2,1,0:T(8,128)(2,1)S(1)} %collective-permute-done.6.far, f32[4,2,128,128]{3,2,1,0:T(8,128)S(1)} %bitcast.81, ...), custom_call_target="tpu_custom_call" | custom-call | flops 12000000 | bytes 1048576 | tf_op jit(solution)/shard_map/gated_rows/pallas_call | solution.py:369
  59.3 0.5 collective-permute-start.8
  59.8 3.2 %collective-permute-start.7 = (bf16[256,1024]{1,0:T(8,128)(2,1)S(1)}, bf16[256,1024]{1,0:T(8,128)(2,1)S(1)}, u32[]{:S(2)}, u32[]{:S(2)}) collective-permute-start(bf16[256,1024]{1,0:T(8,128)(2,1)S(1)} %gated_rows.1.refs_0_), channel_id=1, source_target_pairs={{0,48},{16,0},{32,16},{48,32},{1,49},{17,1},{33,17},{49,33},{2,50}... | collective-permute-start | bytes 1572872 | tf_op jit(solution)/shard_map/ppermute | solution.py:455
  63.0 6.3 %collective-permute-done.10.refs_5_.refs_4_ = bf16[2,1024,256]{2,1,0:T(8,128)(2,1)S(1)} collective-permute-done((bf16[2,1024,256]{2,1,0:T(8,128)(2,1)S(1)}, bf16[2,1024,256]{2,1,0:T(8,128)(2,1)S(1)}, u32[]{:S(2)}, u32[]{:S(2)}) %collective-permute-start.10) | collective-permute-done | bytes 1048608 | tf_op jit(solution)/shard_map/ppermute | solution.py:455
  69.3 1.9 %collective-permute-start.11 = (bf16[1024,256]{1,0:T(8,128)(2,1)S(1)}, bf16[1024,256]{1,0:T(8,128)(2,1)S(1)}, u32[]{:S(2)}, u32[]{:S(2)}) collective-permute-start(bf16[1024,256]{1,0:T(8,128)(2,1)S(1)} %slice_bitcast_fusion.3), channel_id=1, source_target_pairs={{0,64},{64,128},{128,192},{192,0},{1,65},{65,129},{129,193},{193,1... | collective-permute-start | bytes 1572872 | tf_op jit(solution)/shard_map/ppermute | solution.py:455
  71.3 0.9 collective-permute-start.12
  72.2 3.1 %collective-permute-done.8.refs_2_ = bf16[256,1024]{1,0:T(8,128)(2,1)S(1)} collective-permute-done((bf16[256,1024]{1,0:T(8,128)(2,1)S(1)}, bf16[256,1024]{1,0:T(8,128)(2,1)S(1)}, u32[]{:S(2)}, u32[]{:S(2)}) %collective-permute-start.8) | collective-permute-done | bytes 524320 | tf_op jit(solution)/shard_map/ppermute | solution.py:455
  75.3 9.6 %collective-permute-done.7.refs_1_ = bf16[256,1024]{1,0:T(8,128)(2,1)S(1)} collective-permute-done((bf16[256,1024]{1,0:T(8,128)(2,1)S(1)}, bf16[256,1024]{1,0:T(8,128)(2,1)S(1)}, u32[]{:S(2)}, u32[]{:S(2)}) %collective-permute-start.7) | collective-permute-done | bytes 524320 | tf_op jit(solution)/shard_map/ppermute | solution.py:455
  84.9 3.6 %products_near.1 = bf16[2,4,384,512]{3,2,1,0:T(8,128)(2,1)S(1)} custom-call(bf16[256,1024]{1,0:T(8,128)(2,1)S(1)} %gated_rows.1.refs_0_, bf16[256,1024]{1,0:T(8,128)(2,1)S(1)} %collective-permute-done.7.refs_1_, bf16[256,1024]{1,0:T(8,128)(2,1)S(1)} %collective-permute-done.8.refs_2_, bf16[2,1024,256]{2,1,0:T(8,128)(2,1)S(1)} %pad_maximum_fusion.refs_3_.refs_2_, ...), custom_call_target="tpu_custom_call" | custom-call | flops 1000000000 | bytes 1048576 | tf_op jit(solution)/shard_map/products_near/pallas_call | solution.py:414
  88.5 0.1 slice_bitcast_fusion
  88.6 2.0 %collective-permute-start.15 = (bf16[4,384,512]{2,1,0:T(8,128)(2,1)S(1)}, bf16[4,384,512]{2,1,0:T(8,128)(2,1)S(1)}, u32[]{:S(2)}, u32[]{:S(2)}) collective-permute-start(bf16[4,384,512]{2,1,0:T(8,128)(2,1)S(1)} %slice_bitcast_fusion), channel_id=1, source_target_pairs={{0,1},{1,0},{2,3},{3,2},{4,5},{5,4},{6,7},{7,6},{8,9},{9,8},{10,11... | collective-permute-start | bytes 4718600 | tf_op jit(solution)/shard_map/ppermute | solution.py:498
  90.6 3.0 %collective-permute-done.15 = bf16[4,384,512]{2,1,0:T(8,128)(2,1)S(1)} collective-permute-done((bf16[4,384,512]{2,1,0:T(8,128)(2,1)S(1)}, bf16[4,384,512]{2,1,0:T(8,128)(2,1)S(1)}, u32[]{:S(2)}, u32[]{:S(2)}) %collective-permute-start.15) | collective-permute-done | bytes 1572896 | tf_op jit(solution)/shard_map/ppermute | solution.py:498
  93.6 0.4 fusion
  94.1 0.1 slice_bitcast_fusion.4
  94.1 2.6 %collective-permute-start.18 = (bf16[384,512]{1,0:T(8,128)(2,1)S(1)}, bf16[384,512]{1,0:T(8,128)(2,1)S(1)}, u32[]{:S(2)}, u32[]{:S(2)}) collective-permute-start(bf16[384,512]{1,0:T(8,128)(2,1)S(1)} %get-tuple-element.67), channel_id=1, source_target_pairs={{0,6},{2,0},{4,2},{6,4},{1,7},{3,1},{5,3},{7,5},{8,14},{10,8},{12,... | collective-permute-start | bytes 1179656 | tf_op jit(solution)/shard_map/ppermute | solution.py:455
  96.7 0.0 collective-permute-start.17
  96.7 1.7 %collective-permute-start.16 = (bf16[384,512]{1,0:T(8,128)(2,1)S(1)}, bf16[384,512]{1,0:T(8,128)(2,1)S(1)}, u32[]{:S(2)}, u32[]{:S(2)}) collective-permute-start(bf16[384,512]{1,0:T(8,128)(2,1)S(1)} %get-tuple-element.69), channel_id=1, source_target_pairs={{0,4},{2,6},{4,0},{6,2},{1,5},{3,7},{5,1},{7,3},{8,12},{10,14},{12... | collective-permute-start | bytes 1179656 | tf_op jit(solution)/shard_map/ppermute | solution.py:455
  98.5 2.4 %collective-permute-start.14 = (bf16[128,1024]{1,0:T(8,128)(2,1)S(1)}, bf16[128,1024]{1,0:T(8,128)(2,1)S(1)}, u32[]{:S(2)}, u32[]{:S(2)}) collective-permute-start(bf16[128,1024]{1,0:T(8,128)(2,1)S(1)} %slice.133), channel_id=1, source_target_pairs={{0,16},{16,32},{32,48},{48,0},{1,17},{17,33},{33,49},{49,1},{2,18}... | collective-permute-start | bytes 786440 | tf_op jit(solution)/shard_map/ppermute | solution.py:455
  100.8 1.7 %collective-permute-start.13 = (bf16[128,1024]{1,0:T(8,128)(2,1)S(1)}, bf16[128,1024]{1,0:T(8,128)(2,1)S(1)}, u32[]{:S(2)}, u32[]{:S(2)}) collective-permute-start(bf16[128,1024]{1,0:T(8,128)(2,1)S(1)} %slice.132), channel_id=1, source_target_pairs={{0,48},{16,0},{32,16},{48,32},{1,49},{17,1},{33,17},{49,33},{2,50}... | collective-permute-start | bytes 786440 | tf_op jit(solution)/shard_map/ppermute | solution.py:455
  102.5 10.7 %collective-permute-done.14.refs_1_ = bf16[128,1024]{1,0:T(8,128)(2,1)S(1)} collective-permute-done((bf16[128,1024]{1,0:T(8,128)(2,1)S(1)}, bf16[128,1024]{1,0:T(8,128)(2,1)S(1)}, u32[]{:S(2)}, u32[]{:S(2)}) %collective-permute-start.14) | collective-permute-done | bytes 262176 | tf_op jit(solution)/shard_map/ppermute | solution.py:455
  113.2 0.5 collective-permute-done.13.refs_0_
  113.8 1.7 %collective-permute-done.16 = bf16[384,512]{1,0:T(8,128)(2,1)S(1)} collective-permute-done((bf16[384,512]{1,0:T(8,128)(2,1)S(1)}, bf16[384,512]{1,0:T(8,128)(2,1)S(1)}, u32[]{:S(2)}, u32[]{:S(2)}) %collective-permute-start.16) | collective-permute-done | bytes 393248 | tf_op jit(solution)/shard_map/ppermute | solution.py:455
  115.4 1.3 products_far.1
  116.7 4.4 %collective-permute-start.20 = (bf16[4,256,512]{2,1,0:T(8,128)(2,1)S(1)}, bf16[4,256,512]{2,1,0:T(8,128)(2,1)S(1)}, u32[]{:S(2)}, u32[]{:S(2)}) collective-permute-start(bf16[4,256,512]{2,1,0:T(8,128)(2,1)S(1)} %bitcast.80), channel_id=1, source_target_pairs={{1,0},{17,16},{32,33},{48,49},{3,2},{19,18},{34,35},{50,51},{5,4},... | collective-permute-start | bytes 3145736 | tf_op jit(solution)/shard_map/ppermute | solution.py:520
  121.1 2.2 %collective-permute-done.20 = bf16[4,256,512]{2,1,0:T(8,128)(2,1)S(1)} collective-permute-done((bf16[4,256,512]{2,1,0:T(8,128)(2,1)S(1)}, bf16[4,256,512]{2,1,0:T(8,128)(2,1)S(1)}, u32[]{:S(2)}, u32[]{:S(2)}) %collective-permute-start.20) | collective-permute-done | bytes 1048608 | tf_op jit(solution)/shard_map/ppermute | solution.py:520
  123.3 0.3 add_convert_fusion
  123.6 0.1 slice_bitcast_fusion.9
  123.7 0.7 collective-permute-start.21
  124.4 0.7 collective-permute-start.23
  125.1 0.7 collective-permute-start.22
  125.7 0.2 fusion.3
  126.0 3.2 %collective-permute-start.25 = (bf16[256,512]{1,0:T(8,128)(2,1)S(1)}, bf16[256,512]{1,0:T(8,128)(2,1)S(1)}, u32[]{:S(2)}, u32[]{:S(2)}) collective-permute-start(bf16[256,512]{1,0:T(8,128)(2,1)S(1)} %slice.164), channel_id=1, source_target_pairs={{0,16},{1,48},{16,32},{17,0},{32,49},{33,17},{48,1},{49,33},{2,18}... | collective-permute-start | bytes 786440 | tf_op jit(solution)/shard_map/ppermute | solution.py:506
  129.2 0.1 fusion.6
  129.3 1.3 collective-permute-start.24
  130.7 10.2 %collective-permute-start.19 = (bf16[128,512]{1,0:T(8,128)(2,1)S(1)}, bf16[128,512]{1,0:T(8,128)(2,1)S(1)}, u32[]{:S(2)}, u32[]{:S(2)}) collective-permute-start(bf16[128,512]{1,0:T(8,128)(2,1)S(1)} %slice.159.near_own), channel_id=1, source_target_pairs={{0,1},{1,0},{2,3},{3,2},{4,5},{5,4},{6,7},{7,6},{8,9},{9,8},{10,11... | collective-permute-start | bytes 393224 | tf_op jit(solution)/shard_map/ppermute | solution.py:528
  140.9 1.0 collective-permute-done.19.near_other
  141.9 4.9 %collective-permute-done.24.far = bf16[256,512]{1,0:T(8,128)(2,1)S(1)} collective-permute-done((bf16[256,512]{1,0:T(8,128)(2,1)S(1)}, bf16[256,512]{1,0:T(8,128)(2,1)S(1)}, u32[]{:S(2)}, u32[]{:S(2)}) %collective-permute-start.24) | collective-permute-done | bytes 262176 | tf_op jit(solution)/shard_map/ppermute | solution.py:531
  146.8 0.8 assemble.1
  (44 shorter events, 0.3 us)
Async XLA Ops:
  0.8 7.1 %collective-permute-start = (bf16[3,8,1024]{2,1,0:T(8,128)(2,1)S(1)}, bf16[3,8,1024]{2,1,0:T(8,128)(2,1)S(1)}, u32[]{:S(2)}, u32[]{:S(2)}) collective-permute-start(bf16[3,8,1024]{2,1,0:T(8,128)(2,1)S(1)} %slice.117), channel_id=1, source_target_pairs={{0,8},{8,16},{16,24},{24,32},{32,40},{40,48},{48,56},{56,64},{64,7... | collective-permute-start | bytes 147464 | tf_op jit(solution)/shard_map/ppermute | solution.py:451
  7.9 1.7 %copy-start.7 = (bf16[3,8,1024]{2,1,0:T(8,128)(2,1)}, bf16[3,8,1024]{2,1,0:T(8,128)(2,1)S(1)}, u32[]{:S(2)}) copy-start(bf16[3,8,1024]{2,1,0:T(8,128)(2,1)S(1)} %collective-permute-done.border) | copy-start | bytes 147460
  7.9 26.9 %collective-permute-start.4 = (bf16[1024,256]{1,0:T(8,128)(2,1)}, bf16[1024,256]{1,0:T(8,128)(2,1)S(1)}, u32[]{:S(2)}, u32[]{:S(2)}) collective-permute-start(bf16[1024,256]{1,0:T(8,128)(2,1)} %param.19), channel_id=1, source_target_pairs={{0,8},{8,0},{1,9},{9,1},{2,10},{10,2},{3,11},{11,3},{4,12},{12,4},... | collective-permute-start | bytes 1572872 | tf_op jit(solution)/shard_map/ppermute | solution.py:470
  9.6 21.9 %copy-start = (bf16[3,256,1024]{2,1,0:T(8,128)(2,1)S(1)}, bf16[3,256,1024]{2,1,0:T(8,128)(2,1)}, u32[]{:S(2)}) copy-start(bf16[3,256,1024]{2,1,0:T(8,128)(2,1)} %feat.3) | copy-start | bytes 4718596
  9.6 21.9 %copy-start.5 = (s32[8192]{0:T(1024)S(1)}, s32[8192]{0:T(1024)}, u32[]{:S(2)}) copy-start(s32[8192]{0:T(1024)} %ids.7) | copy-start | bytes 98308
  9.6 21.9 %copy-start.6 = (f32[7,3,8,128]{3,2,1,0:T(8,128)S(1)}, f32[7,3,8,128]{3,2,1,0:T(8,128)}, u32[]{:S(2)}) copy-start(f32[7,3,8,128]{3,2,1,0:T(8,128)} %get-tuple-element.38.taps) | copy-start | bytes 258052
  19.1 15.7 %copy-start.3 = (f32[4,2,16,8,128]{4,3,2,1,0:T(8,128)S(1)}, f32[4,2,16,8,128]{4,3,2,1,0:T(8,128)}, u32[]{:S(2)}) copy-start(f32[4,2,16,8,128]{4,3,2,1,0:T(8,128)} %get-tuple-element.41) | copy-start | bytes 1572868
  19.1 15.6 %collective-permute-start.3 = (bf16[2,128,128]{2,1,0:T(8,128)(2,1)}, bf16[2,128,128]{2,1,0:T(8,128)(2,1)S(1)}, u32[]{:S(2)}, u32[]{:S(2)}) collective-permute-start(bf16[2,128,128]{2,1,0:T(8,128)(2,1)} %get-tuple-element.40), channel_id=1, source_target_pairs={{0,24},{8,32},{16,40},{24,48},{32,56},{40,64},{48,72},{56,80},{64,... | collective-permute-start | bytes 196616 | tf_op jit(solution)/shard_map/ppermute | solution.py:451
  25.3 9.5 %collective-permute-start.2 = (bf16[2,128,128]{2,1,0:T(8,128)(2,1)}, bf16[2,128,128]{2,1,0:T(8,128)(2,1)S(1)}, u32[]{:S(2)}, u32[]{:S(2)}) collective-permute-start(bf16[2,128,128]{2,1,0:T(8,128)(2,1)} %get-tuple-element.40), channel_id=1, source_target_pairs={{0,16},{8,24},{16,32},{24,40},{32,48},{40,56},{48,64},{56,72},{64,... | collective-permute-start | bytes 196616 | tf_op jit(solution)/shard_map/ppermute | solution.py:451
  29.6 5.2 %collective-permute-start.1 = (bf16[2,128,128]{2,1,0:T(8,128)(2,1)}, bf16[2,128,128]{2,1,0:T(8,128)(2,1)S(1)}, u32[]{:S(2)}, u32[]{:S(2)}) collective-permute-start(bf16[2,128,128]{2,1,0:T(8,128)(2,1)} %get-tuple-element.40), channel_id=1, source_target_pairs={{0,8},{8,16},{16,24},{24,32},{32,40},{40,48},{48,56},{56,64},{64,7... | collective-permute-start | bytes 196616 | tf_op jit(solution)/shard_map/ppermute | solution.py:451
  31.5 0.8 copy-start.8
  34.7 0.8 copy-start.13
  34.7 11.0 %copy-start.12 = (bf16[1024,256]{1,0:T(8,128)(2,1)S(1)}, bf16[1024,256]{1,0:T(8,128)(2,1)}, u32[]{:S(2)}) copy-start(bf16[1024,256]{1,0:T(8,128)(2,1)} %param.19) | copy-start | bytes 1572868
  34.9 15.3 %copy-start.1 = (f32[8,2,16,1024]{3,2,1,0:T(8,128)S(1)}, f32[8,2,16,1024]{3,2,1,0:T(8,128)}, u32[]{:S(2)}) copy-start(f32[8,2,16,1024]{3,2,1,0:T(8,128)} %entry.3) | copy-start | bytes 3145732
  34.9 15.3 %copy-start.2 = (f32[4,2,16,8,128]{4,3,2,1,0:T(8,128)S(1)}, f32[4,2,16,8,128]{4,3,2,1,0:T(8,128)}, u32[]{:S(2)}) copy-start(f32[4,2,16,8,128]{4,3,2,1,0:T(8,128)} %get-tuple-element.39.pole) | copy-start | bytes 1572868
  34.9 15.3 %copy-start.4 = (f32[256,8,128]{2,1,0:T(8,128)S(1)}, f32[256,8,128]{2,1,0:T(8,128)}, u32[]{:S(2)}) copy-start(f32[256,8,128]{2,1,0:T(8,128)} %get-tuple-element.50.product) | copy-start | bytes 3145732
  34.9 15.3 %copy-start.9 = (f32[2,16,1024]{2,1,0:T(8,128)S(1)}, f32[2,16,1024]{2,1,0:T(8,128)}, u32[]{:S(2)}) copy-start(f32[2,16,1024]{2,1,0:T(8,128)} %res.1) | copy-start | bytes 393220
  34.9 15.3 %copy-start.10 = (f32[1024]{0:T(1024)S(1)}, f32[1024]{0:T(1024)}, u32[]{:S(2)}) copy-start(f32[1024]{0:T(1024)} %param.15) | copy-start | bytes 12292
  34.9 15.3 %copy-start.11 = (s32[8]{0:T(128)S(1)}, s32[8]{0:T(128)}, u32[]{:S(2)}) copy-start(s32[8]{0:T(128)} %picks.3) | copy-start | bytes 100
  35.6 8.9 %collective-permute-start.6 = (bf16[2,128,128]{2,1,0:T(8,128)(2,1)S(1)}, bf16[2,128,128]{2,1,0:T(8,128)(2,1)S(1)}, u32[]{:S(2)}, u32[]{:S(2)}) collective-permute-start(bf16[2,128,128]{2,1,0:T(8,128)(2,1)S(1)} %fusion.9), channel_id=1, source_target_pairs={{0,40},{8,48},{16,56},{24,64},{32,72},{40,80},{48,88},{56,96},{64,... | collective-permute-start | bytes 196616 | tf_op jit(solution)/shard_map/ppermute | solution.py:451
  41.5 4.3 %collective-permute-start.5 = (bf16[2,128,128]{2,1,0:T(8,128)(2,1)S(1)}, bf16[2,128,128]{2,1,0:T(8,128)(2,1)S(1)}, u32[]{:S(2)}, u32[]{:S(2)}) collective-permute-start(bf16[2,128,128]{2,1,0:T(8,128)(2,1)S(1)} %fusion.9), channel_id=1, source_target_pairs={{0,8},{8,16},{16,24},{24,32},{32,40},{40,48},{48,56},{56,64},{64,7... | collective-permute-start | bytes 196616 | tf_op jit(solution)/shard_map/ppermute | solution.py:451
  45.9 23.4 %collective-permute-start.10 = (bf16[2,1024,256]{2,1,0:T(8,128)(2,1)S(1)}, bf16[2,1024,256]{2,1,0:T(8,128)(2,1)S(1)}, u32[]{:S(2)}, u32[]{:S(2)}) collective-permute-start(bf16[2,1024,256]{2,1,0:T(8,128)(2,1)S(1)} %pad_maximum_fusion.refs_3_.refs_2_), channel_id=1, source_target_pairs={{0,64},{64,128},{128,192},{192,0},{1,65},{65,129},{129,193},{193,1... | collective-permute-start | bytes 3145736 | tf_op jit(solution)/shard_map/ppermute | solution.py:455
  49.6 21.6 %collective-permute-start.9 = (bf16[2,1024,256]{2,1,0:T(8,128)(2,1)S(1)}, bf16[2,1024,256]{2,1,0:T(8,128)(2,1)S(1)}, u32[]{:S(2)}, u32[]{:S(2)}) collective-permute-start(bf16[2,1024,256]{2,1,0:T(8,128)(2,1)S(1)} %pad_maximum_fusion.refs_3_.refs_2_), channel_id=1, source_target_pairs={{0,192},{64,0},{128,64},{192,128},{1,193},{65,1},{129,65},{193,129... | collective-permute-start | bytes 3145736 | tf_op jit(solution)/shard_map/ppermute | solution.py:455
  59.3 15.9 %collective-permute-start.8 = (bf16[256,1024]{1,0:T(8,128)(2,1)S(1)}, bf16[256,1024]{1,0:T(8,128)(2,1)S(1)}, u32[]{:S(2)}, u32[]{:S(2)}) collective-permute-start(bf16[256,1024]{1,0:T(8,128)(2,1)S(1)} %gated_rows.1.refs_0_), channel_id=1, source_target_pairs={{0,16},{16,32},{32,48},{48,0},{1,17},{17,33},{33,49},{49,1},{2,18}... | collective-permute-start | bytes 1572872 | tf_op jit(solution)/shard_map/ppermute | solution.py:455
  59.8 25.1 %collective-permute-start.7 = (bf16[256,1024]{1,0:T(8,128)(2,1)S(1)}, bf16[256,1024]{1,0:T(8,128)(2,1)S(1)}, u32[]{:S(2)}, u32[]{:S(2)}) collective-permute-start(bf16[256,1024]{1,0:T(8,128)(2,1)S(1)} %gated_rows.1.refs_0_), channel_id=1, source_target_pairs={{0,48},{16,0},{32,16},{48,32},{1,49},{17,1},{33,17},{49,33},{2,50}... | collective-permute-start | bytes 1572872 | tf_op jit(solution)/shard_map/ppermute | solution.py:455
  69.3 15.6 %collective-permute-start.11 = (bf16[1024,256]{1,0:T(8,128)(2,1)S(1)}, bf16[1024,256]{1,0:T(8,128)(2,1)S(1)}, u32[]{:S(2)}, u32[]{:S(2)}) collective-permute-start(bf16[1024,256]{1,0:T(8,128)(2,1)S(1)} %slice_bitcast_fusion.3), channel_id=1, source_target_pairs={{0,64},{64,128},{128,192},{192,0},{1,65},{65,129},{129,193},{193,1... | collective-permute-start | bytes 1572872 | tf_op jit(solution)/shard_map/ppermute | solution.py:455
  71.3 13.6 %collective-permute-start.12 = (bf16[1024,256]{1,0:T(8,128)(2,1)S(1)}, bf16[1024,256]{1,0:T(8,128)(2,1)S(1)}, u32[]{:S(2)}, u32[]{:S(2)}) collective-permute-start(bf16[1024,256]{1,0:T(8,128)(2,1)S(1)} %slice_bitcast_fusion.2), channel_id=1, source_target_pairs={{0,192},{64,0},{128,64},{192,128},{1,193},{65,1},{129,65},{193,129... | collective-permute-start | bytes 1572872 | tf_op jit(solution)/shard_map/ppermute | solution.py:455
  88.6 5.0 %collective-permute-start.15 = (bf16[4,384,512]{2,1,0:T(8,128)(2,1)S(1)}, bf16[4,384,512]{2,1,0:T(8,128)(2,1)S(1)}, u32[]{:S(2)}, u32[]{:S(2)}) collective-permute-start(bf16[4,384,512]{2,1,0:T(8,128)(2,1)S(1)} %slice_bitcast_fusion), channel_id=1, source_target_pairs={{0,1},{1,0},{2,3},{3,2},{4,5},{5,4},{6,7},{7,6},{8,9},{9,8},{10,11... | collective-permute-start | bytes 4718600 | tf_op jit(solution)/shard_map/ppermute | solution.py:498
  94.1 19.6 %collective-permute-start.18 = (bf16[384,512]{1,0:T(8,128)(2,1)S(1)}, bf16[384,512]{1,0:T(8,128)(2,1)S(1)}, u32[]{:S(2)}, u32[]{:S(2)}) collective-permute-start(bf16[384,512]{1,0:T(8,128)(2,1)S(1)} %get-tuple-element.67), channel_id=1, source_target_pairs={{0,6},{2,0},{4,2},{6,4},{1,7},{3,1},{5,3},{7,5},{8,14},{10,8},{12,... | collective-permute-start | bytes 1179656 | tf_op jit(solution)/shard_map/ppermute | solution.py:455
  96.7 17.1 %collective-permute-start.17 = (bf16[384,512]{1,0:T(8,128)(2,1)S(1)}, bf16[384,512]{1,0:T(8,128)(2,1)S(1)}, u32[]{:S(2)}, u32[]{:S(2)}) collective-permute-start(bf16[384,512]{1,0:T(8,128)(2,1)S(1)} %get-tuple-element.68), channel_id=1, source_target_pairs={{0,2},{2,4},{4,6},{6,0},{1,3},{3,5},{5,7},{7,1},{8,10},{10,12},{12... | collective-permute-start | bytes 1179656 | tf_op jit(solution)/shard_map/ppermute | solution.py:455
  96.7 18.7 %collective-permute-start.16 = (bf16[384,512]{1,0:T(8,128)(2,1)S(1)}, bf16[384,512]{1,0:T(8,128)(2,1)S(1)}, u32[]{:S(2)}, u32[]{:S(2)}) collective-permute-start(bf16[384,512]{1,0:T(8,128)(2,1)S(1)} %get-tuple-element.69), channel_id=1, source_target_pairs={{0,4},{2,6},{4,0},{6,2},{1,5},{3,7},{5,1},{7,3},{8,12},{10,14},{12... | collective-permute-start | bytes 1179656 | tf_op jit(solution)/shard_map/ppermute | solution.py:455
  98.5 14.7 %collective-permute-start.14 = (bf16[128,1024]{1,0:T(8,128)(2,1)S(1)}, bf16[128,1024]{1,0:T(8,128)(2,1)S(1)}, u32[]{:S(2)}, u32[]{:S(2)}) collective-permute-start(bf16[128,1024]{1,0:T(8,128)(2,1)S(1)} %slice.133), channel_id=1, source_target_pairs={{0,16},{16,32},{32,48},{48,0},{1,17},{17,33},{33,49},{49,1},{2,18}... | collective-permute-start | bytes 786440 | tf_op jit(solution)/shard_map/ppermute | solution.py:455
  100.8 12.9 %collective-permute-start.13 = (bf16[128,1024]{1,0:T(8,128)(2,1)S(1)}, bf16[128,1024]{1,0:T(8,128)(2,1)S(1)}, u32[]{:S(2)}, u32[]{:S(2)}) collective-permute-start(bf16[128,1024]{1,0:T(8,128)(2,1)S(1)} %slice.132), channel_id=1, source_target_pairs={{0,48},{16,0},{32,16},{48,32},{1,49},{17,1},{33,17},{49,33},{2,50}... | collective-permute-start | bytes 786440 | tf_op jit(solution)/shard_map/ppermute | solution.py:455
  116.7 6.6 %collective-permute-start.20 = (bf16[4,256,512]{2,1,0:T(8,128)(2,1)S(1)}, bf16[4,256,512]{2,1,0:T(8,128)(2,1)S(1)}, u32[]{:S(2)}, u32[]{:S(2)}) collective-permute-start(bf16[4,256,512]{2,1,0:T(8,128)(2,1)S(1)} %bitcast.80), channel_id=1, source_target_pairs={{1,0},{17,16},{32,33},{48,49},{3,2},{19,18},{34,35},{50,51},{5,4},... | collective-permute-start | bytes 3145736 | tf_op jit(solution)/shard_map/ppermute | solution.py:520
  123.7 5.5 %collective-permute-start.21 = (bf16[256,512]{1,0:T(8,128)(2,1)S(1)}, bf16[256,512]{1,0:T(8,128)(2,1)S(1)}, u32[]{:S(2)}, u32[]{:S(2)}) collective-permute-start(bf16[256,512]{1,0:T(8,128)(2,1)S(1)} %get-tuple-element.70), channel_id=1, source_target_pairs={{0,4},{2,6},{4,0},{6,2},{16,20},{18,22},{20,16},{22,18},{33,37},{3... | collective-permute-start | bytes 786440 | tf_op jit(solution)/shard_map/ppermute | solution.py:525
  124.4 4.8 %collective-permute-start.23 = (bf16[256,512]{1,0:T(8,128)(2,1)S(1)}, bf16[256,512]{1,0:T(8,128)(2,1)S(1)}, u32[]{:S(2)}, u32[]{:S(2)}) collective-permute-start(bf16[256,512]{1,0:T(8,128)(2,1)S(1)} %get-tuple-element.71), channel_id=1, source_target_pairs={{0,6},{2,0},{4,2},{6,4},{16,22},{18,16},{20,18},{22,20},{33,39},{3... | collective-permute-start | bytes 786440 | tf_op jit(solution)/shard_map/ppermute | solution.py:525
  125.1 4.1 %collective-permute-start.22 = (bf16[256,512]{1,0:T(8,128)(2,1)S(1)}, bf16[256,512]{1,0:T(8,128)(2,1)S(1)}, u32[]{:S(2)}, u32[]{:S(2)}) collective-permute-start(bf16[256,512]{1,0:T(8,128)(2,1)S(1)} %get-tuple-element.72), channel_id=1, source_target_pairs={{0,2},{2,4},{4,6},{6,0},{16,18},{18,20},{20,22},{22,16},{33,35},{3... | collective-permute-start | bytes 786440 | tf_op jit(solution)/shard_map/ppermute | solution.py:525
  126.0 15.9 %collective-permute-start.25 = (bf16[256,512]{1,0:T(8,128)(2,1)S(1)}, bf16[256,512]{1,0:T(8,128)(2,1)S(1)}, u32[]{:S(2)}, u32[]{:S(2)}) collective-permute-start(bf16[256,512]{1,0:T(8,128)(2,1)S(1)} %slice.164), channel_id=1, source_target_pairs={{0,16},{1,48},{16,32},{17,0},{32,49},{33,17},{48,1},{49,33},{2,18}... | collective-permute-start | bytes 786440 | tf_op jit(solution)/shard_map/ppermute | solution.py:506
  129.3 17.4 %collective-permute-start.24 = (bf16[256,512]{1,0:T(8,128)(2,1)S(1)}, bf16[256,512]{1,0:T(8,128)(2,1)S(1)}, u32[]{:S(2)}, u32[]{:S(2)}) collective-permute-start(bf16[256,512]{1,0:T(8,128)(2,1)S(1)} %fusion.6), channel_id=1, source_target_pairs={{0,32},{16,48},{33,1},{49,17},{2,34},{18,50},{35,3},{51,19},{4,36}... | collective-permute-start | bytes 786440 | tf_op jit(solution)/shard_map/ppermute | solution.py:531
  130.7 11.2 %collective-permute-start.19 = (bf16[128,512]{1,0:T(8,128)(2,1)S(1)}, bf16[128,512]{1,0:T(8,128)(2,1)S(1)}, u32[]{:S(2)}, u32[]{:S(2)}) collective-permute-start(bf16[128,512]{1,0:T(8,128)(2,1)S(1)} %slice.159.near_own), channel_id=1, source_target_pairs={{0,1},{1,0},{2,3},{3,2},{4,5},{5,4},{6,7},{7,6},{8,9},{9,8},{10,11... | collective-permute-start | bytes 393224 | tf_op jit(solution)/shard_map/ppermute | solution.py:528
